TPU v7x, 128 devices: a whole 4x4x4 slice. The times are simulated.
128 devices in a mesh: dp: 32 (over x, z, core), mp: 4 (over y).
Axes of the slice: x: 4, y: 4, z: 4, core: 2. Of those that a mesh axis runs over, the one named last changes fastest.
Arguments:
- hidden_in: bfloat16 [32768, 2048], P('dp', 'mp'), may hold values from -6 to 6
- token_ids: int32 [32768], P('dp'), may hold values from 0 to 128001, as said below
- passage_counts: int32 [64], P('dp'), may hold values from 1 to 4, as said below
- positive_doc: int32 [4096], P('dp'), may hold values from 0 to 63
- queries: bfloat16 [4096, 2048], P('dp', 'mp'), may hold values from -6 to 6
- norm_gain: float32 [2048], replicated, may hold values from 0.5 to 1.5
- w_gate: bfloat16 [2048, 7168], P(None, 'mp'), may hold values from -0.125 to 0.125
- w_up: bfloat16 [2048, 7168], P(None, 'mp'), may hold values from -0.125 to 0.125
- w_down: bfloat16 [7168, 2048], P('mp'), may hold values from -0.0625 to 0.0625
Outputs:
- query_loss: float32 [4096], P('dp')
- hidden_grad: bfloat16 [32768, 2048], P('dp', 'mp')
Inputs may be any that keep to these rules, and one draw needn't show every extreme that they name: `passage_counts`: A document has 1 to 4 passages; every draw has a dp index whose documents all have 4. The live passages hold 160 passages in all. `token_ids`: 128001 marks padding; it stands only at the tail of a document's last live passage, and every live passage has a token that is not padding.
All inputs are finite; a program needn't handle non-finite values.
Results may differ from a plain program's by a relative error of at most 0.023.
Values may be sent and summed in bfloat16 or wider, within the bound.
No kernel may reach another device: no remote copies, remote signals or barrier semaphores. Data moves between devices by JAX's collectives and lax.ppermute only.
A program may use at most 128 MiB of HBM per device.

v0:
```python
import math

import jax
import jax.numpy as jnp
from jax import lax
from jax.sharding import PartitionSpec as P

L = 128


pad_token = 128001
score_scale = 20.0
loss_seed = 4096.0
norm_epsilon = 1e-05
unit_epsilon = 1e-06


def sent_to_all(x, axis):
    copies = jnp.broadcast_to(x, (lax.axis_size(axis), *x.shape))
    return lax.all_to_all(copies, axis, split_axis=0, concat_axis=0, tiled=True)


def joined_along(blocks, dim):
    lengths = list(blocks.shape[1:])
    lengths[dim] *= blocks.shape[0]
    return jnp.moveaxis(blocks, 0, dim).reshape(lengths)


def gathered_copies(x, axis, dim):
    blocks = sent_to_all(x, axis)
    return joined_along(blocks, dim)


def cut_along(x, dim, devices):
    before, after = (x.shape[:dim], x.shape[dim + 1 :])
    return jnp.moveaxis(x.reshape(*before, devices, -1, *after), dim, 0)


def summed_on_arrival(x, axis, dim):
    blocks = cut_along(x, dim, lax.axis_size(axis))
    arrived = lax.all_to_all(blocks, axis, split_axis=0, concat_axis=0, tiled=True)
    return arrived.astype(jnp.float32).sum(axis=0)


def sent_together(arrays, axis, dim, along):
    widths = [math.prod(a.shape[along:]) for a in arrays]
    both = jnp.concatenate(
        [a.reshape(*a.shape[:along], w) for a, w in zip(arrays, widths)], axis=along
    )
    result = summed_on_arrival(both, axis, dim)
    blocks = jnp.split(result, [sum(widths[:k]) for k in range(1, len(widths))], axis=along)
    return tuple(
        (b.reshape(*result.shape[:along], *a.shape[along:]) for a, b in zip(arrays, blocks))
    )


def contract_rows(left, right):
    return lax.dot_general(
        left, right, (((1,), (1,)), ((), ())), preferred_element_type=jnp.float32
    )


def packing_order(received_flag, received_mask, slot_capacity):
    flag = received_flag.reshape(-1).astype(jnp.float32)
    place = jnp.cumsum(flag) - flag
    packed_rows = flag[None, :] * (
        place[None, :] == jnp.arange(slot_capacity, dtype=jnp.float32)[:, None]
    ).astype(jnp.float32)
    packed_half_rows = packed_rows.astype(jnp.bfloat16)
    task_row_mask = jnp.dot(
        packed_half_rows,
        received_mask.reshape(flag.shape[0], -1),
        preferred_element_type=jnp.float32,
    )
    return (packed_rows, packed_half_rows, task_row_mask)


def per_device(
    hidden_in, token_ids, passage_counts, positive_doc, queries, norm_gain, w_gate, w_up, w_down
):
    dp_count = lax.axis_size("dp")
    row_count, part_width = hidden_in.shape
    model_width = norm_gain.shape[0]
    docs_here = passage_counts.shape[0]
    quarters = 4
    block_len = L // quarters
    src_blocks = row_count // block_len
    most_pass = src_blocks // (docs_here * quarters)
    slot_count = src_blocks // dp_count
    slot_capacity = docs_here * 2 * (most_pass + 1)
    passes_here = docs_here * most_pass
    received = dp_count * slot_count
    all_counts = lax.all_gather(passage_counts, "dp", axis=0, tiled=True)
    doc_total = all_counts.shape[0]
    before = (jnp.arange(doc_total, dtype=jnp.int32) < lax.axis_index("dp") * docs_here).astype(
        jnp.int32
    )
    offset = quarters * jnp.sum(all_counts * before)
    block_index = jnp.arange(src_blocks, dtype=jnp.int32)
    live_block = block_index // quarters % most_pass < jnp.repeat(
        passage_counts, most_pass * quarters
    )
    live_int = live_block.astype(jnp.int32)
    global_order = offset + jnp.cumsum(live_int) - live_int
    target = global_order % dp_count
    token_live = (token_ids.reshape(src_blocks, block_len) != pad_token) & live_block[:, None]
    device_hit = live_block.astype(jnp.float32)[:, None] * (
        target[:, None] == jnp.arange(dp_count, dtype=jnp.int32)[None, :]
    ).astype(jnp.float32)
    earlier = jnp.cumsum(device_hit, axis=0) - device_hit
    slot_match = (
        earlier[:, :, None] == jnp.arange(slot_count, dtype=jnp.float32)[None, None, :]
    ).astype(jnp.float32)
    select = (device_hit[:, :, None] * slot_match).reshape(src_blocks, received).T
    select_half = select.astype(jnp.bfloat16)
    send_mask = jnp.dot(
        select_half, token_live.astype(jnp.bfloat16), preferred_element_type=jnp.float32
    )
    send_mask = send_mask.astype(jnp.bfloat16).reshape(dp_count, slot_count, block_len)
    send_flag = jnp.sum(select, axis=1).astype(jnp.bfloat16).reshape(dp_count, slot_count)
    mp_start = lax.axis_index("mp") * part_width
    send = jnp.dot(
        select_half,
        hidden_in.reshape(src_blocks, block_len * part_width),
        preferred_element_type=jnp.float32,
    )
    send = send.astype(jnp.bfloat16).reshape(dp_count, slot_count, block_len, part_width)
    got, received_mask, received_flag = (
        lax.all_to_all(send, "dp", split_axis=0, concat_axis=0, tiled=True),
        lax.all_to_all(send_mask, "dp", split_axis=0, concat_axis=0, tiled=True),
        lax.all_to_all(send_flag, "dp", split_axis=0, concat_axis=0, tiled=True),
    )
    packed_rows, packed_half_rows, task_row_mask = packing_order(
        received_flag, received_mask, slot_capacity
    )
    own_rows = jnp.dot(
        packed_half_rows,
        got.reshape(received, block_len * part_width),
        preferred_element_type=jnp.float32,
    )
    own_rows = own_rows.astype(jnp.bfloat16).reshape(slot_capacity * block_len, part_width)
    task_rows = gathered_copies(own_rows, "mp", 1)
    row_float = task_rows.astype(jnp.float32)
    rms_scale = lax.rsqrt(jnp.mean(row_float * row_float, axis=1, keepdims=True) + norm_epsilon)
    normed = (row_float * rms_scale * norm_gain[None, :]).astype(jnp.bfloat16)
    gate = jnp.dot(normed, w_gate, preferred_element_type=jnp.float32)
    up = jnp.dot(normed, w_up, preferred_element_type=jnp.float32)
    sigmoid_gate = jax.nn.sigmoid(gate)
    hidden = (gate * sigmoid_gate * up).astype(jnp.bfloat16)
    layer_part = jnp.dot(hidden, w_down, preferred_element_type=jnp.float32)
    token_weight = task_row_mask[:, :, None]
    layer_pool = jnp.sum(
        layer_part.reshape(slot_capacity, block_len, model_width) * token_weight, axis=1
    )
    layer_pool = summed_on_arrival(layer_pool.astype(jnp.bfloat16), "mp", 1)
    own_input = own_rows.astype(jnp.float32)
    pooled = (
        jnp.sum(own_input.reshape(slot_capacity, block_len, part_width) * token_weight, axis=1)
        + layer_pool
    )
    spread = jnp.dot(packed_rows.T, pooled)
    home = lax.all_to_all(
        spread.reshape(dp_count, slot_count, part_width).astype(jnp.bfloat16),
        "dp",
        split_axis=0,
        concat_axis=0,
        tiled=True,
    ).astype(jnp.float32)
    block_sums = jnp.dot(select.T, home.reshape(received, part_width))
    passage_sum = block_sums.reshape(passes_here, quarters, part_width).sum(axis=1)
    token_total = jnp.sum(
        token_live.reshape(passes_here, quarters * block_len).astype(jnp.float32), axis=1
    )
    divisor = jnp.maximum(token_total, 1.0)
    passage_vec = (passage_sum / divisor[:, None]).astype(jnp.bfloat16)
    all_vec = lax.all_gather(passage_vec, "dp", axis=0, tiled=True)
    pass_total = all_vec.shape[0]
    all_live = (
        jnp.arange(pass_total, dtype=jnp.int32) % most_pass < jnp.repeat(all_counts, most_pass)
    ).astype(jnp.float32)
    vec_float = all_vec.astype(jnp.float32)
    query_float = queries.astype(jnp.float32)
    score_part = contract_rows(queries, all_vec)
    raw_score, passage_sq, query_sq = (
        lax.psum(score_part.astype(jnp.bfloat16), "mp").astype(jnp.float32),
        lax.psum(jnp.sum(vec_float * vec_float, axis=1).astype(jnp.bfloat16), "mp").astype(
            jnp.float32
        ),
        lax.psum(jnp.sum(query_float * query_float, axis=1).astype(jnp.bfloat16), "mp").astype(
            jnp.float32
        ),
    )
    query_scale = lax.rsqrt(query_sq + unit_epsilon)
    passage_scale = lax.rsqrt(passage_sq + unit_epsilon)
    scores = score_scale * raw_score * query_scale[:, None] * passage_scale[None, :]
    weights = all_live[None, :] * jnp.exp(scores)
    doc_mass = weights.reshape(queries.shape[0], doc_total, most_pass).sum(axis=2)
    total_mass = doc_mass.sum(axis=1)
    positive_hit = (
        positive_doc[:, None] == jnp.arange(doc_total, dtype=jnp.int32)[None, :]
    ).astype(jnp.float32)
    positive_mass = jnp.sum(doc_mass * positive_hit, axis=1)
    query_loss = jnp.log(total_mass) - jnp.log(positive_mass)
    positive_pass = jnp.repeat(positive_hit, most_pass, axis=1)
    coefficient = (
        loss_seed
        * score_scale
        * query_scale[:, None]
        * (weights / total_mass[:, None] - positive_pass * weights / positive_mass[:, None])
    )
    weighted_queries = lax.dot_general(
        coefficient.astype(jnp.bfloat16),
        queries,
        (((0,), (0,)), ((), ())),
        preferred_element_type=jnp.float32,
    )
    norm_term = jnp.sum(coefficient * raw_score, axis=0)
    vec_grad, norm_grad = sent_together(
        (weighted_queries.astype(jnp.bfloat16), norm_term.astype(jnp.bfloat16)), "dp", 0, 1
    )
    own_scale = lax.dynamic_slice_in_dim(
        passage_scale, lax.axis_index("dp") * passes_here, passes_here
    )
    own_vec = passage_vec.astype(jnp.float32)
    vec_change = own_scale[:, None] * vec_grad - own_vec * (own_scale**3 * norm_grad)[:, None]
    token_grad = (vec_change / divisor[:, None]).astype(jnp.bfloat16)
    block_grad = jnp.repeat(token_grad, quarters, axis=0)
    grad_send = jnp.dot(select_half, block_grad, preferred_element_type=jnp.float32).astype(
        jnp.bfloat16
    )
    grad_got = lax.all_to_all(
        grad_send.reshape(dp_count, slot_count, part_width),
        "dp",
        split_axis=0,
        concat_axis=0,
        tiled=True,
    )
    grad_task = jnp.dot(
        packed_half_rows, grad_got.reshape(received, part_width), preferred_element_type=jnp.float32
    ).astype(jnp.bfloat16)
    grad_full = lax.all_gather(grad_task, "mp", axis=1, tiled=True)
    out_grad = (
        (token_weight * grad_full[:, None, :].astype(jnp.float32))
        .astype(jnp.bfloat16)
        .reshape(slot_capacity * block_len, model_width)
    )
    own_out_grad = (token_weight * grad_task[:, None, :].astype(jnp.float32)).reshape(
        slot_capacity * block_len, part_width
    )
    hidden_grad = contract_rows(out_grad, w_down)
    gate_grad = (hidden_grad * up * sigmoid_gate * (1.0 + gate * (1.0 - sigmoid_gate))).astype(
        jnp.bfloat16
    )
    up_grad = (hidden_grad * gate * sigmoid_gate).astype(jnp.bfloat16)
    normed_grad = contract_rows(gate_grad, w_gate) + contract_rows(up_grad, w_up)
    own_gain = lax.dynamic_slice_in_dim(norm_gain, mp_start, part_width)
    own_normed = lax.psum_scatter(
        normed_grad.astype(jnp.bfloat16), "mp", scatter_dimension=1, tiled=True
    ).astype(jnp.float32)
    inner_part = jnp.sum(own_input * own_gain[None, :] * own_normed, axis=1)
    inner = lax.psum(inner_part, "mp") / model_width
    input_grad = (
        own_out_grad
        + rms_scale * own_gain[None, :] * own_normed
        - own_input * rms_scale**3 * inner[:, None]
    )
    input_half = input_grad.astype(jnp.bfloat16).reshape(slot_capacity, block_len * part_width)
    back = jnp.dot(packed_half_rows.T, input_half, preferred_element_type=jnp.float32).astype(
        jnp.bfloat16
    )
    back_got = lax.all_to_all(
        back.reshape(dp_count, slot_count, block_len * part_width),
        "dp",
        split_axis=0,
        concat_axis=0,
        tiled=True,
    )
    grad_rows = jnp.dot(
        select_half.T,
        back_got.reshape(received, block_len * part_width),
        preferred_element_type=jnp.float32,
    )
    return (query_loss, grad_rows.astype(jnp.bfloat16).reshape(row_count, part_width))


def solution(mesh):
    return jax.shard_map(
        per_device,
        mesh=mesh,
        in_specs=(
            P("dp", "mp"),
            P("dp"),
            P("dp"),
            P("dp"),
            P("dp", "mp"),
            P(),
            P(None, "mp"),
            P(None, "mp"),
            P("mp", None),
        ),
        out_specs=(P("dp"), P("dp", "mp")),
        check_vma=False,
    )
```

profile of v0, /device:TPU:0, one launch (start us, length us, event | category | flops | bytes accessed | tf_op | source)
XLA Modules:
  0.0 399.2 jit_solution(1453509648983306713)
XLA Ops:
  11.0 18.0 %all-reduce = s32[64]{0:T(128)S(1)} all-reduce(s32[64]{0:T(128)S(1)} %dynamic-update-slice), channel_id=1, replica_groups=mesh['dp'=32,'mp'=4] {'dp'}, use_global_device_ids=true, to_apply=%add | all-reduce | flops 64 | bytes 512
  48.1 15.4 %all-to-all-done.1 = bf16[32,1,32,512]{3,2,1,0:T(8,128)(2,1)S(1)} async-done(((bf16[32,1,32,512]{3,2,1,0:T(8,128)(2,1)}), bf16[32,1,32,512]{3,2,1,0:T(8,128)(2,1)S(1)}, u32[]{:S(2)}, u32[]{:S(2)}) %all-to-all-start.1) | async-done | bytes 1048608 | tf_op jit(solution)/shard_map/all_to_all | solution.py:129
  70.4 4.4 %all-to-all-done.2 = bf16[32,1,32]{2,1,0:T(2,128)(2,1)S(1)} async-done(((bf16[32,1,32]{2,1,0:T(2,128)(2,1)}), bf16[32,1,32]{2,1,0:T(2,128)(2,1)S(1)}, u32[]{:S(2)}, u32[]{:S(2)}) %all-to-all-start.2) | async-done | bytes 2080 | tf_op jit(solution)/shard_map/all_to_all | solution.py:130
  76.6 4.7 %all-to-all-start.3 = ((bf16[4,640,512]{1,2,0:T(8,128)(2,1)}), bf16[4,640,512]{1,2,0:T(8,128)(2,1)S(1)}, u32[]{:S(2)}, u32[]{:S(2)}) async-start(bf16[4,640,512]{1,2,0:T(8,128)(2,1)} %broadcast_in_dim.18), calls=%async_computation.3 | async-start | bytes 5242880 | tf_op jit(solution)/shard_map/all_to_all | solution.py:20
  85.6 27.5 %all-to-all-done.3 = bf16[4,640,512]{1,2,0:T(8,128)(2,1)S(1)} async-done(((bf16[4,640,512]{1,2,0:T(8,128)(2,1)}), bf16[4,640,512]{1,2,0:T(8,128)(2,1)S(1)}, u32[]{:S(2)}, u32[]{:S(2)}) %all-to-all-start.3) | async-done | bytes 2621472 | tf_op jit(solution)/shard_map/all_to_all | solution.py:20
  114.4 8.6 %fusion.85 = f32[640,1792]{1,0:T(8,128)S(1)} fusion(bf16[640,2048]{0,1:T(8,128)(2,1)S(1)} %fusion.2, bf16[2048,1792]{1,0:T(8,128)(2,1)} %param.16), kind=kOutput, calls=%fused_computation.172 | convolution fusion | flops 4697620480 | bytes 14548992 | tf_op jit(solution)/shard_map/dot_general | solution.py:147
  123.1 5.5 %fusion.84 = f32[640,1792]{1,0:T(8,128)S(1)} fusion(bf16[640,2048]{0,1:T(8,128)(2,1)S(1)} %fusion.2, bf16[2048,1792]{1,0:T(8,128)(2,1)S(1)} %bitcast.102), kind=kOutput, calls=%fused_computation.171 | convolution fusion | flops 4697620480 | bytes 14548992 | tf_op jit(solution)/shard_map/dot_general | solution.py:146
  128.6 5.0 %fusion.4 = f32[640,2048]{1,0:T(8,128)S(1)} fusion(bf16[1792,2048]{1,0:T(8,128)(2,1)S(1)} %bitcast.100, f32[640,1792]{1,0:T(8,128)S(1)} %fusion.85, f32[640,1792]{1,0:T(8,128)S(1)} %fusion.84), kind=kOutput, calls=%fused_computation.17 | convolution fusion | flops 4704501760 | bytes 21757952 | tf_op jit(solution)/shard_map/dot_general | solution.py:150
  138.9 5.5 %all-to-all-done.4 = bf16[4,20,512]{2,1,0:T(8,128)(2,1)S(1)} async-done(((bf16[4,20,512]{2,1,0:T(8,128)(2,1)}), bf16[4,20,512]{2,1,0:T(8,128)(2,1)S(1)}, u32[]{:S(2)}, u32[]{:S(2)}) %all-to-all-start.4) | async-done | bytes 81952 | tf_op jit(solution)/shard_map/all_to_all | solution.py:41
  150.6 7.2 %all-to-all-done.5 = bf16[32,2,256]{2,1,0:T(2,128)(2,1)S(1)} async-done(((bf16[32,2,256]{2,1,0:T(2,128)(2,1)}), bf16[32,2,256]{2,1,0:T(2,128)(2,1)S(1)}, u32[]{:S(2)}, u32[]{:S(2)}) %all-to-all-start.5) | async-done | bytes 32800 | tf_op jit(solution)/shard_map/all_to_all | solution.py:162
  158.0 22.9 %all_gather.10 = bf16[256,512]{1,0:T(8,128)(2,1)S(1)} all-gather(bf16[8,512]{1,0:T(8,128)(2,1)S(1)} %divide_convert_fusion), channel_id=1, replica_groups=mesh['dp'=32,'mp'=4] {'dp'}, dimensions={0}, use_global_device_ids=true | all-gather | bytes 270336 | tf_op jit(solution)/shard_map/all_gather | solution.py:176
  181.8 8.9 %all-reduce.1 = (bf16[256]{0:T(256)(128)(2,1)S(1)}, bf16[128]{0:T(256)(128)(2,1)S(1)}) all-reduce(bf16[256]{0:T(256)(128)(2,1)S(1)} %multiply_reduce_fusion.2, bf16[128]{0:T(256)(128)(2,1)S(1)} %multiply_reduce_fusion.3), channel_id=1, replica_groups=mesh['dp'=32,'mp'=4] {'mp'}, use_global_device_ids=true, to_apply=%region_15.16 | all-reduce | flops 384 | bytes 1536 | tf_op jit(solution)/shard_map/psum | solution.py:186
  190.8 37.5 %all-reduce.4.cloned.1.call-done = bf16[128,256]{0,1:T(8,128)(2,1)} async-done(((bf16[128,256]{0,1:T(8,128)(2,1)}), bf16[128,256]{0,1:T(8,128)(2,1)}) %all-reduce.4.cloned.1.call-update) | async-done | bytes 65552 | tf_op jit(solution)/shard_map/psum | solution.py:185
  232.6 7.2 %all-to-all-start.6 = ((bf16[32,8,513]{2,1,0:T(8,128)(2,1)}), bf16[32,8,513]{2,1,0:T(8,128)(2,1)S(1)}, u32[]{:S(2)}, u32[]{:S(2)}) async-start(bf16[32,8,513]{2,1,0:T(8,128)(2,1)} %pad_maximum_fusion), calls=%async_computation.6 | async-start | bytes 655360 | tf_op jit(solution)/shard_map/all_to_all | solution.py:41
  239.8 9.4 %all-to-all-done.6 = bf16[32,8,513]{2,1,0:T(8,128)(2,1)S(1)} async-done(((bf16[32,8,513]{2,1,0:T(8,128)(2,1)}), bf16[32,8,513]{2,1,0:T(8,128)(2,1)S(1)}, u32[]{:S(2)}, u32[]{:S(2)}) %all-to-all-start.6) | async-done | bytes 262688 | tf_op jit(solution)/shard_map/all_to_all | solution.py:41
  255.1 7.3 %all-to-all-done.7 = bf16[32,2,256]{2,1,0:T(2,128)(2,1)S(1)} async-done(((bf16[32,2,256]{2,1,0:T(2,128)(2,1)}), bf16[32,2,256]{2,1,0:T(2,128)(2,1)S(1)}, u32[]{:S(2)}, u32[]{:S(2)}) %all-to-all-start.7) | async-done | bytes 32800 | tf_op jit(solution)/shard_map/all_to_all | solution.py:231
  262.5 11.9 %all_gather.11 = bf16[20,2048]{1,0:T(8,128)(2,1)S(1)} all-gather(bf16[20,512]{1,0:T(8,128)(2,1)S(1)} %get-tuple-element.20), channel_id=1, replica_groups=mesh['dp'=32,'mp'=4] {'mp'}, dimensions={1}, use_global_device_ids=true | all-gather | bytes 102400 | tf_op jit(solution)/shard_map/all_gather | solution.py:241
  274.8 10.2 %fusion.86 = f32[640,1792]{1,0:T(8,128)} fusion(bf16[640,2048]{1,0:T(8,128)(2,1)S(1)} %fusion.3, bf16[1792,2048]{1,0:T(8,128)(2,1)} %param.17), kind=kOutput, calls=%fused_computation.173 | convolution fusion | flops 4697620480 | bytes 14548992 | tf_op jit(solution)/shard_map/dot_general | solution.py:58
  285.1 14.2 %fusion.7 = f32[640,2048]{1,0:T(8,128)} fusion(bf16[2048,1792]{1,0:T(8,128)(2,1)S(1)} %bitcast.104, f32[640,1792]{1,0:T(8,128)} %copy-done.6, f32[640,1792]{1,0:T(8,128)} %fusion.86, f32[640,1792]{1,0:T(8,128)} %copy-done.7), kind=kOutput, calls=%fused_computation.20 | convolution fusion | flops 4709089280 | bytes 26345472 | tf_op jit(solution)/shard_map/dot_general | solution.py:58
  299.3 13.7 %add_convert_fusion = bf16[640,2048]{1,0:T(8,128)(2,1)} fusion(f32[640,2048]{1,0:T(8,128)} %fusion.7, bf16[2048,1792]{1,0:T(8,128)(2,1)} %param.16, f32[640,1792]{1,0:T(8,128)} %fusion.86, f32[640,1792]{1,0:T(8,128)} %copy-done.6), kind=kOutput, calls=%fused_computation.10 | convolution fusion | flops 4707123200 | bytes 24379392 | tf_op jit(solution)/shard_map/dot_general | solution.py:58
  313.1 30.1 %reduce-scatter.2.cloned.1.call-done = bf16[640,512]{1,0:T(8,128)(2,1)} async-done(((bf16[640,2048]{1,0:T(8,128)(2,1)}), bf16[640,512]{1,0:T(8,128)(2,1)}) %reduce-scatter.2.cloned.1.call-update) | async-done | bytes 655376 | tf_op jit(solution)/shard_map/reduce_scatter | solution.py:257
  344.6 8.6 %psum.31 = f32[640]{0:T(1024)S(1)} all-reduce(f32[640]{0:T(1024)S(1)} %fusion.11), channel_id=1, replica_groups=mesh['dp'=32,'mp'=4] {'mp'}, use_global_device_ids=true, to_apply=%region_23.24 | all-reduce | flops 640 | bytes 5120 | tf_op jit(solution)/shard_map/psum | solution.py:261
  358.7 7.4 %all-to-all-start.8 = ((bf16[32,2,8192]{2,1,0:T(2,128)(2,1)}), bf16[32,2,8192]{2,1,0:T(2,128)(2,1)}, u32[]{:S(2)}, u32[]{:S(2)}) async-start(bf16[32,2,8192]{2,1,0:T(2,128)(2,1)} %reshape.479), calls=%async_computation.9 | async-start | bytes 2097152 | tf_op jit(solution)/shard_map/all_to_all | solution.py:271
  366.5 16.3 %all-to-all-done.8 = bf16[32,2,8192]{2,1,0:T(2,128)(2,1)} async-done(((bf16[32,2,8192]{2,1,0:T(2,128)(2,1)}), bf16[32,2,8192]{2,1,0:T(2,128)(2,1)}, u32[]{:S(2)}, u32[]{:S(2)}) %all-to-all-start.8) | async-done | bytes 1048608 | tf_op jit(solution)/shard_map/all_to_all | solution.py:271
  (145 shorter events, 75.6 us)
Async XLA Ops:
  7.2 39.5 %copy-start.3 = (s32[1024]{0:T(1024)S(1)}, s32[1024]{0:T(1024)}, u32[]{:S(2)}) copy-start(s32[1024]{0:T(1024)} %param.10) | copy-start | bytes 12292
  31.5 11.2 %all-to-all-start = ((bf16[32,1,1]{2,1,0:T(2,128)(2,1)}), bf16[32,1,1]{2,1,0:T(2,128)(2,1)S(1)}, u32[]{:S(2)}, u32[]{:S(2)}) async-start(bf16[32,1,1]{2,1,0:T(2,128)(2,1)} %copy.74), calls=%async_computation | async-start | bytes 32768 | tf_op jit(solution)/shard_map/all_to_all | solution.py:131
  42.7 20.7 %all-to-all-start.1 = ((bf16[32,1,32,512]{3,2,1,0:T(8,128)(2,1)}), bf16[32,1,32,512]{3,2,1,0:T(8,128)(2,1)S(1)}, u32[]{:S(2)}, u32[]{:S(2)}) async-start(bf16[32,1,32,512]{3,2,1,0:T(8,128)(2,1)} %bitcast.5), calls=%async_computation.1 | async-start | bytes 2097152 | tf_op jit(solution)/shard_map/all_to_all | solution.py:129
  63.4 11.4 %all-to-all-start.2 = ((bf16[32,1,32]{2,1,0:T(2,128)(2,1)}), bf16[32,1,32]{2,1,0:T(2,128)(2,1)S(1)}, u32[]{:S(2)}, u32[]{:S(2)}) async-start(bf16[32,1,32]{2,1,0:T(2,128)(2,1)} %copy.77), calls=%async_computation.2 | async-start | bytes 32768 | tf_op jit(solution)/shard_map/all_to_all | solution.py:130
  70.4 11.0 %copy-start.5 = (s32[2]{0:T(128)S(1)}, s32[2]{0:T(128)}, u32[]{:S(2)}) copy-start(s32[2]{0:T(128)} %param.11) | copy-start | bytes 28
  70.4 11.6 %copy-start.4 = (s32[128]{0:T(128)S(1)}, s32[128]{0:T(128)}, u32[]{:S(2)}) copy-start(s32[128]{0:T(128)} %param.12) | copy-start | bytes 1540
  76.6 37.2 %copy-start.2 = (f32[2048]{0:T(1024)S(1)}, f32[2048]{0:T(1024)}, u32[]{:S(2)}) copy-start(f32[2048]{0:T(1024)} %param.14) | copy-start | bytes 24580
  76.6 36.6 %all-to-all-start.3 = ((bf16[4,640,512]{1,2,0:T(8,128)(2,1)}), bf16[4,640,512]{1,2,0:T(8,128)(2,1)S(1)}, u32[]{:S(2)}, u32[]{:S(2)}) async-start(bf16[4,640,512]{1,2,0:T(8,128)(2,1)} %broadcast_in_dim.18), calls=%async_computation.3 | async-start | bytes 5242880 | tf_op jit(solution)/shard_map/all_to_all | solution.py:20
  113.7 9.3 %slice-start.2 = ((s8[7340032]{0:T(1024)(128)(4,1)}), s8[4194304]{0:T(1024)(128)(4,1)S(1)}, s32[]{:S(2)}) async-start(s8[7340032]{0:T(1024)(128)(4,1)} %bitcast.101), calls=%async_computation.14 | async-start | bytes 8388608
  113.7 14.9 %slice-start = ((s8[7340032]{0:T(1024)(128)(4,1)}), s8[4194304]{0:T(1024)(128)(4,1)S(1)}, s32[]{:S(2)}) async-start(s8[7340032]{0:T(1024)(128)(4,1)} %bitcast.99), calls=%async_computation.12 | async-start | bytes 8388608
  114.4 8.7 %slice-start.3 = ((s8[7340032]{0:T(1024)(128)(4,1)}), s8[3145728]{0:T(1024)(128)(4,1)S(1)}, s32[]{:S(2)}) async-start(s8[7340032]{0:T(1024)(128)(4,1)} %bitcast.101), calls=%async_computation.15 | async-start | bytes 6291456
  114.4 14.2 %slice-start.1 = ((s8[7340032]{0:T(1024)(128)(4,1)}), s8[3145728]{0:T(1024)(128)(4,1)S(1)}, s32[]{:S(2)}) async-start(s8[7340032]{0:T(1024)(128)(4,1)} %bitcast.99), calls=%async_computation.13 | async-start | bytes 6291456
  123.1 5.5 %copy-start.7 = (f32[640,1792]{1,0:T(8,128)}, f32[640,1792]{1,0:T(8,128)S(1)}, u32[]{:S(2)}) copy-start(f32[640,1792]{1,0:T(8,128)S(1)} %fusion.85) | copy-start | bytes 13762564
  128.6 5.0 %copy-start.6 = (f32[640,1792]{1,0:T(8,128)}, f32[640,1792]{1,0:T(8,128)S(1)}, u32[]{:S(2)}) copy-start(f32[640,1792]{1,0:T(8,128)S(1)} %fusion.84) | copy-start | bytes 13762564
  133.7 16.7 %copy-start.1 = (bf16[128,512]{1,0:T(8,128)(2,1)S(1)}, bf16[128,512]{1,0:T(8,128)(2,1)}, u32[]{:S(2)}) copy-start(bf16[128,512]{1,0:T(8,128)(2,1)} %param.13) | copy-start | bytes 393220
  135.3 9.1 %all-to-all-start.4 = ((bf16[4,20,512]{2,1,0:T(8,128)(2,1)}), bf16[4,20,512]{2,1,0:T(8,128)(2,1)S(1)}, u32[]{:S(2)}, u32[]{:S(2)}) async-start(bf16[4,20,512]{2,1,0:T(8,128)(2,1)} %copy.79), calls=%async_computation.4 | async-start | bytes 196608 | tf_op jit(solution)/shard_map/all_to_all | solution.py:41
  146.4 11.3 %all-to-all-start.5 = ((bf16[32,2,256]{2,1,0:T(2,128)(2,1)}), bf16[32,2,256]{2,1,0:T(2,128)(2,1)S(1)}, u32[]{:S(2)}, u32[]{:S(2)}) async-start(bf16[32,2,256]{2,1,0:T(2,128)(2,1)} %reshape.475), calls=%async_computation.5 | async-start | bytes 65536 | tf_op jit(solution)/shard_map/all_to_all | solution.py:162
  150.3 77.9 %all-reduce.4.cloned.1.call-start = ((), (), s32[]{:S(2)}) async-start(), calls=%async_computation.10 | async-start | bytes 131072 | tf_op jit(solution)/shard_map/psum | solution.py:185
  232.6 16.7 %all-to-all-start.6 = ((bf16[32,8,513]{2,1,0:T(8,128)(2,1)}), bf16[32,8,513]{2,1,0:T(8,128)(2,1)S(1)}, u32[]{:S(2)}, u32[]{:S(2)}) async-start(bf16[32,8,513]{2,1,0:T(8,128)(2,1)} %pad_maximum_fusion), calls=%async_computation.6 | async-start | bytes 655360 | tf_op jit(solution)/shard_map/all_to_all | solution.py:41
  251.1 11.3 %all-to-all-start.7 = ((bf16[32,2,256]{2,1,0:T(2,128)(2,1)}), bf16[32,2,256]{2,1,0:T(2,128)(2,1)S(1)}, u32[]{:S(2)}, u32[]{:S(2)}) async-start(bf16[32,2,256]{2,1,0:T(2,128)(2,1)} %reshape.477), calls=%async_computation.7 | async-start | bytes 65536 | tf_op jit(solution)/shard_map/all_to_all | solution.py:231
  254.9 88.3 %reduce-scatter.2.cloned.1.call-start = ((), (), s32[]{:S(2)}) async-start(), calls=%async_computation.11 | async-start | bytes 3276800 | tf_op jit(solution)/shard_map/reduce_scatter | solution.py:257
  274.5 10.6 %slice-start.4 = ((s8[7340032]{0:T(1024)(128)(4,1)}), s8[4194304]{0:T(1024)(128)(4,1)S(1)}, s32[]{:S(2)}) async-start(s8[7340032]{0:T(1024)(128)(4,1)} %bitcast.103), calls=%async_computation.16 | async-start | bytes 8388608
  274.8 10.2 %slice-start.5 = ((s8[7340032]{0:T(1024)(128)(4,1)}), s8[3145728]{0:T(1024)(128)(4,1)S(1)}, s32[]{:S(2)}) async-start(s8[7340032]{0:T(1024)(128)(4,1)} %bitcast.103), calls=%async_computation.17 | async-start | bytes 6291456
  358.7 24.1 %all-to-all-start.8 = ((bf16[32,2,8192]{2,1,0:T(2,128)(2,1)}), bf16[32,2,8192]{2,1,0:T(2,128)(2,1)}, u32[]{:S(2)}, u32[]{:S(2)}) async-start(bf16[32,2,8192]{2,1,0:T(2,128)(2,1)} %reshape.479), calls=%async_computation.9 | async-start | bytes 2097152 | tf_op jit(solution)/shard_map/all_to_all | solution.py:271
  (1 other events, 5.0 us)
Sparse Core Ops, SparseCore 0:
  190.9 37.3 all-reduce.3
  313.1 30.0 reduce-scatter.1
where the time goes:
time: 406 us; the launch traced here: 399 us
  waiting for transfers between devices  165 us (41%)
  blocking collectives  70.2 us (17%)
  matrix products  65.2 us (16%)
  starting transfers between devices  42.2 us (10%)
  local copies, waits for them, and re-layouts  26.3 us (6%)
  between operations  16.3 us (4%)
  other arithmetic  14.4 us (4%)
    dot_general x4, matrix products, contract_rows(): lax.dot_general(left, right, (((1,), (1,)), ((), ())), preferred_element_...  39 us
    psum x1, waiting for transfers between devices, per_device(): lax.psum(score_part.astype(jnp.bfloat16), 'mp').astype(jnp.float32)  37.5 us
    reduce_scatter x1, waiting for transfers between devices, per_device(): lax.psum_scatter(normed_grad.astype(jnp.bfloat16), 'mp', scatter_dimensio...  30.1 us
    all_to_all x1, waiting for transfers between devices, sent_to_all(): return lax.all_to_all(copies, axis, split_axis=0, concat_axis=0, tiled=True)  27.5 us
    all_gather x1, blocking collectives, per_device(): all_vec = lax.all_gather(passage_vec, 'dp', axis=0, tiled=True)  22.9 us
    unnamed x1, blocking collectives  18 us
    all_to_all x1, waiting for transfers between devices, per_device(): lax.all_to_all(back.reshape(dp_count, slot_count, block_len * part_width)...  16.3 us
    all_to_all x1, waiting for transfers between devices, per_device(): lax.all_to_all(send, 'dp', split_axis=0, concat_axis=0, tiled=True)  15.4 us
  transfers between devices with their start and end apart: 11, of which 11 were waited for; matrix products, arithmetic and copies ran while one was open for 3% of the time, Pallas kernels for 0%

commit v1 on v0

v1 whole, which is shorter than its diff:
```python
import functools

import jax
import jax.numpy as jnp
from jax import lax
from jax.experimental import pallas as pl
from jax.experimental.pallas import tpu as pltpu
from jax.sharding import Mesh, PartitionSpec as P

L = 128
pad_token = 128001
score_scale = 20.0
loss_seed = 4096.0
norm_epsilon = 1e-05
unit_epsilon = 1e-06
MP = 4
FT = 256
CHUNKS = (640, 384)
bf16 = jnp.bfloat16
f32 = jnp.float32


def shifted(x, by):
    return lax.ppermute(x, "mp", [(i, (i + by) % MP) for i in range(MP)])


def swapped(x):
    return lax.ppermute(x, "core", [(0, 1), (1, 0)])


def copies_to_all(x, axes, count):
    return lax.all_to_all(
        jnp.broadcast_to(x, (count, *x.shape)), axes, split_axis=0, concat_axis=0, tiled=True
    )


def encode_kernel(
    m_ref, own_ref, left_ref, right_ref, opp_ref, mask_ref, gain_ref, wg_ref, wu_ref,
    a_ref, b_ref, c_ref, pool_ref, rms_ref, xpool_ref, xs,
):
    passes = pool_ref.shape[0]
    m = m_ref[0]

    @pl.when(pl.program_id(0) == 0)
    def _():
        pieces = [own_ref, right_ref, opp_ref, left_ref]
        total = None
        for piece in pieces:
            v = piece[...].astype(f32)
            part = jnp.sum(v * v, axis=1, keepdims=True)
            total = part if total is None else total + part
        width = MP * own_ref.shape[1]
        rms = lax.rsqrt(total / width + norm_epsilon)
        rms_ref[...] = rms
        mask = mask_ref[...]
        for k, piece in enumerate(pieces):
            j = lax.rem(m + k, MP)
            v = piece[...].astype(f32)
            xs[j] = (v * rms * gain_ref[j]).astype(bf16)
            live = v * mask
            for p in range(passes):
                xpool_ref[j, p : p + 1] = jnp.sum(live[p * L : (p + 1) * L], axis=0, keepdims=True)

    part = own_ref.shape[1]
    gate = None
    up = None
    for j in range(MP):
        rows = slice(j * part, (j + 1) * part)
        g = jnp.dot(xs[j], wg_ref[rows], preferred_element_type=f32)
        u = jnp.dot(xs[j], wu_ref[rows], preferred_element_type=f32)
        gate = g if gate is None else gate + g
        up = u if up is None else up + u
    sig = jax.nn.sigmoid(gate)
    b = gate * sig
    act = (b * up).astype(bf16).astype(f32) * mask_ref[...]
    for p in range(passes):
        pool_ref[p : p + 1] = jnp.sum(act[p * L : (p + 1) * L], axis=0, keepdims=True)
    a = up * sig * (1.0 + gate * (1.0 - sig))
    a_ref[...] = a.astype(bf16)
    b_ref[...] = b.astype(bf16)
    c_ref[...] = (a * gate + b * up).astype(bf16)


def encode(m, own, left, right, opp, mask, gain, w_gate, w_up):
    rows, part = own.shape
    width, ff = w_gate.shape
    passes = rows // L
    whole = lambda n, m_: (0, 0)
    piece = pl.BlockSpec((rows, part), whole)
    column = pl.BlockSpec((rows, 1), whole)
    weight = pl.BlockSpec((width, FT), lambda n, m_: (0, n))
    tile = pl.BlockSpec((rows, FT), lambda n, m_: (0, n))
    return pl.pallas_call(
        encode_kernel,
        grid_spec=pltpu.PrefetchScalarGridSpec(
            num_scalar_prefetch=1,
            grid=(ff // FT,),
            in_specs=[piece] * 4
            + [column, pl.BlockSpec((MP, 1, part), lambda n, m_: (0, 0, 0)), weight, weight],
            out_specs=[tile, tile, tile]
            + [
                pl.BlockSpec((passes, FT), lambda n, m_: (0, n)),
                column,
                pl.BlockSpec((MP, passes, part), lambda n, m_: (0, 0, 0)),
            ],
            scratch_shapes=[pltpu.VMEM((MP, rows, part), bf16)],
        ),
        out_shape=[jax.ShapeDtypeStruct((rows, ff), bf16)] * 3
        + [
            jax.ShapeDtypeStruct((passes, ff), f32),
            jax.ShapeDtypeStruct((rows, 1), f32),
            jax.ShapeDtypeStruct((MP, passes, part), f32),
        ],
        compiler_params=pltpu.CompilerParams(vmem_limit_bytes=48 << 20),
        cost_estimate=pl.CostEstimate(
            flops=4 * rows * width * ff,
            transcendentals=rows * ff,
            bytes_accessed=4 * width * ff + 2 * rows * width + 6 * rows * ff,
        ),
        name="encode",
    )(m, own, left, right, opp, mask, gain, w_gate, w_up)


def back_kernel(with_sum, m_ref, a_ref, b_ref, *refs):
    if with_sum:
        c_ref, g_ref, mask_ref, wg_ref, wu_ref, out_ref, s_ref = refs
    else:
        g_ref, mask_ref, wg_ref, wu_ref, out_ref = refs
    rows = a_ref.shape[0]
    base = pl.program_id(1) * (rows // L)
    dg = []
    du = []
    for p in range(rows // L):
        part = slice(p * L, (p + 1) * L)
        dact = g_ref[pl.ds(base + p, 1)] * mask_ref[part]
        dg.append((dact * a_ref[part].astype(f32)).astype(bf16))
        du.append((dact * b_ref[part].astype(f32)).astype(bf16))
        if with_sum:
            s_ref[part] = jnp.sum(dact * c_ref[part].astype(f32), axis=1, keepdims=True)
    contract = (((1,), (1,)), ((), ()))
    out = lax.dot_general(jnp.concatenate(dg, 0), wg_ref[...], contract, preferred_element_type=f32)
    out += lax.dot_general(jnp.concatenate(du, 0), wu_ref[...], contract, preferred_element_type=f32)
    out_ref[0] = out.astype(bf16)


def back(m, steps, a, b, c, g, mask, w_gate, w_up):
    rows, ff = a.shape
    width = w_gate.shape[0]
    part = width // MP
    rt = 256
    first, stride = steps[0], (steps[1] - steps[0]) if len(steps) > 1 else 0
    with_sum = c is not None
    tile = pl.BlockSpec((rt, ff), lambda k, r, m_: (r, 0))
    column = pl.BlockSpec((rt, 1), lambda k, r, m_: (r, 0))
    weight = pl.BlockSpec((part, ff), lambda k, r, m_: (lax.rem(m_[0] + first + stride * k, MP), 0))
    out_specs = [pl.BlockSpec((1, rt, part), lambda k, r, m_: (k, r, 0))]
    out_shape = [jax.ShapeDtypeStruct((len(steps), rows, part), bf16)]
    if with_sum:
        out_specs.append(column)
        out_shape.append(jax.ShapeDtypeStruct((rows, 1), f32))
    return pl.pallas_call(
        functools.partial(back_kernel, with_sum),
        grid_spec=pltpu.PrefetchScalarGridSpec(
            num_scalar_prefetch=1,
            grid=(len(steps), rows // rt),
            in_specs=[tile, tile]
            + ([tile] if with_sum else [])
            + [pl.BlockSpec((g.shape[0], ff), lambda k, r, m_: (0, 0)), column, weight, weight],
            out_specs=out_specs,
        ),
        out_shape=out_shape,
        compiler_params=pltpu.CompilerParams(vmem_limit_bytes=48 << 20),
        cost_estimate=pl.CostEstimate(
            flops=4 * rows * part * len(steps) * ff,
            transcendentals=0,
            bytes_accessed=(4 * part * ff + 4 * rows * ff + 2 * rows * part) * len(steps),
        ),
        name="back",
    )(m, a, b, *([c] if with_sum else []), g, mask, w_gate, w_up)


def per_device(
    hidden_in, token_ids, passage_counts, positive_doc, queries, norm_gain, w_gate, w_up, w_down
):
    row_count, part = hidden_in.shape
    width = norm_gain.shape[0]
    docs = passage_counts.shape[0]
    passes = row_count // L
    most = passes // docs
    query_rows = queries.shape[0]
    share = query_rows // MP
    chips = lax.axis_size(("x", "z"))
    mi = lax.axis_index("mp")
    core = lax.axis_index("core")
    chip = lax.axis_index(("x", "z"))
    m = mi.astype(jnp.int32).reshape(1)

    chunks = []
    at = 0
    for rows in CHUNKS:
        own = hidden_in[at : at + rows]
        chunks.append((at, rows, own, shifted(own, 1), shifted(own, -1)))
        at += rows

    mine = lax.all_to_all(
        queries.reshape(MP, share, part), "mp", split_axis=0, concat_axis=0, tiled=True
    )
    mine = jnp.moveaxis(mine, 0, 1).reshape(share, width)
    own_positive = lax.dynamic_slice_in_dim(positive_doc, mi * share, share)
    extra = jnp.pad(own_positive.astype(bf16)[:, None], ((0, 0), (0, L - 1)))
    all_q = copies_to_all(jnp.concatenate([mine, extra], axis=1), ("x", "z"), chips)
    all_q = all_q.reshape(chips * share, width + L)
    q = all_q[:, :width]
    positive = all_q[:, width].astype(f32)
    q_float = q.astype(f32)
    query_scale = lax.rsqrt(jnp.sum(q_float * q_float, axis=1) + unit_epsilon)

    live_pass = jnp.arange(passes, dtype=jnp.int32) % most < jnp.repeat(passage_counts, most)
    token_live = (token_ids.reshape(passes, L) != pad_token) & live_pass[:, None]
    live_float = token_live.astype(f32)
    mask = live_float.reshape(row_count, 1)
    divisor = jnp.maximum(jnp.sum(live_float, axis=1), 1.0)[:, None]
    gain = norm_gain.reshape(MP, 1, part)

    done = []
    for at, rows, own, left, right in chunks:
        half = rows // 2
        opp = jnp.concatenate([shifted(left[:half], 1), shifted(right[half:], -1)], axis=0)
        done.append(
            encode(m, own, left, right, opp, mask[at : at + rows], gain, w_gate, w_up)
        )
    a, b, c, pool, rms = (jnp.concatenate([d[k] for d in done], axis=0) for k in range(5))
    xpool = jnp.concatenate([d[5] for d in done], axis=1)
    xpool = jnp.moveaxis(xpool, 0, 1).reshape(passes, width)

    high = pool.astype(bf16)
    low = (pool - high.astype(f32)).astype(bf16)
    branch = jnp.dot(jnp.concatenate([high, low], 0), w_down, preferred_element_type=f32)
    branch = (branch[:passes] + branch[passes:]).astype(bf16)
    branch = copies_to_all(branch, "mp", MP).astype(f32).sum(axis=0)
    vec = ((xpool + branch) / divisor).astype(bf16)

    flag = jnp.broadcast_to(live_pass.astype(bf16)[:, None], (passes, L))
    packed = jnp.concatenate([vec, flag], axis=1)
    packed = jnp.concatenate([packed, swapped(packed)], axis=0)
    vecs = packed[:, :width]
    live = packed[:, width].astype(f32)[:, None]
    vec_float = vecs.astype(f32)
    vec_scale = lax.rsqrt(jnp.sum(vec_float * vec_float, axis=1, keepdims=True) + unit_epsilon)

    raw = lax.dot_general(vecs, q, (((1,), (1,)), ((), ())), preferred_element_type=f32)
    weights = live * jnp.exp(score_scale * raw * query_scale[None, :] * vec_scale)
    first_doc = (chip * 2 + core) * docs
    other_doc = (chip * 2 + 1 - core) * docs
    k = jnp.arange(2 * passes, dtype=jnp.int32)
    doc = jnp.where(k < passes, first_doc + k // most, other_doc + (k - passes) // most)
    hit = (positive[None, :] == doc.astype(f32)[:, None]).astype(f32)
    mass = jnp.stack([jnp.sum(weights, axis=0), jnp.sum(weights * hit, axis=0)])
    mass = copies_to_all(mass.reshape(8, -1), ("x", "z"), chips).sum(axis=0).reshape(2, -1)
    total, held = mass[0], mass[1]
    loss = jnp.log(total) - jnp.log(held)
    own_loss = lax.dynamic_slice_in_dim(loss, chip * share, share)

    coef = (loss_seed * score_scale) * query_scale[None, :] * (
        weights / total[None, :] - hit * weights / held[None, :]
    )
    grad = jnp.dot(coef.astype(bf16), q, preferred_element_type=f32)
    term = jnp.sum(coef * raw, axis=1, keepdims=True)
    grad = jnp.concatenate([grad, jnp.broadcast_to(term, (2 * passes, L))], axis=1)
    grad = grad[:passes] + swapped(grad[passes:])
    grad = copies_to_all(grad.astype(bf16), "mp", MP).astype(f32).sum(axis=0)
    scale = vec_scale[:passes]
    change = scale * grad[:, :width] - vec_float[:passes] * (scale**3 * grad[:, width : width + 1])
    token_grad = (change / divisor).astype(bf16)
    dact = lax.dot_general(token_grad, w_down, (((1,), (1,)), ((), ())), preferred_element_type=f32)

    half = row_count // 2
    opp, s = back(m, (2,), a, b, c, dact, mask, w_gate, w_up)
    opp = opp[0]
    from_right = shifted(opp[:half], -1)
    from_left = shifted(opp[half:], 1)
    sides = back(m, (1, 3), a, b, None, dact, mask, w_gate, w_up)[0]
    right, left = sides[0], sides[1]
    left_low = shifted(left[half:], -1)
    right_high = shifted(right[:half], 1)
    left_high = shifted((left[:half].astype(f32) + from_right.astype(f32)).astype(bf16), -1)
    right_low = shifted((right[half:].astype(f32) + from_left.astype(f32)).astype(bf16), 1)
    own = back(m, (0,), a, b, None, dact, mask, w_gate, w_up)[0][0]
    small = jnp.concatenate(
        [s.reshape(passes, L), jnp.pad(own_loss[None, :], ((0, 7), (0, L - share)))], axis=0
    )
    small = copies_to_all(small, "mp", MP)
    inner = small[:, :passes].sum(axis=0).reshape(row_count, 1) / width
    query_loss = small[:, passes, :share].reshape(MP * share)
    normed_grad = own.astype(f32) + jnp.concatenate(
        [
            left_high.astype(f32) + right_high.astype(f32),
            left_low.astype(f32) + right_low.astype(f32),
        ],
        axis=0,
    )
    own_gain = lax.dynamic_slice_in_dim(norm_gain, mi * part, part)
    own_token = lax.dynamic_slice_in_dim(token_grad, mi * part, part, axis=1).astype(f32)
    own_out = (live_float[:, :, None] * own_token[:, None, :]).reshape(row_count, part)
    hidden_grad = (
        own_out
        + rms * own_gain[None, :] * normed_grad
        - hidden_in.astype(f32) * (rms * rms * inner)
    )
    return query_loss, hidden_grad.astype(bf16)


def solution(mesh):
    shape = (4, 4, 2, MP)
    split = Mesh(mesh.devices.reshape(shape), ("x", "z", "core", "mp"))
    dp = ("x", "z", "core")
    return jax.shard_map(
        per_device,
        mesh=split,
        in_specs=(
            P(dp, "mp"),
            P(dp),
            P(dp),
            P(dp),
            P(dp, "mp"),
            P(),
            P(None, "mp"),
            P(None, "mp"),
            P("mp", None),
        ),
        out_specs=(P(dp), P(dp, "mp")),
        check_vma=False,
    )
```

time: 406 us -> 250 us (0.62); the launches traced: 399 us -> 249 us
  waiting for transfers between devices: 165 us -> 84.8 us
  blocking collectives: 70.2 us -> 0 us
  Pallas kernels: 0 us -> 60.6 us
  matrix products: 65.2 us -> 10.4 us
  between operations: 16.3 us -> 1.16 us
  local copies, waits for them, and re-layouts: 26.3 us -> 32.2 us
    pallas_call x0 -> x5, Pallas kernels: none -> 60.6 us  [the longest x3 31.8 us: back(): pl.pallas_call(functools.partial(back_kernel, with_sum), grid_spec=pltpu....]
    dot_general x18 -> x4, matrix products: 65.2 us -> 10.4 us  [the longest x1 5.08 us: per_device(): lax.dot_general(token_grad, w_down, (((1,), (1,)), ((), ())), preferred_e...]
    all_to_all x9 -> x6, waiting for transfers between devices: 96.9 us -> 55.8 us  [the longest x5 40.4 us: copies_to_all(): lax.all_to_all(jnp.broadcast_to(x, (count, *x.shape)), axes, split_axis=0...]
    psum x1 -> x0, waiting for transfers between devices: 37.5 us -> none  [per_device(): lax.psum(score_part.astype(jnp.bfloat16), 'mp').astype(jnp.float32)]
    all_gather x2 -> x0, blocking collectives: 34.8 us -> none  [the longest x1 22.9 us: per_device(): all_vec = lax.all_gather(passage_vec, 'dp', axis=0, tiled=True)]
    reduce_scatter x1 -> x0, waiting for transfers between devices: 30.1 us -> none  [per_device(): lax.psum_scatter(normed_grad.astype(jnp.bfloat16), 'mp', scatter_dimensio...]
    ppermute x0 -> x16, waiting for transfers between devices: none -> 29 us  [the longest x14 26.7 us: shifted(): return lax.ppermute(x, 'mp', [(i, (i + by) % MP) for i in range(MP)])]
    unnamed x1 -> x0, blocking collectives: 18 us -> none
  transfers between devices with their start and end apart: 11 -> 22, of which waited for: 11 -> 13; matrix products, arithmetic and copies ran while one was open for 3% -> 8% of each run, Pallas kernels for 0% -> 8%
where the time goes in v1:
time: 250 us; the launch traced here: 249 us
  waiting for transfers between devices  84.8 us (34%)
  Pallas kernels  60.6 us (24%)
  starting transfers between devices  45.6 us (18%)
  local copies, waits for them, and re-layouts  32.2 us (13%)
  other arithmetic  14 us (6%)
  matrix products  10.4 us (4%)
    all_to_all x5, waiting for transfers between devices, copies_to_all(): lax.all_to_all(jnp.broadcast_to(x, (count, *x.shape)), axes, split_axis=0...  40.4 us
    pallas_call x3, Pallas kernels, back(): pl.pallas_call(functools.partial(back_kernel, with_sum), grid_spec=pltpu....  31.8 us
    pallas_call x2, Pallas kernels, encode(): pl.pallas_call(encode_kernel, grid_spec=pltpu.PrefetchScalarGridSpec(num_...  28.8 us
    ppermute x14, waiting for transfers between devices, shifted(): return lax.ppermute(x, 'mp', [(i, (i + by) % MP) for i in range(MP)])  26.7 us
    all_to_all x5, starting transfers between devices, copies_to_all(): lax.all_to_all(jnp.broadcast_to(x, (count, *x.shape)), axes, split_axis=0...  23.9 us
    ppermute x14, starting transfers between devices, shifted(): return lax.ppermute(x, 'mp', [(i, (i + by) % MP) for i in range(MP)])  16.9 us
    unnamed x68, local copies, waits for them, and re-layouts  15.7 us
    all_to_all x1, waiting for transfers between devices, per_device(): lax.all_to_all(queries.reshape(MP, share, part), 'mp', split_axis=0, conc...  15.4 us
  transfers between devices with their start and end apart: 22, of which 13 were waited for; matrix products, arithmetic and copies ran while one was open for 8% of the time, Pallas kernels for 8%

profile of v1, /device:TPU:0, one launch (start us, length us, event | category | flops | bytes accessed | tf_op | source)
XLA Modules:
  0.0 248.7 jit_solution(6164619213128638335)
XLA Ops:
  1.7 3.2 %collective-permute-start.5 = (bf16[384,512]{1,0:T(8,128)(2,1)S(1)}, bf16[384,512]{1,0:T(8,128)(2,1)}, u32[]{:S(2)}, u32[]{:S(2)}) collective-permute-start(bf16[384,512]{1,0:T(8,128)(2,1)S(1)} %slice.126.own_ref), channel_id=1, source_target_pairs={{0,3},{1,0},{2,1},{3,2},{4,7},{5,4},{6,5},{7,6},{8,11},{9,8},{10,9... | collective-permute-start | bytes 1179656 | tf_op jit(solution)/shard_map/ppermute | solution.py:24
  6.0 3.3 %collective-permute-start.1 = (bf16[640,512]{1,0:T(8,128)(2,1)S(1)}, bf16[640,512]{1,0:T(8,128)(2,1)S(1)}, u32[]{:S(2)}, u32[]{:S(2)}) collective-permute-start(bf16[640,512]{1,0:T(8,128)(2,1)S(1)} %slice.121.own_ref), channel_id=1, source_target_pairs={{0,3},{1,0},{2,1},{3,2},{4,7},{5,4},{6,5},{7,6},{8,11},{9,8},{10,9... | collective-permute-start | bytes 1966088 | tf_op jit(solution)/shard_map/ppermute | solution.py:24
  9.3 4.5 %all-to-all-start.1 = ((bf16[4,32,512]{2,1,0:T(8,128)(2,1)}), bf16[4,32,512]{2,1,0:T(8,128)(2,1)}, u32[]{:S(2)}, u32[]{:S(2)}) async-start(bf16[4,32,512]{2,1,0:T(8,128)(2,1)} %bitcast.93), calls=%async_computation.1 | async-start | bytes 262144 | tf_op jit(solution)/shard_map/all_to_all | solution.py:205
  16.8 15.4 %all-to-all-done.1 = bf16[4,32,512]{2,1,0:T(8,128)(2,1)} async-done(((bf16[4,32,512]{2,1,0:T(8,128)(2,1)}), bf16[4,32,512]{2,1,0:T(8,128)(2,1)}, u32[]{:S(2)}, u32[]{:S(2)}) %all-to-all-start.1) | async-done | bytes 131104 | tf_op jit(solution)/shard_map/all_to_all | solution.py:205
  46.0 12.2 %encode.3 = (bf16[384,1792]{1,0:T(8,128)(2,1)S(1)}, bf16[384,1792]{1,0:T(8,128)(2,1)S(1)}, bf16[384,1792]{1,0:T(8,128)(2,1)S(1)}, f32[3,1792]{1,0:T(4,128)S(1)},...) custom-call(s32[1]{0:T(128)} %bitcast.m_ref, bf16[384,512]{1,0:T(8,128)(2,1)S(1)} %slice.126.own_ref, ...), custom_call_target="tpu_custom_call" | custom-call | flops 5637144576 | bytes 20381696 | tf_op jit(solution)/shard_map/encode/pallas_call | solution.py:93
  66.8 16.5 %encode.2 = (bf16[640,1792]{1,0:T(8,128)(2,1)S(1)}, bf16[640,1792]{1,0:T(8,128)(2,1)}, bf16[640,1792]{1,0:T(8,128)(2,1)}, f32[5,1792]{1,0:T(8,128)S(1)}, f32[640,1]{1,0:T(8,128)S(1)}, /*index=5*/f32[4,5,512]{2,1,0:T(8,128)S(1)}) custom-call(s32[1]{0:T(128)} %bitcast.m_ref, bf16[640,512]{1,0:T(8,128)(2,1)S(1)} %copy-done.10, bf16[640,512]{1,0:T(8,128)(2,1)S(1)} %copy-done.14, ...), custom_call_target="tpu_custom_call" | custom-call | flops 9395240960 | bytes 24182784 | tf_op jit(solution)/shard_map/encode/pallas_call | solution.py:93
  84.1 4.2 %fusion.20 = f32[16,2048]{1,0:T(8,128)S(1)} fusion(bf16[1792,2048]{1,0:T(8,128)(2,1)} %param.17, bf16[8,1792]{1,0:T(8,128)(2,1)S(1)} %subtract_convert_fusion, bf16[8,1792]{1,0:T(8,128)(2,1)S(1)} %fusion.24), kind=kOutput, calls=%fused_computation.52 | convolution fusion | flops 117555200 | bytes 7528448 | tf_op jit(solution)/shard_map/dot_general | solution.py:238
  89.0 3.3 %all-to-all-start = ((bf16[4,8,2048]{2,1,0:T(8,128)(2,1)}), bf16[4,8,2048]{2,1,0:T(8,128)(2,1)S(1)}, u32[]{:S(2)}, u32[]{:S(2)}) async-start(bf16[4,8,2048]{2,1,0:T(8,128)(2,1)} %broadcast_in_dim.21), calls=%async_computation | async-start | bytes 262144 | tf_op jit(solution)/shard_map/all_to_all | solution.py:32
  104.7 8.0 %all-to-all-start.2 = ((bf16[16,32,2176]{2,1,0:T(8,128)(2,1)}), bf16[16,32,2176]{2,1,0:T(8,128)(2,1)S(1)}, u32[]{:S(2)}, u32[]{:S(2)}) async-start(bf16[16,32,2176]{2,1,0:T(8,128)(2,1)} %broadcast_in_dim.24), calls=%async_computation.2 | async-start | bytes 4456448 | tf_op jit(solution)/shard_map/all_to_all | solution.py:32
  114.6 26.9 %all-to-all-done.2 = bf16[16,32,2176]{2,1,0:T(8,128)(2,1)S(1)} async-done(((bf16[16,32,2176]{2,1,0:T(8,128)(2,1)}), bf16[16,32,2176]{2,1,0:T(8,128)(2,1)S(1)}, u32[]{:S(2)}, u32[]{:S(2)}) %all-to-all-start.2) | async-done | bytes 2228256 | tf_op jit(solution)/shard_map/all_to_all | solution.py:32
  143.4 4.7 %all-to-all-start.3 = ((f32[16,8,128]{2,1,0:T(8,128)}), f32[16,8,128]{2,1,0:T(8,128)S(1)}, u32[]{:S(2)}, u32[]{:S(2)}) async-start(f32[16,8,128]{2,1,0:T(8,128)} %broadcast_in_dim.25), calls=%async_computation.3 | async-start | bytes 131072 | tf_op jit(solution)/shard_map/all_to_all | solution.py:32
  148.2 7.6 %all-to-all-done.3 = f32[16,8,128]{2,1,0:T(8,128)S(1)} async-done(((f32[16,8,128]{2,1,0:T(8,128)}), f32[16,8,128]{2,1,0:T(8,128)S(1)}, u32[]{:S(2)}, u32[]{:S(2)}) %all-to-all-start.3) | async-done | bytes 65568 | tf_op jit(solution)/shard_map/all_to_all | solution.py:32
  158.6 4.6 %all-to-all-start.4 = ((bf16[4,8,2176]{2,1,0:T(8,128)(2,1)}), bf16[4,8,2176]{2,1,0:T(8,128)(2,1)S(1)}, u32[]{:S(2)}, u32[]{:S(2)}) async-start(bf16[4,8,2176]{2,1,0:T(8,128)(2,1)} %broadcast_in_dim.54), calls=%async_computation.4 | async-start | bytes 278528 | tf_op jit(solution)/shard_map/all_to_all | solution.py:32
  163.3 5.9 %all-to-all-done.4 = bf16[4,8,2176]{2,1,0:T(8,128)(2,1)S(1)} async-done(((bf16[4,8,2176]{2,1,0:T(8,128)(2,1)}), bf16[4,8,2176]{2,1,0:T(8,128)(2,1)S(1)}, u32[]{:S(2)}, u32[]{:S(2)}) %all-to-all-start.4) | async-done | bytes 139296 | tf_op jit(solution)/shard_map/all_to_all | solution.py:32
  169.4 5.1 %fusion.43.refs_1_.refs_0_ = f32[8,1792]{1,0:T(8,128)S(1)} fusion(bf16[8,2048]{1,0:T(8,128)(2,1)S(1)} %fusion.18, bf16[1792,2048]{1,0:T(8,128)(2,1)} %param.17), kind=kOutput, calls=%fused_computation.120 | convolution fusion | flops 58720256 | bytes 7430144 | tf_op jit(solution)/shard_map/dot_general | solution.py:275
  174.5 14.2 %back.5 = bf16[2,1024,512]{2,1,0:T(8,128)(2,1)S(1)} custom-call(s32[1]{0:T(128)} %bitcast.m_ref, bf16[1024,1792]{1,0:T(8,128)(2,1)} %get-tuple-element.49.a_ref, bf16[1024,1792]{1,0:T(8,128)(2,1)} %copy-done.18, f32[8,1792]{1,0:T(8,128)S(1)} %fusion.43.refs_1_.refs_0_, f32[1024,1]{1,0:T(8,128)S(1)} %copy.53.refs_2_.refs_1_, bf16[2048,1792]{1,0:T(8,128)(2,1)} %refs_2_.3, ...), custom_call_target="tpu_custom_call" | custom-call | flops 7516192768 | bytes 24117248 | tf_op jit(solution)/shard_map/back/pallas_call | solution.py:161
  188.7 9.9 %back.3 = (bf16[1,1024,512]{2,1,0:T(8,128)(2,1)S(1)}, f32[1024,1]{1,0:T(8,128)S(1)}) custom-call(s32[1]{0:T(128)} %bitcast.m_ref, bf16[1024,1792]{1,0:T(8,128)(2,1)} %get-tuple-element.49.a_ref, bf16[1024,1792]{1,0:T(8,128)(2,1)} %copy-done.18, bf16[1024,1792]{1,0:T(8,128)(2,1)} %pad_maximum_fusion.refs_0_, f32[8,1792]{1,0:T(8,128)S(1)} %fusion.43.refs_1_.refs_0_, ...), custom_call_target="tpu_custom_call" | custom-call | flops 3758096384 | bytes 12058624 | tf_op jit(solution)/shard_map/back/pallas_call | solution.py:161
  200.4 3.3 %all-to-all-start.5 = ((f32[4,16,128]{2,1,0:T(8,128)}), f32[4,16,128]{2,1,0:T(8,128)S(1)}, u32[]{:S(2)}, u32[]{:S(2)}) async-start(f32[4,16,128]{2,1,0:T(8,128)} %broadcast_in_dim.56), calls=%async_computation.5 | async-start | bytes 65536 | tf_op jit(solution)/shard_map/all_to_all | solution.py:32
  205.0 3.3 %collective-permute-start.10 = (bf16[512,512]{1,0:T(8,128)(2,1)S(1)}, bf16[512,512]{1,0:T(8,128)(2,1)S(1)}, u32[]{:S(2)}, u32[]{:S(2)}) collective-permute-start(bf16[512,512]{1,0:T(8,128)(2,1)S(1)} %get-tuple-element.40), channel_id=1, source_target_pairs={{0,3},{1,0},{2,1},{3,2},{4,7},{5,4},{6,5},{7,6},{8,11},{9,8},{10,9... | collective-permute-start | bytes 1572872 | tf_op jit(solution)/shard_map/ppermute | solution.py:24
  210.0 7.7 %back.4 = bf16[1,1024,512]{2,1,0:T(8,128)(2,1)S(1)} custom-call(s32[1]{0:T(128)} %bitcast.m_ref, bf16[1024,1792]{1,0:T(8,128)(2,1)} %get-tuple-element.49.a_ref, bf16[1024,1792]{1,0:T(8,128)(2,1)} %copy-done.18, f32[8,1792]{1,0:T(8,128)S(1)} %fusion.43.refs_1_.refs_0_, f32[1024,1]{1,0:T(8,128)S(1)} %copy.53.refs_2_.refs_1_, bf16[2048,1792]{1,0:T(8,128)(2,1)} %refs_2_.3, ...), custom_call_target="tpu_custom_call" | custom-call | flops 3758096384 | bytes 12058624 | tf_op jit(solution)/shard_map/back/pallas_call | solution.py:161
  218.0 6.3 %collective-permute-done.14 = bf16[512,512]{1,0:T(8,128)(2,1)S(1)} collective-permute-done((bf16[512,512]{1,0:T(8,128)(2,1)S(1)}, bf16[512,512]{1,0:T(8,128)(2,1)S(1)}, u32[]{:S(2)}, u32[]{:S(2)}) %collective-permute-start.14) | collective-permute-done | bytes 524320 | tf_op jit(solution)/shard_map/ppermute | solution.py:24
  228.2 7.4 %collective-permute-done.12 = bf16[512,512]{1,0:T(8,128)(2,1)} collective-permute-done((bf16[512,512]{1,0:T(8,128)(2,1)}, bf16[512,512]{1,0:T(8,128)(2,1)}, u32[]{:S(2)}, u32[]{:S(2)}) %collective-permute-start.12) | collective-permute-done | bytes 524320 | tf_op jit(solution)/shard_map/ppermute | solution.py:24
  235.7 3.9 %collective-permute-done.11 = bf16[512,512]{1,0:T(8,128)(2,1)} collective-permute-done((bf16[512,512]{1,0:T(8,128)(2,1)}, bf16[512,512]{1,0:T(8,128)(2,1)}, u32[]{:S(2)}, u32[]{:S(2)}) %collective-permute-start.11) | collective-permute-done | bytes 524320 | tf_op jit(solution)/shard_map/ppermute | solution.py:24
  240.9 4.3 %collective-permute-done.13 = bf16[512,512]{1,0:T(8,128)(2,1)} collective-permute-done((bf16[512,512]{1,0:T(8,128)(2,1)S(1)}, bf16[512,512]{1,0:T(8,128)(2,1)}, u32[]{:S(2)}, u32[]{:S(2)}) %collective-permute-start.13) | collective-permute-done | bytes 524320 | tf_op jit(solution)/shard_map/ppermute | solution.py:24
  (175 shorter events, 61.8 us)
Async XLA Ops:
  1.7 31.4 %collective-permute-start.5 = (bf16[384,512]{1,0:T(8,128)(2,1)S(1)}, bf16[384,512]{1,0:T(8,128)(2,1)}, u32[]{:S(2)}, u32[]{:S(2)}) collective-permute-start(bf16[384,512]{1,0:T(8,128)(2,1)S(1)} %slice.126.own_ref), channel_id=1, source_target_pairs={{0,3},{1,0},{2,1},{3,2},{4,7},{5,4},{6,5},{7,6},{8,11},{9,8},{10,9... | collective-permute-start | bytes 1179656 | tf_op jit(solution)/shard_map/ppermute | solution.py:24
  4.9 29.6 %collective-permute-start.4 = (bf16[384,512]{1,0:T(8,128)(2,1)S(1)}, bf16[384,512]{1,0:T(8,128)(2,1)}, u32[]{:S(2)}, u32[]{:S(2)}) collective-permute-start(bf16[384,512]{1,0:T(8,128)(2,1)S(1)} %slice.126.own_ref), channel_id=1, source_target_pairs={{0,1},{1,2},{2,3},{3,0},{4,5},{5,6},{6,7},{7,4},{8,9},{9,10},{10,1... | collective-permute-start | bytes 1179656 | tf_op jit(solution)/shard_map/ppermute | solution.py:24
  6.0 38.0 %copy-start.9 = (bf16[640,512]{1,0:T(8,128)(2,1)}, bf16[640,512]{1,0:T(8,128)(2,1)S(1)}, u32[]{:S(2)}) copy-start(bf16[640,512]{1,0:T(8,128)(2,1)S(1)} %slice.121.own_ref) | copy-start | bytes 1966084
  6.0 36.3 %collective-permute-start.1 = (bf16[640,512]{1,0:T(8,128)(2,1)S(1)}, bf16[640,512]{1,0:T(8,128)(2,1)S(1)}, u32[]{:S(2)}, u32[]{:S(2)}) collective-permute-start(bf16[640,512]{1,0:T(8,128)(2,1)S(1)} %slice.121.own_ref), channel_id=1, source_target_pairs={{0,3},{1,0},{2,1},{3,2},{4,7},{5,4},{6,5},{7,6},{8,11},{9,8},{10,9... | collective-permute-start | bytes 1966088 | tf_op jit(solution)/shard_map/ppermute | solution.py:24
  9.3 33.9 %collective-permute-start = (bf16[640,512]{1,0:T(8,128)(2,1)S(1)}, bf16[640,512]{1,0:T(8,128)(2,1)S(1)}, u32[]{:S(2)}, u32[]{:S(2)}) collective-permute-start(bf16[640,512]{1,0:T(8,128)(2,1)S(1)} %slice.121.own_ref), channel_id=1, source_target_pairs={{0,1},{1,2},{2,3},{3,0},{4,5},{5,6},{6,7},{7,4},{8,9},{9,10},{10,1... | collective-permute-start | bytes 1966088 | tf_op jit(solution)/shard_map/ppermute | solution.py:24
  9.3 22.9 %all-to-all-start.1 = ((bf16[4,32,512]{2,1,0:T(8,128)(2,1)}), bf16[4,32,512]{2,1,0:T(8,128)(2,1)}, u32[]{:S(2)}, u32[]{:S(2)}) async-start(bf16[4,32,512]{2,1,0:T(8,128)(2,1)} %bitcast.93), calls=%async_computation.1 | async-start | bytes 262144 | tf_op jit(solution)/shard_map/all_to_all | solution.py:205
  34.1 5.7 %collective-permute-start.7 = (bf16[192,512]{1,0:T(8,128)(2,1)S(1)}, bf16[192,512]{1,0:T(8,128)(2,1)S(1)}, u32[]{:S(2)}, u32[]{:S(2)}) collective-permute-start(bf16[192,512]{1,0:T(8,128)(2,1)S(1)} %slice.163), channel_id=1, source_target_pairs={{0,3},{1,0},{2,1},{3,2},{4,7},{5,4},{6,5},{7,6},{8,11},{9,8},{10,9... | collective-permute-start | bytes 589832 | tf_op jit(solution)/shard_map/ppermute | solution.py:24
  35.4 6.9 %collective-permute-start.6 = (bf16[192,512]{1,0:T(8,128)(2,1)S(1)}, bf16[192,512]{1,0:T(8,128)(2,1)S(1)}, u32[]{:S(2)}, u32[]{:S(2)}) collective-permute-start(bf16[192,512]{1,0:T(8,128)(2,1)S(1)} %slice.162), channel_id=1, source_target_pairs={{0,1},{1,2},{2,3},{3,0},{4,5},{5,6},{6,7},{7,4},{8,9},{9,10},{10,1... | collective-permute-start | bytes 589832 | tf_op jit(solution)/shard_map/ppermute | solution.py:24
  43.2 19.2 %collective-permute-start.3 = (bf16[320,512]{1,0:T(8,128)(2,1)}, bf16[320,512]{1,0:T(8,128)(2,1)}, u32[]{:S(2)}, u32[]{:S(2)}) collective-permute-start(bf16[320,512]{1,0:T(8,128)(2,1)} %slice.161), channel_id=1, source_target_pairs={{0,3},{1,0},{2,1},{3,2},{4,7},{5,4},{6,5},{7,6},{8,11},{9,8},{10,9... | collective-permute-start | bytes 983048 | tf_op jit(solution)/shard_map/ppermute | solution.py:24
  44.0 18.4 %collective-permute-start.2 = (bf16[320,512]{1,0:T(8,128)(2,1)}, bf16[320,512]{1,0:T(8,128)(2,1)}, u32[]{:S(2)}, u32[]{:S(2)}) collective-permute-start(bf16[320,512]{1,0:T(8,128)(2,1)} %slice.160), channel_id=1, source_target_pairs={{0,1},{1,2},{2,3},{3,0},{4,5},{5,6},{6,7},{7,4},{8,9},{9,10},{10,1... | collective-permute-start | bytes 983048 | tf_op jit(solution)/shard_map/ppermute | solution.py:24
  89.0 14.1 %all-to-all-start = ((bf16[4,8,2048]{2,1,0:T(8,128)(2,1)}), bf16[4,8,2048]{2,1,0:T(8,128)(2,1)S(1)}, u32[]{:S(2)}, u32[]{:S(2)}) async-start(bf16[4,8,2048]{2,1,0:T(8,128)(2,1)} %broadcast_in_dim.21), calls=%async_computation | async-start | bytes 262144 | tf_op jit(solution)/shard_map/all_to_all | solution.py:32
  104.7 36.8 %all-to-all-start.2 = ((bf16[16,32,2176]{2,1,0:T(8,128)(2,1)}), bf16[16,32,2176]{2,1,0:T(8,128)(2,1)S(1)}, u32[]{:S(2)}, u32[]{:S(2)}) async-start(bf16[16,32,2176]{2,1,0:T(8,128)(2,1)} %broadcast_in_dim.24), calls=%async_computation.2 | async-start | bytes 4456448 | tf_op jit(solution)/shard_map/all_to_all | solution.py:32
  112.7 29.4 %copy-start.26 = (f32[16]{0:T(128)S(1)}, f32[16]{0:T(128)}, u32[]{:S(2)}) copy-start(f32[16]{0:T(128)} %fusion.38) | copy-start | bytes 196
  112.9 1.4 collective-permute-start.8
  143.4 12.4 %all-to-all-start.3 = ((f32[16,8,128]{2,1,0:T(8,128)}), f32[16,8,128]{2,1,0:T(8,128)S(1)}, u32[]{:S(2)}, u32[]{:S(2)}) async-start(f32[16,8,128]{2,1,0:T(8,128)} %broadcast_in_dim.25), calls=%async_computation.3 | async-start | bytes 131072 | tf_op jit(solution)/shard_map/all_to_all | solution.py:32
  156.6 1.3 collective-permute-start.9
  158.6 10.6 %all-to-all-start.4 = ((bf16[4,8,2176]{2,1,0:T(8,128)(2,1)}), bf16[4,8,2176]{2,1,0:T(8,128)(2,1)S(1)}, u32[]{:S(2)}, u32[]{:S(2)}) async-start(bf16[4,8,2176]{2,1,0:T(8,128)(2,1)} %broadcast_in_dim.54), calls=%async_computation.4 | async-start | bytes 278528 | tf_op jit(solution)/shard_map/all_to_all | solution.py:32
  200.4 25.2 %all-to-all-start.5 = ((f32[4,16,128]{2,1,0:T(8,128)}), f32[4,16,128]{2,1,0:T(8,128)S(1)}, u32[]{:S(2)}, u32[]{:S(2)}) async-start(f32[4,16,128]{2,1,0:T(8,128)} %broadcast_in_dim.56), calls=%async_computation.5 | async-start | bytes 65536 | tf_op jit(solution)/shard_map/all_to_all | solution.py:32
  205.0 13.1 %collective-permute-start.10 = (bf16[512,512]{1,0:T(8,128)(2,1)S(1)}, bf16[512,512]{1,0:T(8,128)(2,1)S(1)}, u32[]{:S(2)}, u32[]{:S(2)}) collective-permute-start(bf16[512,512]{1,0:T(8,128)(2,1)S(1)} %get-tuple-element.40), channel_id=1, source_target_pairs={{0,3},{1,0},{2,1},{3,2},{4,7},{5,4},{6,5},{7,6},{8,11},{9,8},{10,9... | collective-permute-start | bytes 1572872 | tf_op jit(solution)/shard_map/ppermute | solution.py:24
  208.2 16.1 %collective-permute-start.14 = (bf16[512,512]{1,0:T(8,128)(2,1)S(1)}, bf16[512,512]{1,0:T(8,128)(2,1)S(1)}, u32[]{:S(2)}, u32[]{:S(2)}) collective-permute-start(bf16[512,512]{1,0:T(8,128)(2,1)S(1)} %get-tuple-element.41), channel_id=1, source_target_pairs={{0,1},{1,2},{2,3},{3,0},{4,5},{5,6},{6,7},{7,4},{8,9},{9,10},{10,1... | collective-permute-start | bytes 1572872 | tf_op jit(solution)/shard_map/ppermute | solution.py:24
  209.1 26.5 %collective-permute-start.12 = (bf16[512,512]{1,0:T(8,128)(2,1)}, bf16[512,512]{1,0:T(8,128)(2,1)}, u32[]{:S(2)}, u32[]{:S(2)}) collective-permute-start(bf16[512,512]{1,0:T(8,128)(2,1)} %get-tuple-element.38), channel_id=1, source_target_pairs={{0,1},{1,2},{2,3},{3,0},{4,5},{5,6},{6,7},{7,4},{8,9},{9,10},{10,1... | collective-permute-start | bytes 1572872 | tf_op jit(solution)/shard_map/ppermute | solution.py:24
  225.4 14.1 %collective-permute-start.11 = (bf16[512,512]{1,0:T(8,128)(2,1)}, bf16[512,512]{1,0:T(8,128)(2,1)}, u32[]{:S(2)}, u32[]{:S(2)}) collective-permute-start(bf16[512,512]{1,0:T(8,128)(2,1)} %get-tuple-element.36), channel_id=1, source_target_pairs={{0,3},{1,0},{2,1},{3,2},{4,7},{5,4},{6,5},{7,6},{8,11},{9,8},{10,9... | collective-permute-start | bytes 1572872 | tf_op jit(solution)/shard_map/ppermute | solution.py:24
  225.4 19.7 %collective-permute-start.13 = (bf16[512,512]{1,0:T(8,128)(2,1)S(1)}, bf16[512,512]{1,0:T(8,128)(2,1)}, u32[]{:S(2)}, u32[]{:S(2)}) collective-permute-start(bf16[512,512]{1,0:T(8,128)(2,1)S(1)} %get-tuple-element.39), channel_id=1, source_target_pairs={{0,3},{1,0},{2,1},{3,2},{4,7},{5,4},{6,5},{7,6},{8,11},{9,8},{10,9... | collective-permute-start | bytes 1572872 | tf_op jit(solution)/shard_map/ppermute | solution.py:24
  225.7 19.5 %collective-permute-start.15 = (bf16[512,512]{1,0:T(8,128)(2,1)S(1)}, bf16[512,512]{1,0:T(8,128)(2,1)}, u32[]{:S(2)}, u32[]{:S(2)}) collective-permute-start(bf16[512,512]{1,0:T(8,128)(2,1)S(1)} %get-tuple-element.37), channel_id=1, source_target_pairs={{0,1},{1,2},{2,3},{3,0},{4,5},{5,6},{6,7},{7,4},{8,9},{9,10},{10,1... | collective-permute-start | bytes 1572872 | tf_op jit(solution)/shard_map/ppermute | solution.py:24
  (28 other events, 196.2 us)

commit v2 on v1

v2 whole, which is shorter than its diff:
```python
import functools

import jax
import jax.numpy as jnp
from jax import lax
from jax.experimental import pallas as pl
from jax.experimental.pallas import tpu as pltpu
from jax.sharding import Mesh, PartitionSpec as P

L = 128
pad_token = 128001
score_scale = 20.0
loss_seed = 4096.0
norm_epsilon = 1e-05
unit_epsilon = 1e-06
MP = 4
FT = 256
CHUNKS = (512, 512)
bf16 = jnp.bfloat16
f32 = jnp.float32


def shifted(x, by):
    return lax.ppermute(x, "mp", [(i, (i + by) % MP) for i in range(MP)])


def swapped(x):
    return lax.ppermute(x, "core", [(0, 1), (1, 0)])


def copies_to_all(x, axes, count):
    return lax.all_to_all(
        jnp.broadcast_to(x, (count, *x.shape)), axes, split_axis=0, concat_axis=0, tiled=True
    )


def in_hbm(x):
    return pltpu.with_memory_space_constraint(x, pltpu.HBM)


def encode_kernel(
    chunk, count, m_ref, own_ref, right_ref, left_ref, high_ref, low_ref, mask_ref, gain_ref, wg_ref, wu_ref, *refs
):
    a_out, b_out, c_out, pool_ref, rms_ref, xpool_ref = refs[count : count + 6]
    xin, xs, w, a_buf, b_buf, c_buf, in_sem, w_sem, out_sem = refs[count + 6 :]
    rows, part = own_ref.shape
    half = rows // 2
    tiles = w.shape[0]
    m = m_ref[0]
    sources = [
        (own_ref, xin.at[0]),
        (right_ref, xin.at[1]),
        (left_ref, xin.at[3]),
        (high_ref, xin.at[2, pl.ds(0, half)]),
        (low_ref, xin.at[2, pl.ds(half, half)]),
    ]
    arriving = [pltpu.make_async_copy(a, b, in_sem.at[k]) for k, (a, b) in enumerate(sources)]
    for copy in arriving:
        copy.start()
    weights = []
    for n in range(tiles):
        columns = pl.ds(n * FT, FT)
        for k in range(MP):
            at = pl.multiple_of(lax.rem(m + k, MP) * part, part)
            for i, ref in enumerate((wg_ref, wu_ref)):
                weights.append(
                    pltpu.make_async_copy(
                        ref.at[pl.ds(at, part), columns],
                        w.at[n, pl.ds(k * part, part), pl.ds(i * FT, FT)],
                        w_sem.at[n, 2 * k + i],
                    )
                )
    for copy in weights:
        copy.start()
    for copy in arriving:
        copy.wait()

    total = None
    for k in range(MP):
        v = xin[k].astype(f32)
        square = jnp.sum(v * v, axis=1, keepdims=True)
        total = square if total is None else total + square
    rms = lax.rsqrt(total / (MP * part) + norm_epsilon)
    rms_ref[...] = rms
    mask = mask_ref[...]
    for k in range(MP):
        j = lax.rem(m + k, MP)
        v = xin[k].astype(f32)
        xs[:, k * part : (k + 1) * part] = (v * rms * gain_ref[j]).astype(bf16)
        live = v * mask
        for p in range(rows // L):
            xpool_ref[j, p : p + 1] = jnp.sum(live[p * L : (p + 1) * L], axis=0, keepdims=True)

    def product(n):
        for copy in weights[n * 2 * MP : (n + 1) * 2 * MP]:
            copy.wait()
        return jnp.dot(xs[...], w[n], preferred_element_type=f32)

    leaving = []
    both = product(0)
    for n in range(tiles):
        gate, up = both[:, :FT], both[:, FT:]
        if n + 1 < tiles:
            both = product(n + 1)
        columns = slice(n * FT, (n + 1) * FT)
        sig = jax.nn.sigmoid(gate)
        b = gate * sig
        bu = b * up
        act = bu.astype(bf16).astype(f32) * mask
        for p in range(rows // L):
            pool_ref[p : p + 1, columns] = jnp.sum(act[p * L : (p + 1) * L], axis=0, keepdims=True)
        a = up * (sig + b * (1.0 - sig))
        a_buf[:, columns] = a.astype(bf16)
        b_buf[:, columns] = b.astype(bf16)
        c_buf[:, columns] = (a * gate + bu).astype(bf16)
        for i, (buf, out) in enumerate(((a_buf, a_out), (b_buf, b_out), (c_buf, c_out))):
            copy = pltpu.make_async_copy(
                buf.at[:, pl.ds(n * FT, FT)],
                out.at[pl.ds(chunk * rows, rows), pl.ds(n * FT, FT)],
                out_sem.at[n, i],
            )
            copy.start()
            leaving.append(copy)
    for copy in leaving:
        copy.wait()


def encode(m, chunk, total, before, own, right, left, high, low, mask, gain, w_gate, w_up):
    rows, part = own.shape
    width, ff = w_gate.shape
    passes = rows // L
    tiles = ff // FT
    anywhere = pl.BlockSpec(memory_space=pl.ANY)
    vmem = pl.BlockSpec(memory_space=pltpu.VMEM)
    return pl.pallas_call(
        functools.partial(encode_kernel, chunk, len(before)),
        in_specs=[pl.BlockSpec(memory_space=pltpu.SMEM)]
        + [anywhere] * 5
        + [vmem, vmem, anywhere, anywhere]
        + [anywhere] * len(before),
        out_specs=[anywhere] * 3 + [vmem] * 3,
        out_shape=[pltpu.HBM((total, ff), bf16)] * 3
        + [
            jax.ShapeDtypeStruct((passes, ff), f32),
            jax.ShapeDtypeStruct((rows, 1), f32),
            jax.ShapeDtypeStruct((MP, passes, part), f32),
        ],
        scratch_shapes=[
            pltpu.VMEM((MP, rows, part), bf16),
            pltpu.VMEM((rows, width), bf16),
            pltpu.VMEM((tiles, width, 2 * FT), bf16),
        ]
        + [pltpu.VMEM((rows, ff), bf16)] * 3
        + [
            pltpu.SemaphoreType.DMA((5,)),
            pltpu.SemaphoreType.DMA((tiles, 2 * MP)),
            pltpu.SemaphoreType.DMA((tiles, 3)),
        ],
        compiler_params=pltpu.CompilerParams(vmem_limit_bytes=44 << 20),
        cost_estimate=pl.CostEstimate(
            flops=4 * rows * width * ff,
            transcendentals=rows * ff,
            bytes_accessed=4 * width * ff + 2 * rows * width + 6 * rows * ff,
        ),
        input_output_aliases={10 + k: k for k in range(len(before))},
        name="encode",
    )(
        m, *map(in_hbm, (own, right, left, high, low)), mask, gain,
        in_hbm(w_gate), in_hbm(w_up), *map(in_hbm, before),
    )


def contract_rows(left, right):
    return lax.dot_general(
        left, right, (((1,), (1,)), ((), ())), preferred_element_type=f32
    )


def load_weights(m, steps, wg_ref, wu_ref, w, sem):
    part, ff = w.shape[1], wg_ref.shape[1]
    copies = []
    for k, step in enumerate(steps):
        at = pl.multiple_of(lax.rem(m + step, MP) * part, part)
        for i, ref in enumerate((wg_ref, wu_ref)):
            copies.append(
                pltpu.make_async_copy(
                    ref.at[pl.ds(at, part)], w.at[k, :, pl.ds(i * ff, ff)], sem.at[k, i]
                )
            )
    return copies


def back_far_kernel(m_ref, a_ref, b_ref, c_ref, g_ref, mask_ref, wg_ref, wu_ref, *refs):
    high_ref, low_ref, s_ref, d_out = refs[:4]
    abc, d, w, in_sem, w_sem, out_sem = refs[4:]
    ff = a_ref.shape[1]
    tiles, _, rt, _ = abc.shape
    weights = load_weights(m_ref[0], (2,), wg_ref, wu_ref, w, w_sem)
    arriving = [
        [
            pltpu.make_async_copy(ref.at[pl.ds(r * rt, rt)], abc.at[r, i], in_sem.at[r, i])
            for i, ref in enumerate((a_ref, b_ref, c_ref))
        ]
        for r in range(tiles)
    ]
    for copy in arriving[0] + weights + sum(arriving[1:], []):
        copy.start()

    def scaled(r):
        for copy in arriving[r]:
            copy.wait()
        for p in range(rt // L):
            part = slice(p * L, (p + 1) * L)
            at = r * rt + p * L
            dact = g_ref[at // L : at // L + 1] * mask_ref[at : at + L]
            d[r, part, :ff] = (dact * abc[r, 0, part].astype(f32)).astype(bf16)
            d[r, part, ff:] = (dact * abc[r, 1, part].astype(f32)).astype(bf16)
            s_ref[at : at + L] = jnp.sum(dact * abc[r, 2, part].astype(f32), axis=1, keepdims=True)
        copy = pltpu.make_async_copy(d.at[r], d_out.at[pl.ds(r * rt, rt)], out_sem.at[r])
        copy.start()
        return copy

    leaving = [scaled(0)]
    for copy in weights:
        copy.wait()
    for r in range(tiles):
        out = contract_rows(d[r], w[0]).astype(bf16)
        if r + 1 < tiles:
            leaving.append(scaled(r + 1))
        half = tiles // 2
        target, at = (high_ref, r) if r < half else (low_ref, r - half)
        target[at * rt : (at + 1) * rt] = out
    for copy in leaving:
        copy.wait()


def back_far(m, a, b, c, g, mask, w_gate, w_up):
    rows, ff = a.shape
    part = w_gate.shape[0] // MP
    rt = 256
    tiles = rows // rt
    anywhere = pl.BlockSpec(memory_space=pl.ANY)
    vmem = pl.BlockSpec(memory_space=pltpu.VMEM)
    return pl.pallas_call(
        back_far_kernel,
        in_specs=[pl.BlockSpec(memory_space=pltpu.SMEM)]
        + [anywhere] * 3
        + [vmem, vmem, anywhere, anywhere],
        out_specs=[vmem, vmem, vmem, anywhere],
        out_shape=[
            jax.ShapeDtypeStruct((rows // 2, part), bf16),
            jax.ShapeDtypeStruct((rows // 2, part), bf16),
            jax.ShapeDtypeStruct((rows, 1), f32),
            pltpu.HBM((rows, 2 * ff), bf16),
        ],
        scratch_shapes=[
            pltpu.VMEM((tiles, 3, rt, ff), bf16),
            pltpu.VMEM((tiles, rt, 2 * ff), bf16),
            pltpu.VMEM((1, part, 2 * ff), bf16),
            pltpu.SemaphoreType.DMA((tiles, 3)),
            pltpu.SemaphoreType.DMA((1, 2)),
            pltpu.SemaphoreType.DMA((tiles,)),
        ],
        compiler_params=pltpu.CompilerParams(vmem_limit_bytes=44 << 20),
        cost_estimate=pl.CostEstimate(flops=1, transcendentals=0, bytes_accessed=1),
        name="back_far",
    )(m, *map(in_hbm, (a, b, c)), g, mask, in_hbm(w_gate), in_hbm(w_up))


def back_near_kernel(m_ref, d_ref, wg_ref, wu_ref, *refs):
    outs = refs[:6]
    d, w, in_sem, w_sem = refs[6:]
    tiles, rt, _ = d.shape
    weights = load_weights(m_ref[0], (1, 3, 0), wg_ref, wu_ref, w, w_sem)
    arriving = [
        pltpu.make_async_copy(d_ref.at[pl.ds(r * rt, rt)], d.at[r], in_sem.at[r])
        for r in range(tiles)
    ]
    for copy in weights[:2] + arriving + weights[2:]:
        copy.start()
    for k in range(3):
        for copy in weights[2 * k : 2 * k + 2]:
            copy.wait()
        for r in range(tiles):
            if k == 0:
                arriving[r].wait()
            outs[2 * k + r][...] = contract_rows(d[r], w[k]).astype(bf16)


def back_near(m, d, w_gate, w_up):
    rows, ff2 = d.shape
    part = w_gate.shape[0] // MP
    tiles = 2
    rt = rows // tiles
    anywhere = pl.BlockSpec(memory_space=pl.ANY)
    return pl.pallas_call(
        back_near_kernel,
        in_specs=[pl.BlockSpec(memory_space=pltpu.SMEM)] + [anywhere] * 3,
        out_specs=[pl.BlockSpec(memory_space=pltpu.VMEM)] * 6,
        out_shape=[jax.ShapeDtypeStruct((rt, part), bf16)] * 6,
        scratch_shapes=[
            pltpu.VMEM((tiles, rt, ff2), bf16),
            pltpu.VMEM((3, part, ff2), bf16),
            pltpu.SemaphoreType.DMA((tiles,)),
            pltpu.SemaphoreType.DMA((3, 2)),
        ],
        compiler_params=pltpu.CompilerParams(vmem_limit_bytes=44 << 20),
        cost_estimate=pl.CostEstimate(flops=1, transcendentals=0, bytes_accessed=1),
        name="back_near",
    )(m, in_hbm(d), in_hbm(w_gate), in_hbm(w_up))


def finish_kernel(
    count, x_ref, own_ref, one_ref, two_ref, rms_ref, inner_ref, mask_ref, token_ref, gain_ref, *refs
):
    out_ref = refs[count]
    rms = rms_ref[...]
    normed = own_ref[...].astype(f32) + one_ref[...].astype(f32) + two_ref[...].astype(f32)
    grad = rms * gain_ref[...] * normed - x_ref[...].astype(f32) * (rms * rms * inner_ref[...])
    mask = mask_ref[...]
    for p in range(out_ref.shape[0] // L):
        part = slice(p * L, (p + 1) * L)
        out_ref[part] = (grad[part] + mask[part] * token_ref[0, p : p + 1]).astype(bf16)


def finish(chunk, before, x, own, one, two, rms, inner, mask, token, gain):
    rows, part = own.shape
    rt = 256
    steps = rows // rt
    here = pl.BlockSpec((rt, part), lambda r: (r, 0))
    whole = pl.BlockSpec((rt, part), lambda r: (chunk * steps + r, 0))
    column = pl.BlockSpec((rt, 1), lambda r: (chunk * steps + r, 0))
    return pl.pallas_call(
        functools.partial(finish_kernel, len(before)),
        grid=(steps,),
        in_specs=[whole, here, here, here, column, column, column]
        + [
            pl.BlockSpec((1, rt // L, part), lambda r: (chunk * steps + r, 0, 0)),
            pl.BlockSpec((1, part), lambda r: (0, 0)),
        ]
        + [pl.BlockSpec(memory_space=pl.ANY)] * len(before),
        out_specs=whole,
        out_shape=jax.ShapeDtypeStruct(x.shape, bf16),
        input_output_aliases={9 + k: k for k in range(len(before))},
        name="finish",
    )(x, own, one, two, rms, inner, mask, token.reshape(-1, rt // L, part), gain, *before)


def per_device(
    hidden_in, token_ids, passage_counts, positive_doc, queries, norm_gain, w_gate, w_up, w_down
):
    row_count, part = hidden_in.shape
    width = norm_gain.shape[0]
    docs = passage_counts.shape[0]
    passes = row_count // L
    most = passes // docs
    query_rows = queries.shape[0]
    share = query_rows // MP
    chips = lax.axis_size(("x", "z"))
    mi = lax.axis_index("mp")
    core = lax.axis_index("core")
    chip = lax.axis_index(("x", "z"))
    m = mi.astype(jnp.int32).reshape(1)

    mine = lax.all_to_all(
        queries.reshape(MP, share, part), "mp", split_axis=0, concat_axis=0, tiled=True
    )
    mine, hidden_in = lax.optimization_barrier((mine, hidden_in))

    chunks = []
    at = 0
    for rows in CHUNKS:
        own = hidden_in[at : at + rows]
        chunks.append((at, rows, own, shifted(own, 1), shifted(own, -1)))
        at += rows

    mine = jnp.moveaxis(mine, 0, 1).reshape(share, width)
    own_positive = lax.dynamic_slice_in_dim(positive_doc, mi * share, share)
    extra = jnp.pad(own_positive.astype(bf16)[:, None], ((0, 0), (0, L - 1)))
    all_q = lax.all_gather(jnp.concatenate([mine, extra], axis=1), ("x", "z"), axis=0)

    live_pass = jnp.arange(passes, dtype=jnp.int32) % most < jnp.repeat(passage_counts, most)
    token_live = (token_ids.reshape(passes, L) != pad_token) & live_pass[:, None]
    live_float = token_live.astype(f32)
    mask = live_float.reshape(row_count, 1)
    divisor = jnp.maximum(jnp.sum(live_float, axis=1), 1.0)[:, None]
    gain = norm_gain.reshape(MP, 1, part)

    done = []
    before = ()
    for k, (at, rows, own, left, right) in enumerate(chunks):
        half = rows // 2
        high, low = shifted(left[:half], 1), shifted(right[half:], -1)
        part_mask = mask[at : at + rows]
        done.append(
            encode(
                m, k, row_count, before, own, right, left, high, low, part_mask, gain, w_gate, w_up
            )
        )
        before = done[-1][:3]
    a, b, c = before
    all_q = all_q.reshape(chips * share, width + L)
    q = all_q[:, :width]
    positive = all_q[:, width].astype(f32)
    q_float = q.astype(f32)
    query_scale = lax.rsqrt(jnp.sum(q_float * q_float, axis=1) + unit_epsilon)
    pool, rms = (jnp.concatenate([d[k] for d in done], axis=0) for k in (3, 4))
    xpool = jnp.concatenate([d[5] for d in done], axis=1)
    xpool = jnp.moveaxis(xpool, 0, 1).reshape(passes, width)

    high = pool.astype(bf16)
    low = (pool - high.astype(f32)).astype(bf16)
    branch = jnp.dot(jnp.concatenate([high, low], 0), w_down, preferred_element_type=f32)
    branch = (branch[:passes] + branch[passes:]).astype(bf16)
    branch = copies_to_all(branch, "mp", MP).astype(f32).sum(axis=0)
    vec = ((xpool + branch) / divisor).astype(bf16)

    flag = jnp.broadcast_to(live_pass.astype(bf16)[:, None], (passes, L))
    packed = jnp.concatenate([vec, flag], axis=1)
    packed = jnp.concatenate([packed, swapped(packed)], axis=0)
    vecs = packed[:, :width]
    live = packed[:, width].astype(f32)[:, None]
    vec_float = vecs.astype(f32)
    vec_scale = lax.rsqrt(jnp.sum(vec_float * vec_float, axis=1, keepdims=True) + unit_epsilon)

    raw = lax.dot_general(vecs, q, (((1,), (1,)), ((), ())), preferred_element_type=f32)
    weights = live * jnp.exp(score_scale * raw * query_scale[None, :] * vec_scale)
    first_doc = (chip * 2 + core) * docs
    other_doc = (chip * 2 + 1 - core) * docs
    k = jnp.arange(2 * passes, dtype=jnp.int32)
    doc = jnp.where(k < passes, first_doc + k // most, other_doc + (k - passes) // most)
    hit = (positive[None, :] == doc.astype(f32)[:, None]).astype(f32)
    mass = jnp.stack([jnp.sum(weights, axis=0), jnp.sum(weights * hit, axis=0)])
    mass = copies_to_all(mass.reshape(8, -1), ("x", "z"), chips).sum(axis=0).reshape(2, -1)
    total, held = mass[0], mass[1]
    loss = jnp.log(total) - jnp.log(held)
    own_loss = lax.dynamic_slice_in_dim(loss, chip * share, share)

    coef = (loss_seed * score_scale) * query_scale[None, :] * (
        weights / total[None, :] - hit * weights / held[None, :]
    )
    grad = jnp.dot(coef.astype(bf16), q, preferred_element_type=f32)
    term = jnp.sum(coef * raw, axis=1, keepdims=True)
    grad = jnp.concatenate([grad, jnp.broadcast_to(term, (2 * passes, L))], axis=1)
    grad = grad[:passes] + swapped(grad[passes:])
    grad = copies_to_all(grad.astype(bf16), "mp", MP).astype(f32).sum(axis=0)
    scale = vec_scale[:passes]
    change = scale * grad[:, :width] - vec_float[:passes] * (scale**3 * grad[:, width : width + 1])
    token_grad = (change / divisor).astype(bf16)
    dact = lax.dot_general(token_grad, w_down, (((1,), (1,)), ((), ())), preferred_element_type=f32)

    high, low, s, d = back_far(m, a, b, c, dact, mask, w_gate, w_up)
    from_right = shifted(high, -1)
    from_left = shifted(low, 1)
    right_high, right_low, left_high, left_low, own_high, own_low = back_near(m, d, w_gate, w_up)
    left_low = shifted(left_low, -1)
    right_low = shifted((right_low.astype(f32) + from_left.astype(f32)).astype(bf16), 1)
    left_high = shifted((left_high.astype(f32) + from_right.astype(f32)).astype(bf16), -1)
    right_high = shifted(right_high, 1)
    small = jnp.concatenate(
        [s.reshape(passes, L), jnp.pad(own_loss[None, :], ((0, 7), (0, L - share)))], axis=0
    )
    left_low, small = lax.optimization_barrier((left_low, small))
    small = copies_to_all(small, "mp", MP)
    inner = small[:, :passes].sum(axis=0).reshape(row_count, 1) / width
    query_loss = small[:, passes, :share].reshape(MP * share)
    own_gain = lax.dynamic_slice_in_dim(norm_gain, mi * part, part)[None, :]
    own_token = lax.dynamic_slice_in_dim(token_grad, mi * part, part, axis=1).astype(f32)
    rest = (rms, inner, mask, own_token, own_gain)
    hidden_grad = finish(1, (), hidden_in, own_low, left_low, right_low, *rest)
    hidden_grad = finish(0, (hidden_grad,), hidden_in, own_high, left_high, right_high, *rest)
    return query_loss, hidden_grad


def solution(mesh):
    shape = (4, 4, 2, MP)
    split = Mesh(mesh.devices.reshape(shape), ("x", "z", "core", "mp"))
    dp = ("x", "z", "core")
    return jax.shard_map(
        per_device,
        mesh=split,
        in_specs=(
            P(dp, "mp"),
            P(dp),
            P(dp),
            P(dp),
            P(dp, "mp"),
            P(),
            P(None, "mp"),
            P(None, "mp"),
            P("mp", None),
        ),
        out_specs=(P(dp), P(dp, "mp")),
        check_vma=False,
    )
```

time: 250 us -> 233 us (0.932)
  the two profiles are of different devices: /device:TPU:0 before, /device:TPU:24 now
where the time goes in v2:
time: 233 us; the launch traced here: 229 us
  Pallas kernels  74.9 us (32%)
  waiting for transfers between devices  57.3 us (25%)
  starting transfers between devices  47.7 us (20%)
  local copies, waits for them, and re-layouts  16.5 us (7%)
  between operations  14.7 us (6%)
  other arithmetic  9.22 us (4%)
  matrix products  8.85 us (4%)
    pallas_call x2, Pallas kernels, encode(): pl.pallas_call(functools.partial(encode_kernel, chunk, len(before)), in_s...  41.9 us
    ppermute x14, waiting for transfers between devices, shifted(): return lax.ppermute(x, 'mp', [(i, (i + by) % MP) for i in range(MP)])  39 us
    all_to_all x4, starting transfers between devices, copies_to_all(): lax.all_to_all(jnp.broadcast_to(x, (count, *x.shape)), axes, split_axis=0...  22.7 us
    ppermute x14, starting transfers between devices, shifted(): return lax.ppermute(x, 'mp', [(i, (i + by) % MP) for i in range(MP)])  20.2 us
    pallas_call x1, Pallas kernels, back_near(): pl.pallas_call(back_near_kernel, in_specs=[pl.BlockSpec(memory_space=pltp...  15.4 us
    all_to_all x4, waiting for transfers between devices, copies_to_all(): lax.all_to_all(jnp.broadcast_to(x, (count, *x.shape)), axes, split_axis=0...  13.6 us
    pallas_call x1, Pallas kernels, back_far(): pl.pallas_call(back_far_kernel, in_specs=[pl.BlockSpec(memory_space=pltpu...  12.2 us
    pallas_call x2, Pallas kernels, finish(): pl.pallas_call(functools.partial(finish_kernel, len(before)), grid=(steps...  5.38 us
  transfers between devices with their start and end apart: 22, of which 13 were waited for; matrix products, arithmetic and copies ran while one was open for 7% of the time, Pallas kernels for 26%

profile of v2, /device:TPU:24, one launch (start us, length us, event | category | flops | bytes accessed | tf_op | source)
XLA Modules:
  0.0 229.1 jit_solution(4318775668220396934)
XLA Ops:
  7.2 4.7 %all-to-all-start = ((bf16[4,32,512]{2,1,0:T(8,128)(2,1)}), bf16[4,32,512]{2,1,0:T(8,128)(2,1)S(1)}, u32[]{:S(2)}, u32[]{:S(2)}) async-start(bf16[4,32,512]{2,1,0:T(8,128)(2,1)} %bitcast.51), calls=%async_computation | async-start | bytes 262144 | tf_op jit(solution)/shard_map/all_to_all | solution.py:365
  20.6 3.3 %collective-permute-start.1 = (bf16[512,512]{1,0:T(8,128)(2,1)S(1)}, bf16[512,512]{1,0:T(8,128)(2,1)S(1)}, u32[]{:S(2)}, u32[]{:S(2)}) collective-permute-start(bf16[512,512]{1,0:T(8,128)(2,1)S(1)} %get-tuple-element.61.own_ref), channel_id=1, source_target_pairs={{0,1},{1,2},{2,3},{3,0},{4,5},{5,6},{6,7},{7,4},{8,9},{9,10},{10,1... | collective-permute-start | bytes 1572872 | tf_op jit(solution)/shard_map/ppermute | solution.py:24
  23.9 8.2 %collective-permute-done.5.left_ref = bf16[512,512]{1,0:T(8,128)(2,1)} collective-permute-done((bf16[512,512]{1,0:T(8,128)(2,1)S(1)}, bf16[512,512]{1,0:T(8,128)(2,1)}, u32[]{:S(2)}, u32[]{:S(2)}) %collective-permute-start.5) | collective-permute-done | bytes 524320 | tf_op jit(solution)/shard_map/ppermute | solution.py:24
  33.1 3.3 %collective-permute-start.6 = (bf16[256,512]{1,0:T(8,128)(2,1)S(1)}, bf16[256,512]{1,0:T(8,128)(2,1)S(1)}, u32[]{:S(2)}, u32[]{:S(2)}) collective-permute-start(bf16[256,512]{1,0:T(8,128)(2,1)S(1)} %slice.112), channel_id=1, source_target_pairs={{0,1},{1,2},{2,3},{3,0},{4,5},{5,6},{6,7},{7,4},{8,9},{9,10},{10,1... | collective-permute-start | bytes 786440 | tf_op jit(solution)/shard_map/ppermute | solution.py:24
  38.2 5.1 %collective-permute-done.1.left_ref = bf16[512,512]{1,0:T(8,128)(2,1)S(1)} collective-permute-done((bf16[512,512]{1,0:T(8,128)(2,1)S(1)}, bf16[512,512]{1,0:T(8,128)(2,1)S(1)}, u32[]{:S(2)}, u32[]{:S(2)}) %collective-permute-start.1) | collective-permute-done | bytes 524320 | tf_op jit(solution)/shard_map/ppermute | solution.py:24
  43.3 3.3 %collective-permute-start.2 = (bf16[256,512]{1,0:T(8,128)(2,1)S(1)}, bf16[256,512]{1,0:T(8,128)(2,1)S(1)}, u32[]{:S(2)}, u32[]{:S(2)}) collective-permute-start(bf16[256,512]{1,0:T(8,128)(2,1)S(1)} %slice.110), channel_id=1, source_target_pairs={{0,1},{1,2},{2,3},{3,0},{4,5},{5,6},{6,7},{7,4},{8,9},{9,10},{10,1... | collective-permute-start | bytes 786440 | tf_op jit(solution)/shard_map/ppermute | solution.py:24
  48.9 3.3 %collective-permute-done.7.low_ref = bf16[256,512]{1,0:T(8,128)(2,1)} collective-permute-done((bf16[256,512]{1,0:T(8,128)(2,1)S(1)}, bf16[256,512]{1,0:T(8,128)(2,1)}, u32[]{:S(2)}, u32[]{:S(2)}) %collective-permute-start.7) | collective-permute-done | bytes 262176 | tf_op jit(solution)/shard_map/ppermute | solution.py:24
  52.2 20.8 %encode.2 = (bf16[1024,1792]{1,0:T(8,128)(2,1)}, bf16[1024,1792]{1,0:T(8,128)(2,1)}, bf16[1024,1792]{1,0:T(8,128)(2,1)}, f32[4,1792]{1,0:T(4,128)S(1)}, f32[512,1]{1,0:T(8,128)S(1)}, /*index=5*/f32[4,4,512]{2,1,0:T(4,128)S(1)}) custom-call(s32[1]{0:T(128)} %bitcast.m_ref, bf16[512,512]{1,0:T(8,128)(2,1)} %copy-done.10, ...), custom_call_target="tpu_custom_call" | custom-call | flops 7516192768 | bytes 22282240 | tf_op jit(solution)/shard_map/encode/pallas_call | solution.py:135
  73.8 21.2 %encode.3 = (bf16[1024,1792]{1,0:T(8,128)(2,1)}, bf16[1024,1792]{1,0:T(8,128)(2,1)}, bf16[1024,1792]{1,0:T(8,128)(2,1)}, f32[4,1792]{1,0:T(4,128)S(1)}, f32[512,1]{1,0:T(8,128)S(1)}, /*index=5*/f32[4,4,512]{2,1,0:T(4,128)S(1)}) custom-call(s32[1]{0:T(128)} %bitcast.m_ref, ...), custom_call_target="tpu_custom_call", output_to_operand_aliasing={{0}: (10, {}), {1}: (11, {}), {2}: (12, {})} | custom-call | flops 7516192768 | bytes 22282240 | tf_op jit(solution)/shard_map/encode/pallas_call | solution.py:135
  96.8 4.5 %all-to-all-start.1 = ((bf16[4,8,2048]{2,1,0:T(8,128)(2,1)}), bf16[4,8,2048]{2,1,0:T(8,128)(2,1)S(1)}, u32[]{:S(2)}, u32[]{:S(2)}) async-start(bf16[4,8,2048]{2,1,0:T(8,128)(2,1)} %broadcast_in_dim.21), calls=%async_computation.1 | async-start | bytes 262144 | tf_op jit(solution)/shard_map/all_to_all | solution.py:32
  101.3 3.9 %all-to-all-done.1 = bf16[4,8,2048]{2,1,0:T(8,128)(2,1)S(1)} async-done(((bf16[4,8,2048]{2,1,0:T(8,128)(2,1)}), bf16[4,8,2048]{2,1,0:T(8,128)(2,1)S(1)}, u32[]{:S(2)}, u32[]{:S(2)}) %all-to-all-start.1) | async-done | bytes 131104 | tf_op jit(solution)/shard_map/all_to_all | solution.py:32
  113.1 8.0 %all-to-all-start.2 = ((f32[16,8,128]{2,1,0:T(8,128)}), f32[16,8,128]{2,1,0:T(8,128)S(1)}, u32[]{:S(2)}, u32[]{:S(2)}) async-start(f32[16,8,128]{2,1,0:T(8,128)} %broadcast_in_dim.48), calls=%async_computation.2 | async-start | bytes 131072 | tf_op jit(solution)/shard_map/all_to_all | solution.py:32
  122.9 5.8 %all-to-all-done.2 = f32[16,8,128]{2,1,0:T(8,128)S(1)} async-done(((f32[16,8,128]{2,1,0:T(8,128)}), f32[16,8,128]{2,1,0:T(8,128)S(1)}, u32[]{:S(2)}, u32[]{:S(2)}) %all-to-all-start.2) | async-done | bytes 65568 | tf_op jit(solution)/shard_map/all_to_all | solution.py:32
  131.5 5.8 %all-to-all-start.3 = ((bf16[4,8,2176]{2,1,0:T(8,128)(2,1)}), bf16[4,8,2176]{2,1,0:T(8,128)(2,1)S(1)}, u32[]{:S(2)}, u32[]{:S(2)}) async-start(bf16[4,8,2176]{2,1,0:T(8,128)(2,1)} %broadcast_in_dim.50), calls=%async_computation.3 | async-start | bytes 278528 | tf_op jit(solution)/shard_map/all_to_all | solution.py:32
  137.4 3.8 %all-to-all-done.3 = bf16[4,8,2176]{2,1,0:T(8,128)(2,1)S(1)} async-done(((bf16[4,8,2176]{2,1,0:T(8,128)(2,1)}), bf16[4,8,2176]{2,1,0:T(8,128)(2,1)S(1)}, u32[]{:S(2)}, u32[]{:S(2)}) %all-to-all-start.3) | async-done | bytes 139296 | tf_op jit(solution)/shard_map/all_to_all | solution.py:32
  141.5 5.1 %fusion.38.g_ref = f32[8,1792]{1,0:T(8,128)S(1)} fusion(bf16[8,2048]{1,0:T(8,128)(2,1)S(1)} %fusion.12, bf16[1792,2048]{1,0:T(8,128)(2,1)} %param.17), kind=kOutput, calls=%fused_computation.94 | convolution fusion | flops 58720256 | bytes 7430144 | tf_op jit(solution)/shard_map/dot_general | solution.py:450
  146.5 12.2 %back_far.1 = (bf16[512,512]{1,0:T(8,128)(2,1)S(1)}, bf16[512,512]{1,0:T(8,128)(2,1)S(1)}, f32[1024,1]{1,0:T(8,128)S(1)}, bf16[1024,3584]{1,0:T(8,128)(2,1)}) custom-call(s32[1]{0:T(128)} %bitcast.m_ref, bf16[1024,1792]{1,0:T(8,128)(2,1)} %get-tuple-element.32.a_ref, bf16[1024,1792]{1,0:T(8,128)(2,1)} %get-tuple-element.33.b_ref, ...), custom_call_target="tpu_custom_call" | custom-call | flops 1 | bytes 1 | tf_op jit(solution)/shard_map/back_far/pallas_call | solution.py:244
  162.1 15.4 %back_near.1 = (bf16[512,512]{1,0:T(8,128)(2,1)S(1)}, bf16[512,512]{1,0:T(8,128)(2,1)S(1)}, bf16[512,512]{1,0:T(8,128)(2,1)S(1)}, bf16[512,512]{1,0:T(8,128)(2,1...) custom-call(s32[1]{0:T(128)} %bitcast.m_ref, bf16[1024,3584]{1,0:T(8,128)(2,1)} %get-tuple-element.40.d_ref, ...), custom_call_target="tpu_custom_call" | custom-call | flops 1 | bytes 1 | tf_op jit(solution)/shard_map/back_near/pallas_call | solution.py:296
  179.3 3.1 %collective-permute-start.13 = (bf16[512,512]{1,0:T(8,128)(2,1)S(1)}, bf16[512,512]{1,0:T(8,128)(2,1)}, u32[]{:S(2)}, u32[]{:S(2)}) collective-permute-start(bf16[512,512]{1,0:T(8,128)(2,1)S(1)} %get-tuple-element.47), channel_id=1, source_target_pairs={{0,1},{1,2},{2,3},{3,0},{4,5},{5,6},{6,7},{7,4},{8,9},{9,10},{10,1... | collective-permute-start | bytes 1572872 | tf_op jit(solution)/shard_map/ppermute | solution.py:24
  185.9 9.6 %collective-permute-done.10.one_ref = bf16[512,512]{1,0:T(8,128)(2,1)} collective-permute-done((bf16[512,512]{1,0:T(8,128)(2,1)}, bf16[512,512]{1,0:T(8,128)(2,1)}, u32[]{:S(2)}, u32[]{:S(2)}) %collective-permute-start.10) | collective-permute-done | bytes 524320 | tf_op jit(solution)/shard_map/ppermute | solution.py:24
  196.1 4.5 %all-to-all-start.4 = ((f32[4,16,128]{2,1,0:T(8,128)}), f32[4,16,128]{2,1,0:T(8,128)S(1)}, u32[]{:S(2)}, u32[]{:S(2)}) async-start(f32[4,16,128]{2,1,0:T(8,128)} %broadcast_in_dim.52), calls=%async_computation.4 | async-start | bytes 65536 | tf_op jit(solution)/shard_map/all_to_all | solution.py:32
  200.6 4.1 %collective-permute-done.11 = bf16[512,512]{1,0:T(8,128)(2,1)} collective-permute-done((bf16[512,512]{1,0:T(8,128)(2,1)S(1)}, bf16[512,512]{1,0:T(8,128)(2,1)}, u32[]{:S(2)}, u32[]{:S(2)}) %collective-permute-start.11) | collective-permute-done | bytes 524320 | tf_op jit(solution)/shard_map/ppermute | solution.py:24
  209.1 2.7 %finish.2.refs_0_ = bf16[1024,512]{1,0:T(8,128)(2,1)} custom-call(bf16[1024,512]{1,0:T(8,128)(2,1)} %x_ref.1, bf16[512,512]{1,0:T(8,128)(2,1)} %copy-done.2, bf16[512,512]{1,0:T(8,128)(2,1)} %collective-permute-done.10.one_ref, bf16[512,512]{1,0:T(8,128)(2,1)} %copy-done.8, f32[1024,1]{1,0:T(8,128)} %copy.70.rms_ref, f32[1024,1]{1,0:T(8,128)} %copy.71.inner_ref, ...), custom_call_target="tpu_custom_call" | custom-call | tf_op jit(solution)/shard_map/finish/pallas_call | solution.py:333
  211.8 6.8 %collective-permute-done.12.one_ref = bf16[512,512]{1,0:T(8,128)(2,1)S(1)} collective-permute-done((bf16[512,512]{1,0:T(8,128)(2,1)S(1)}, bf16[512,512]{1,0:T(8,128)(2,1)S(1)}, u32[]{:S(2)}, u32[]{:S(2)}) %collective-permute-start.12) | collective-permute-done | bytes 524320 | tf_op jit(solution)/shard_map/ppermute | solution.py:24
  (142 shorter events, 46.0 us)
Async XLA Ops:
  7.2 8.6 %all-to-all-start = ((bf16[4,32,512]{2,1,0:T(8,128)(2,1)}), bf16[4,32,512]{2,1,0:T(8,128)(2,1)S(1)}, u32[]{:S(2)}, u32[]{:S(2)}) async-start(bf16[4,32,512]{2,1,0:T(8,128)(2,1)} %bitcast.51), calls=%async_computation | async-start | bytes 262144 | tf_op jit(solution)/shard_map/all_to_all | solution.py:365
  11.9 95.0 %all-gather.3.cloned.1.call-start = ((), (), s32[]{:S(2)}) async-start(), calls=%async_computation.5 | async-start | bytes 2367488 | tf_op jit(solution)/shard_map/all_gather | solution.py:380
  17.1 55.9 %copy-start.5 = (bf16[512,512]{1,0:T(8,128)(2,1)}, bf16[512,512]{1,0:T(8,128)(2,1)S(1)}, u32[]{:S(2)}) copy-start(bf16[512,512]{1,0:T(8,128)(2,1)S(1)} %get-tuple-element.61.own_ref) | copy-start | bytes 1572868
  17.1 15.0 %collective-permute-start.5 = (bf16[512,512]{1,0:T(8,128)(2,1)S(1)}, bf16[512,512]{1,0:T(8,128)(2,1)}, u32[]{:S(2)}, u32[]{:S(2)}) collective-permute-start(bf16[512,512]{1,0:T(8,128)(2,1)S(1)} %get-tuple-element.60.own_ref), channel_id=1, source_target_pairs={{0,1},{1,2},{2,3},{3,0},{4,5},{5,6},{6,7},{7,4},{8,9},{9,10},{10,1... | collective-permute-start | bytes 1572872 | tf_op jit(solution)/shard_map/ppermute | solution.py:24
  19.2 17.2 %collective-permute-start.4 = (bf16[512,512]{1,0:T(8,128)(2,1)S(1)}, bf16[512,512]{1,0:T(8,128)(2,1)}, u32[]{:S(2)}, u32[]{:S(2)}) collective-permute-start(bf16[512,512]{1,0:T(8,128)(2,1)S(1)} %get-tuple-element.60.own_ref), channel_id=1, source_target_pairs={{0,3},{1,0},{2,1},{3,2},{4,7},{5,4},{6,5},{7,6},{8,11},{9,8},{10,9... | collective-permute-start | bytes 1572872 | tf_op jit(solution)/shard_map/ppermute | solution.py:24
  20.6 22.7 %collective-permute-start.1 = (bf16[512,512]{1,0:T(8,128)(2,1)S(1)}, bf16[512,512]{1,0:T(8,128)(2,1)S(1)}, u32[]{:S(2)}, u32[]{:S(2)}) collective-permute-start(bf16[512,512]{1,0:T(8,128)(2,1)S(1)} %get-tuple-element.61.own_ref), channel_id=1, source_target_pairs={{0,1},{1,2},{2,3},{3,0},{4,5},{5,6},{6,7},{7,4},{8,9},{9,10},{10,1... | collective-permute-start | bytes 1572872 | tf_op jit(solution)/shard_map/ppermute | solution.py:24
  23.9 22.8 %collective-permute-start = (bf16[512,512]{1,0:T(8,128)(2,1)S(1)}, bf16[512,512]{1,0:T(8,128)(2,1)S(1)}, u32[]{:S(2)}, u32[]{:S(2)}) collective-permute-start(bf16[512,512]{1,0:T(8,128)(2,1)S(1)} %get-tuple-element.61.own_ref), channel_id=1, source_target_pairs={{0,3},{1,0},{2,1},{3,2},{4,7},{5,4},{6,5},{7,6},{8,11},{9,8},{10,9... | collective-permute-start | bytes 1572872 | tf_op jit(solution)/shard_map/ppermute | solution.py:24
  23.9 81.4 %copy-start.14 = (f32[8]{0:T(128)}, f32[8]{0:T(128)S(1)}, u32[]{:S(2)}) copy-start(f32[8]{0:T(128)S(1)} %broadcast_maximum_fusion) | copy-start | bytes 100
  33.1 15.8 %collective-permute-start.6 = (bf16[256,512]{1,0:T(8,128)(2,1)S(1)}, bf16[256,512]{1,0:T(8,128)(2,1)S(1)}, u32[]{:S(2)}, u32[]{:S(2)}) collective-permute-start(bf16[256,512]{1,0:T(8,128)(2,1)S(1)} %slice.112), channel_id=1, source_target_pairs={{0,1},{1,2},{2,3},{3,0},{4,5},{5,6},{6,7},{7,4},{8,9},{9,10},{10,1... | collective-permute-start | bytes 786440 | tf_op jit(solution)/shard_map/ppermute | solution.py:24
  37.4 14.7 %collective-permute-start.7 = (bf16[256,512]{1,0:T(8,128)(2,1)S(1)}, bf16[256,512]{1,0:T(8,128)(2,1)}, u32[]{:S(2)}, u32[]{:S(2)}) collective-permute-start(bf16[256,512]{1,0:T(8,128)(2,1)S(1)} %slice.113), channel_id=1, source_target_pairs={{0,3},{1,0},{2,1},{3,2},{4,7},{5,4},{6,5},{7,6},{8,11},{9,8},{10,9... | collective-permute-start | bytes 786440 | tf_op jit(solution)/shard_map/ppermute | solution.py:24
  43.3 29.7 %collective-permute-start.2 = (bf16[256,512]{1,0:T(8,128)(2,1)S(1)}, bf16[256,512]{1,0:T(8,128)(2,1)S(1)}, u32[]{:S(2)}, u32[]{:S(2)}) collective-permute-start(bf16[256,512]{1,0:T(8,128)(2,1)S(1)} %slice.110), channel_id=1, source_target_pairs={{0,1},{1,2},{2,3},{3,0},{4,5},{5,6},{6,7},{7,4},{8,9},{9,10},{10,1... | collective-permute-start | bytes 786440 | tf_op jit(solution)/shard_map/ppermute | solution.py:24
  46.6 26.4 %collective-permute-start.3 = (bf16[256,512]{1,0:T(8,128)(2,1)S(1)}, bf16[256,512]{1,0:T(8,128)(2,1)S(1)}, u32[]{:S(2)}, u32[]{:S(2)}) collective-permute-start(bf16[256,512]{1,0:T(8,128)(2,1)S(1)} %slice.111), channel_id=1, source_target_pairs={{0,3},{1,0},{2,1},{3,2},{4,7},{5,4},{6,5},{7,6},{8,11},{9,8},{10,9... | collective-permute-start | bytes 786440 | tf_op jit(solution)/shard_map/ppermute | solution.py:24
  96.8 8.4 %all-to-all-start.1 = ((bf16[4,8,2048]{2,1,0:T(8,128)(2,1)}), bf16[4,8,2048]{2,1,0:T(8,128)(2,1)S(1)}, u32[]{:S(2)}, u32[]{:S(2)}) async-start(bf16[4,8,2048]{2,1,0:T(8,128)(2,1)} %broadcast_in_dim.21), calls=%async_computation.1 | async-start | bytes 262144 | tf_op jit(solution)/shard_map/all_to_all | solution.py:32
  105.4 1.2 collective-permute-start.8
  113.1 15.6 %all-to-all-start.2 = ((f32[16,8,128]{2,1,0:T(8,128)}), f32[16,8,128]{2,1,0:T(8,128)S(1)}, u32[]{:S(2)}, u32[]{:S(2)}) async-start(f32[16,8,128]{2,1,0:T(8,128)} %broadcast_in_dim.48), calls=%async_computation.2 | async-start | bytes 131072 | tf_op jit(solution)/shard_map/all_to_all | solution.py:32
  129.5 1.3 collective-permute-start.9
  131.5 9.7 %all-to-all-start.3 = ((bf16[4,8,2176]{2,1,0:T(8,128)(2,1)}), bf16[4,8,2176]{2,1,0:T(8,128)(2,1)S(1)}, u32[]{:S(2)}, u32[]{:S(2)}) async-start(bf16[4,8,2176]{2,1,0:T(8,128)(2,1)} %broadcast_in_dim.50), calls=%async_computation.3 | async-start | bytes 278528 | tf_op jit(solution)/shard_map/all_to_all | solution.py:32
  158.7 23.9 %collective-permute-start.14 = (bf16[512,512]{1,0:T(8,128)(2,1)S(1)}, bf16[512,512]{1,0:T(8,128)(2,1)}, u32[]{:S(2)}, u32[]{:S(2)}) collective-permute-start(bf16[512,512]{1,0:T(8,128)(2,1)S(1)} %get-tuple-element.53), channel_id=1, source_target_pairs={{0,1},{1,2},{2,3},{3,0},{4,5},{5,6},{6,7},{7,4},{8,9},{9,10},{10,1... | collective-permute-start | bytes 1572872 | tf_op jit(solution)/shard_map/ppermute | solution.py:24
  179.1 16.4 %collective-permute-start.10 = (bf16[512,512]{1,0:T(8,128)(2,1)}, bf16[512,512]{1,0:T(8,128)(2,1)}, u32[]{:S(2)}, u32[]{:S(2)}) collective-permute-start(bf16[512,512]{1,0:T(8,128)(2,1)} %get-tuple-element.41), channel_id=1, source_target_pairs={{0,3},{1,0},{2,1},{3,2},{4,7},{5,4},{6,5},{7,6},{8,11},{9,8},{10,9... | collective-permute-start | bytes 1572872 | tf_op jit(solution)/shard_map/ppermute | solution.py:24
  179.1 25.6 %collective-permute-start.11 = (bf16[512,512]{1,0:T(8,128)(2,1)S(1)}, bf16[512,512]{1,0:T(8,128)(2,1)}, u32[]{:S(2)}, u32[]{:S(2)}) collective-permute-start(bf16[512,512]{1,0:T(8,128)(2,1)S(1)} %get-tuple-element.46), channel_id=1, source_target_pairs={{0,3},{1,0},{2,1},{3,2},{4,7},{5,4},{6,5},{7,6},{8,11},{9,8},{10,9... | collective-permute-start | bytes 1572872 | tf_op jit(solution)/shard_map/ppermute | solution.py:24
  179.3 32.5 %collective-permute-start.13 = (bf16[512,512]{1,0:T(8,128)(2,1)S(1)}, bf16[512,512]{1,0:T(8,128)(2,1)}, u32[]{:S(2)}, u32[]{:S(2)}) collective-permute-start(bf16[512,512]{1,0:T(8,128)(2,1)S(1)} %get-tuple-element.47), channel_id=1, source_target_pairs={{0,1},{1,2},{2,3},{3,0},{4,5},{5,6},{6,7},{7,4},{8,9},{9,10},{10,1... | collective-permute-start | bytes 1572872 | tf_op jit(solution)/shard_map/ppermute | solution.py:24
  183.9 24.4 %collective-permute-start.15 = (bf16[512,512]{1,0:T(8,128)(2,1)S(1)}, bf16[512,512]{1,0:T(8,128)(2,1)S(1)}, u32[]{:S(2)}, u32[]{:S(2)}) collective-permute-start(bf16[512,512]{1,0:T(8,128)(2,1)S(1)} %add_convert_fusion), channel_id=1, source_target_pairs={{0,1},{1,2},{2,3},{3,0},{4,5},{5,6},{6,7},{7,4},{8,9},{9,10},{10,1... | collective-permute-start | bytes 1572872 | tf_op jit(solution)/shard_map/ppermute | solution.py:24
  196.1 10.5 %all-to-all-start.4 = ((f32[4,16,128]{2,1,0:T(8,128)}), f32[4,16,128]{2,1,0:T(8,128)S(1)}, u32[]{:S(2)}, u32[]{:S(2)}) async-start(f32[4,16,128]{2,1,0:T(8,128)} %broadcast_in_dim.52), calls=%async_computation.4 | async-start | bytes 65536 | tf_op jit(solution)/shard_map/all_to_all | solution.py:32
  205.8 12.7 %collective-permute-start.12 = (bf16[512,512]{1,0:T(8,128)(2,1)S(1)}, bf16[512,512]{1,0:T(8,128)(2,1)S(1)}, u32[]{:S(2)}, u32[]{:S(2)}) collective-permute-start(bf16[512,512]{1,0:T(8,128)(2,1)S(1)} %add_convert_fusion.1), channel_id=1, source_target_pairs={{0,3},{1,0},{2,1},{3,2},{4,7},{5,4},{6,5},{7,6},{8,11},{9,8},{10,9... | collective-permute-start | bytes 1572872 | tf_op jit(solution)/shard_map/ppermute | solution.py:24
  (17 other events, 301.2 us)
Sparse Core Ops, SparseCore 0:
  38.3 47.9 all-gather.2

commit v3 on v2

v3 whole, which is shorter than its diff:
```python
import functools

import jax
import jax.numpy as jnp
from jax import lax
from jax.experimental import pallas as pl
from jax.experimental.pallas import tpu as pltpu
from jax.sharding import Mesh, PartitionSpec as P

L = 128
pad_token = 128001
score_scale = 20.0
loss_seed = 4096.0
norm_epsilon = 1e-05
unit_epsilon = 1e-06
MP = 4
FT = 256
ROW_STEP = 512
CHUNKS = (512, 512)
bf16 = jnp.bfloat16
f32 = jnp.float32


def shifted(x, by):
    return lax.ppermute(x, "mp", [(i, (i + by) % MP) for i in range(MP)])


def swapped(x):
    return lax.ppermute(x, "core", [(0, 1), (1, 0)])


def copies_to_all(x, axes, count):
    return lax.all_to_all(
        jnp.broadcast_to(x, (count, *x.shape)), axes, split_axis=0, concat_axis=0, tiled=True
    )


def in_hbm(x):
    return pltpu.with_memory_space_constraint(x, pltpu.HBM)


def encode_kernel(
    chunk, count, m_ref, own_ref, right_ref, left_ref, high_ref, low_ref, mask_ref, gain_ref, wg_ref, wu_ref, *refs
):
    a_out, b_out, c_out, pool_ref, rms_ref, xpool_ref = refs[count : count + 6]
    xin, xs, w, results, in_sem, w_sem, out_sem = refs[count + 6 :]
    rows, part = own_ref.shape
    half = rows // 2
    tiles = w.shape[0]
    m = m_ref[0]
    sources = [
        (own_ref, xin.at[0]),
        (right_ref, xin.at[1]),
        (left_ref, xin.at[3]),
        (high_ref, xin.at[2, pl.ds(0, half)]),
        (low_ref, xin.at[2, pl.ds(half, half)]),
    ]
    arriving = [pltpu.make_async_copy(a, b, in_sem.at[k]) for k, (a, b) in enumerate(sources)]
    for copy in arriving:
        copy.start()
    def weight_copies(n):
        columns = pl.ds(pl.multiple_of(n * FT, FT), FT)
        copies = []
        for k in range(MP):
            at = pl.multiple_of(lax.rem(m + k, MP) * part, part)
            for i, ref in enumerate((wg_ref, wu_ref)):
                copies.append(
                    pltpu.make_async_copy(
                        ref.at[pl.ds(at, part), columns],
                        w.at[n, pl.ds(k * part, part), pl.ds(i * FT, FT)],
                        w_sem.at[n, 2 * k + i],
                    )
                )
        return copies

    def result_copies(n):
        return [
            pltpu.make_async_copy(
                results.at[n, i],
                out.at[pl.ds(chunk * rows, rows), pl.ds(pl.multiple_of(n * FT, FT), FT)],
                out_sem.at[n, i],
            )
            for i, out in enumerate((a_out, b_out, c_out))
        ]

    def each(count, body):
        def step(n, carry):
            body(n)
            return carry

        lax.fori_loop(0, count, step, 0)

    def start_weights(n):
        for copy in weight_copies(n):
            copy.start()

    each(tiles, start_weights)
    for copy in arriving:
        copy.wait()

    def normalise(p):
        at = pl.ds(pl.multiple_of(p * L, L), L)
        mask = mask_ref[at]
        total = None
        for k in range(MP):
            v = xin[k, at].astype(f32)
            square = jnp.sum(v * v, axis=1, keepdims=True)
            total = square if total is None else total + square
        rms = lax.rsqrt(total / (MP * part) + norm_epsilon)
        rms_ref[at] = rms
        for k in range(MP):
            j = lax.rem(m + k, MP)
            v = xin[k, at].astype(f32)
            xs[at, k * part : (k + 1) * part] = (v * rms * gain_ref[j]).astype(bf16)
            xpool_ref[p, pl.ds(j, 1)] = jnp.sum(v * mask, axis=0, keepdims=True)

    each(rows // L, normalise)

    def multiply(n):
        for copy in weight_copies(n):
            copy.wait()
        for r in range(0, rows, ROW_STEP):
            at = slice(r, r + ROW_STEP)
            both = jnp.dot(xs[at], w[n], preferred_element_type=f32)
            gate, up = both[:, :FT], both[:, FT:]
            mask = mask_ref[at]
            sig = jax.nn.sigmoid(gate)
            up = up * mask
            b = gate * sig
            bu = b * up
            act = bu.astype(bf16).astype(f32)
            for p in range(ROW_STEP // L):
                q = r // L + p
                pool_ref[n, q : q + 1] = jnp.sum(act[p * L : (p + 1) * L], axis=0, keepdims=True)
            a = up * (sig + b * (1.0 - sig))
            results[n, 0, at] = a.astype(bf16)
            results[n, 1, at] = (b * mask).astype(bf16)
            results[n, 2, at] = (a * gate + bu).astype(bf16)
        for copy in result_copies(n):
            copy.start()

    each(tiles, multiply)

    def wait_results(n):
        for copy in result_copies(n):
            copy.wait()

    each(tiles, wait_results)


def encode(m, chunk, total, before, own, right, left, high, low, mask, gain, w_gate, w_up):
    rows, part = own.shape
    width, ff = w_gate.shape
    passes = rows // L
    tiles = ff // FT
    anywhere = pl.BlockSpec(memory_space=pl.ANY)
    vmem = pl.BlockSpec(memory_space=pltpu.VMEM)
    return pl.pallas_call(
        functools.partial(encode_kernel, chunk, len(before)),
        in_specs=[pl.BlockSpec(memory_space=pltpu.SMEM)]
        + [anywhere] * 5
        + [vmem, vmem, anywhere, anywhere]
        + [anywhere] * len(before),
        out_specs=[anywhere] * 3 + [vmem] * 3,
        out_shape=[pltpu.HBM((total, ff), bf16)] * 3
        + [
            jax.ShapeDtypeStruct((tiles, passes, FT), f32),
            jax.ShapeDtypeStruct((rows, 1), f32),
            jax.ShapeDtypeStruct((passes, MP, part), f32),
        ],
        scratch_shapes=[
            pltpu.VMEM((MP, rows, part), bf16),
            pltpu.VMEM((rows, width), bf16),
            pltpu.VMEM((tiles, width, 2 * FT), bf16),
            pltpu.VMEM((tiles, 3, rows, FT), bf16),
            pltpu.SemaphoreType.DMA((5,)),
            pltpu.SemaphoreType.DMA((tiles, 2 * MP)),
            pltpu.SemaphoreType.DMA((tiles, 3)),
        ],
        compiler_params=pltpu.CompilerParams(vmem_limit_bytes=44 << 20),
        cost_estimate=pl.CostEstimate(
            flops=4 * rows * width * ff,
            transcendentals=rows * ff,
            bytes_accessed=4 * width * ff + 2 * rows * width + 6 * rows * ff,
        ),
        input_output_aliases={10 + k: k for k in range(len(before))},
        name="encode",
    )(
        m, *map(in_hbm, (own, right, left, high, low)), mask, gain,
        in_hbm(w_gate), in_hbm(w_up), *map(in_hbm, before),
    )


def contract_rows(left, right):
    return lax.dot_general(
        left, right, (((1,), (1,)), ((), ())), preferred_element_type=f32
    )


def load_weights(m, steps, wg_ref, wu_ref, w, sem):
    part, ff = w.shape[1], wg_ref.shape[1]
    copies = []
    for k, step in enumerate(steps):
        at = pl.multiple_of(lax.rem(m + step, MP) * part, part)
        for i, ref in enumerate((wg_ref, wu_ref)):
            copies.append(
                pltpu.make_async_copy(
                    ref.at[pl.ds(at, part)], w.at[k, :, pl.ds(i * ff, ff)], sem.at[k, i]
                )
            )
    return copies


def back_far_kernel(m_ref, a_ref, b_ref, c_ref, g_ref, wg_ref, wu_ref, *refs):
    high_ref, low_ref, s_ref, d_out = refs[:4]
    abc, d, w, in_sem, w_sem, out_sem = refs[4:]
    ff = a_ref.shape[1]
    tiles, _, rt, _ = abc.shape
    weights = load_weights(m_ref[0], (2,), wg_ref, wu_ref, w, w_sem)
    half = tiles // 2
    passes = g_ref.shape[0] // 2

    def arriving(r):
        at = pl.ds(pl.multiple_of(r * rt, rt), rt)
        return [
            pltpu.make_async_copy(ref.at[at], abc.at[r, i], in_sem.at[r, i])
            for i, ref in enumerate((a_ref, b_ref, c_ref))
        ]

    def leaving(r):
        at = pl.ds(pl.multiple_of(r * rt, rt), rt)
        return pltpu.make_async_copy(d.at[r], d_out.at[at], out_sem.at[r])

    for copy in arriving(0) + weights + sum((arriving(r) for r in range(1, tiles)), []):
        copy.start()
    for copy in weights:
        copy.wait()

    def step(r, carry):
        for copy in arriving(r):
            copy.wait()
        sums = contract_rows(abc[r, 2], g_ref[...].astype(bf16))
        lane = lax.broadcasted_iota(jnp.int32, (L, 2 * passes), 1)
        for p in range(rt // L):
            part = slice(p * L, (p + 1) * L)
            q = r * (rt // L) + p
            dact = g_ref[pl.ds(q, 1)].astype(bf16)
            d[r, part, :ff] = dact * abc[r, 0, part]
            d[r, part, ff:] = dact * abc[r, 1, part]
            mine = (lane == q) | (lane == q + passes)
            s_ref[pl.ds(pl.multiple_of(q * L, L), L)] = jnp.sum(
                jnp.where(mine, sums[part], 0.0), axis=1, keepdims=True
            )
        leaving(r).start()
        out = contract_rows(d[r], w[0]).astype(bf16)

        @pl.when(r < half)
        def _():
            high_ref[pl.ds(pl.multiple_of(r * rt, rt), rt)] = out

        @pl.when(r >= half)
        def _():
            low_ref[pl.ds(pl.multiple_of((r - half) * rt, rt), rt)] = out

        return carry

    lax.fori_loop(0, tiles, step, 0)
    for r in range(tiles):
        leaving(r).wait()


def back_far(m, a, b, c, g, w_gate, w_up):
    rows, ff = a.shape
    part = w_gate.shape[0] // MP
    rt = 256
    tiles = rows // rt
    anywhere = pl.BlockSpec(memory_space=pl.ANY)
    vmem = pl.BlockSpec(memory_space=pltpu.VMEM)
    return pl.pallas_call(
        back_far_kernel,
        in_specs=[pl.BlockSpec(memory_space=pltpu.SMEM)]
        + [anywhere] * 3
        + [vmem, anywhere, anywhere],
        out_specs=[vmem, vmem, vmem, anywhere],
        out_shape=[
            jax.ShapeDtypeStruct((rows // 2, part), bf16),
            jax.ShapeDtypeStruct((rows // 2, part), bf16),
            jax.ShapeDtypeStruct((rows, 1), f32),
            pltpu.HBM((rows, 2 * ff), bf16),
        ],
        scratch_shapes=[
            pltpu.VMEM((tiles, 3, rt, ff), bf16),
            pltpu.VMEM((tiles, rt, 2 * ff), bf16),
            pltpu.VMEM((1, part, 2 * ff), bf16),
            pltpu.SemaphoreType.DMA((tiles, 3)),
            pltpu.SemaphoreType.DMA((1, 2)),
            pltpu.SemaphoreType.DMA((tiles,)),
        ],
        compiler_params=pltpu.CompilerParams(vmem_limit_bytes=44 << 20),
        cost_estimate=pl.CostEstimate(flops=1, transcendentals=0, bytes_accessed=1),
        name="back_far",
    )(m, *map(in_hbm, (a, b, c)), g, in_hbm(w_gate), in_hbm(w_up))


def back_near_kernel(steps, m_ref, d_ref, wg_ref, wu_ref, *refs):
    count = 2 * len(steps)
    outs = refs[:count]
    d, w, out, in_sem, w_sem, out_sem = refs[count:]
    tiles, rt, _ = d.shape
    half = wg_ref.shape[1]
    weights = load_weights(m_ref[0], steps, wg_ref, wu_ref, w, w_sem)

    def arriving(r):
        at = pl.ds(pl.multiple_of(r * rt, rt), rt)
        return pltpu.make_async_copy(d_ref.at[at], d.at[r], in_sem.at[r])

    for copy in weights[:2] + [arriving(r) for r in range(tiles)] + weights[2:]:
        copy.start()

    def step(j, carry):
        k, r = j // tiles, lax.rem(j, tiles)

        @pl.when(r == 0)
        def _():
            for i in range(2):
                pltpu.make_async_copy(
                    wg_ref.at[pl.ds(0, w.shape[1])], w.at[k, :, pl.ds(i * half, half)], w_sem.at[k, i]
                ).wait()

        @pl.when(k == 0)
        def _():
            arriving(r).wait()

        out[j] = contract_rows(d[r], w[k]).astype(bf16)
        for i, ref in enumerate(outs):

            @pl.when(j == i)
            def _():
                pltpu.make_async_copy(out.at[j], ref, out_sem.at[i]).start()

        return carry

    lax.fori_loop(0, count, step, 0)
    for i, ref in enumerate(outs):
        pltpu.make_async_copy(out.at[i], ref, out_sem.at[i]).wait()


def back_near(m, steps, d, w_gate, w_up, flops):
    rows, ff2 = d.shape
    part = w_gate.shape[0] // MP
    tiles = 2
    count = tiles * len(steps)
    rt = rows // tiles
    anywhere = pl.BlockSpec(memory_space=pl.ANY)
    return pl.pallas_call(
        functools.partial(back_near_kernel, steps),
        in_specs=[pl.BlockSpec(memory_space=pltpu.SMEM)] + [anywhere] * 3,
        out_specs=[anywhere] * count,
        out_shape=[pltpu.HBM((rt, part), bf16)] * count,
        scratch_shapes=[
            pltpu.VMEM((tiles, rt, ff2), bf16),
            pltpu.VMEM((len(steps), part, ff2), bf16),
            pltpu.VMEM((count, rt, part), bf16),
            pltpu.SemaphoreType.DMA((tiles,)),
            pltpu.SemaphoreType.DMA((len(steps), 2)),
            pltpu.SemaphoreType.DMA((count,)),
        ],
        compiler_params=pltpu.CompilerParams(vmem_limit_bytes=44 << 20),
        cost_estimate=pl.CostEstimate(flops=flops, transcendentals=0, bytes_accessed=1),
        name="back_near",
    )(m, in_hbm(d), in_hbm(w_gate), in_hbm(w_up))


def finish_kernel(
    count, x_ref, own_ref, one_ref, two_ref, rms_ref, inner_ref, mask_ref, token_ref, gain_ref, *refs
):
    out_ref = refs[count]
    rms = rms_ref[...]
    normed = own_ref[...].astype(f32) + one_ref[...].astype(f32) + two_ref[...].astype(f32)
    grad = rms * gain_ref[...] * normed - x_ref[...].astype(f32) * (rms * rms * inner_ref[...])
    mask = mask_ref[...]
    for p in range(out_ref.shape[0] // L):
        part = slice(p * L, (p + 1) * L)
        out_ref[part] = (grad[part] + mask[part] * token_ref[0, p : p + 1]).astype(bf16)


def finish(chunk, before, x, own, one, two, rms, inner, mask, token, gain):
    rows, part = own.shape
    rt = 256
    steps = rows // rt
    here = pl.BlockSpec((rt, part), lambda r: (r, 0))
    whole = pl.BlockSpec((rt, part), lambda r: (chunk * steps + r, 0))
    column = pl.BlockSpec((rt, 1), lambda r: (chunk * steps + r, 0))
    return pl.pallas_call(
        functools.partial(finish_kernel, len(before)),
        grid=(steps,),
        in_specs=[whole, here, here, here, column, column, column]
        + [
            pl.BlockSpec((1, rt // L, part), lambda r: (chunk * steps + r, 0, 0)),
            pl.BlockSpec((1, part), lambda r: (0, 0)),
        ]
        + [pl.BlockSpec(memory_space=pl.ANY)] * len(before),
        out_specs=whole,
        out_shape=jax.ShapeDtypeStruct(x.shape, bf16),
        input_output_aliases={9 + k: k for k in range(len(before))},
        name="finish",
    )(x, own, one, two, rms, inner, mask, token.reshape(-1, rt // L, part), gain, *before)


def per_device(
    hidden_in, token_ids, passage_counts, positive_doc, queries, norm_gain, w_gate, w_up, w_down
):
    row_count, part = hidden_in.shape
    width = norm_gain.shape[0]
    docs = passage_counts.shape[0]
    passes = row_count // L
    most = passes // docs
    share = queries.shape[0] // MP
    chips = lax.axis_size(("x", "z"))
    cores = lax.axis_size("core")
    mi = lax.axis_index("mp")
    core = lax.axis_index("core")
    chip = lax.axis_index(("x", "z"))
    m = mi.astype(jnp.int32).reshape(1)

    mine = lax.all_to_all(
        queries.reshape(MP, share, part), "mp", split_axis=0, concat_axis=0, tiled=True
    )
    mine = jnp.moveaxis(mine, 0, 1).reshape(share, width)
    own_positive = lax.dynamic_slice_in_dim(positive_doc, mi * share, share)
    square = jnp.sum(mine.astype(f32) ** 2, axis=1)
    square_high = square.astype(bf16)
    square_low = (square - square_high.astype(f32)).astype(bf16)
    extra = jnp.stack([own_positive.astype(bf16), square_high, square_low], axis=1)
    extra = jnp.pad(extra, ((0, 0), (0, L - 3)))
    sent = jnp.concatenate([mine, extra], axis=1)

    chunks = []
    at = 0
    for k, rows in enumerate(CHUNKS):
        own = hidden_in[at : at + rows]
        if k == 1:
            own, sent = lax.optimization_barrier((own, sent))
        chunks.append((at, rows, own, shifted(own, 1), shifted(own, -1)))
        at += rows
    all_q = lax.all_gather(sent, ("x", "z"), axis=0)

    live_pass = jnp.arange(passes, dtype=jnp.int32) % most < jnp.repeat(passage_counts, most)
    other_live = swapped(live_pass.astype(jnp.int32)) > 0
    live = jnp.where(
        core == 0,
        jnp.concatenate([live_pass, other_live]),
        jnp.concatenate([other_live, live_pass]),
    ).astype(f32)[:, None]
    token_live = (token_ids.reshape(passes, L) != pad_token) & live_pass[:, None]
    live_float = token_live.astype(f32)
    mask = live_float.reshape(row_count, 1)
    divisor = jnp.maximum(jnp.sum(live_float, axis=1), 1.0)[:, None]
    gain = norm_gain.reshape(MP, 1, part)

    done = []
    before = ()
    for k, (at, rows, own, left, right) in enumerate(chunks):
        half = rows // 2
        high, low = shifted(left[:half], 1), shifted(right[half:], -1)
        part_mask = mask[at : at + rows]
        done.append(
            encode(
                m, k, row_count, before, own, right, left, high, low, part_mask, gain, w_gate, w_up
            )
        )
        before = done[-1][:3]
    a, b, c = before
    pool = jnp.concatenate([d[3] for d in done], axis=1)
    pool = jnp.moveaxis(pool, 0, 1).reshape(passes, -1)
    rms = jnp.concatenate([d[4] for d in done], axis=0)
    xpool = jnp.concatenate([d[5] for d in done], axis=0)

    high = pool.astype(bf16)
    low = (pool - high.astype(f32)).astype(bf16)
    branch = jnp.dot(jnp.concatenate([high, low], 0), w_down, preferred_element_type=f32)
    own_x = (jnp.arange(MP) == mi)[None, :, None].astype(f32) * xpool
    summed = (branch[:passes] + branch[passes:] + own_x.reshape(passes, width)) / divisor
    summed = copies_to_all(summed.astype(bf16), ("core", "mp"), cores * MP)
    summed = summed.reshape(cores, MP, passes, width).astype(f32).sum(axis=1)
    vecs = summed.reshape(cores * passes, width).astype(bf16)
    vec_float = vecs.astype(f32)
    vec_scale = lax.rsqrt(jnp.sum(vec_float * vec_float, axis=1, keepdims=True) + unit_epsilon)

    all_q = all_q.reshape(chips * share, width + L)
    q = all_q[:, :width]
    extra = all_q[:, width:].astype(f32)
    positive = extra[:, 0]
    query_scale = lax.rsqrt(extra[:, 1] + extra[:, 2] + unit_epsilon)
    raw = contract_rows(vecs, q)
    weights = live * jnp.exp(score_scale * raw * query_scale[None, :] * vec_scale)
    k = jnp.arange(cores * passes, dtype=jnp.int32)
    doc = chip * (cores * docs) + k // most
    hit = (positive[None, :] == doc.astype(f32)[:, None]).astype(f32)
    mass = jnp.stack([jnp.sum(weights, axis=0), jnp.sum(weights * hit, axis=0)])
    mass = copies_to_all(mass.reshape(8, -1), ("x", "z"), chips).sum(axis=0).reshape(2, -1)
    total, held = mass[0], mass[1]
    loss = jnp.log(total) - jnp.log(held)
    own_loss = lax.dynamic_slice_in_dim(loss, chip * share, share)

    coef = (loss_seed * score_scale) * query_scale[None, :] * (
        weights / total[None, :] - hit * weights / held[None, :]
    )
    grad = jnp.dot(coef.astype(bf16), q, preferred_element_type=f32)
    term = jnp.sum(coef * raw, axis=1, keepdims=True)
    grad = jnp.concatenate([grad, jnp.broadcast_to(term, (cores * passes, L))], axis=1).astype(bf16)
    grad = jnp.broadcast_to(
        grad.reshape(cores, 1, passes, width + L), (cores, MP, passes, width + L)
    ).reshape(cores * MP, passes, width + L)
    grad = lax.all_to_all(grad, ("core", "mp"), split_axis=0, concat_axis=0, tiled=True)
    grad = grad.astype(f32).sum(axis=0)
    own_vec = lax.dynamic_slice_in_dim(vec_float, core * passes, passes)
    scale = lax.dynamic_slice_in_dim(vec_scale, core * passes, passes)
    change = scale * grad[:, :width] - own_vec * (scale**3 * grad[:, width : width + 1])
    token_grad = (change / divisor).astype(bf16)
    dact = contract_rows(token_grad, w_down)
    dact_high = dact.astype(bf16).astype(f32)
    dact = jnp.concatenate([dact_high, dact - dact_high], axis=0)

    high, low, s, d = back_far(m, a, b, c, dact, w_gate, w_up)
    from_right = shifted(high, -1)
    from_left = shifted(low, 1)
    right_high, right_low, left_high, left_low = back_near(m, (1, 3), d, w_gate, w_up, 1)
    left_low = shifted(left_low, -1)
    right_high = shifted(right_high, 1)
    right_low = (right_low.astype(f32) + from_left.astype(f32)).astype(bf16)
    left_high = (left_high.astype(f32) + from_right.astype(f32)).astype(bf16)
    right_low, left_high, d = lax.optimization_barrier((right_low, left_high, d))
    right_low = shifted(right_low, 1)
    left_high = shifted(left_high, -1)
    own_high, own_low = back_near(m, (0,), d, w_gate, w_up, 1 << 38)
    small = jnp.concatenate(
        [s.reshape(passes, L), jnp.pad(own_loss[None, :], ((0, 7), (0, L - share)))], axis=0
    )
    own_high, small = lax.optimization_barrier((own_high, small))
    small = copies_to_all(small, "mp", MP)
    inner = small[:, :passes].sum(axis=0).reshape(row_count, 1) / width
    query_loss = small[:, passes, :share].reshape(MP * share)
    own_gain = lax.dynamic_slice_in_dim(norm_gain, mi * part, part)[None, :]
    own_token = lax.dynamic_slice_in_dim(token_grad, mi * part, part, axis=1).astype(f32)
    rest = (rms, inner, mask, own_token, own_gain)
    hidden_grad = finish(1, (), hidden_in, own_low, left_low, right_low, *rest)
    hidden_grad = finish(0, (hidden_grad,), hidden_in, own_high, left_high, right_high, *rest)
    return query_loss, hidden_grad


def solution(mesh):
    shape = (4, 4, 2, MP)
    split = Mesh(mesh.devices.reshape(shape), ("x", "z", "core", "mp"))
    dp = ("x", "z", "core")
    return jax.shard_map(
        per_device,
        mesh=split,
        in_specs=(
            P(dp, "mp"),
            P(dp),
            P(dp),
            P(dp),
            P(dp, "mp"),
            P(),
            P(None, "mp"),
            P(None, "mp"),
            P("mp", None),
        ),
        out_specs=(P(dp), P(dp, "mp")),
        check_vma=False,
    )
```

time: 233 us -> 208 us (0.89)
  the two profiles are of different devices: /device:TPU:24 before, /device:TPU:0 now
where the time goes in v3:
time: 208 us; the launch traced here: 207 us
  Pallas kernels  67.5 us (32%)
  waiting for transfers between devices  37.7 us (18%)
  starting transfers between devices  37.6 us (18%)
  blocking collectives  15.3 us (7%)
  between operations  14.5 us (7%)
  local copies, waits for them, and re-layouts  13.9 us (7%)
  matrix products  10.4 us (5%)
  other arithmetic  10.3 us (5%)
    pallas_call x2, Pallas kernels, encode(): pl.pallas_call(functools.partial(encode_kernel, chunk, len(before)), in_s...  29.8 us
    ppermute x14, starting transfers between devices, shifted(): return lax.ppermute(x, 'mp', [(i, (i + by) % MP) for i in range(MP)])  21.6 us
    pallas_call x2, Pallas kernels, back_near(): pl.pallas_call(functools.partial(back_near_kernel, steps), in_specs=[pl.B...  20.7 us
    ppermute x14, waiting for transfers between devices, shifted(): return lax.ppermute(x, 'mp', [(i, (i + by) % MP) for i in range(MP)])  16.5 us
    all_to_all x1, blocking collectives, copies_to_all(): lax.all_to_all(jnp.broadcast_to(x, (count, *x.shape)), axes, split_axis=0...  15.3 us
    pallas_call x1, Pallas kernels, back_far(): pl.pallas_call(back_far_kernel, in_specs=[pl.BlockSpec(memory_space=pltpu...  11.6 us
    all_to_all x2, starting transfers between devices, copies_to_all(): lax.all_to_all(jnp.broadcast_to(x, (count, *x.shape)), axes, split_axis=0...  9.01 us
    all_to_all x1, waiting for transfers between devices, per_device(): lax.all_to_all(queries.reshape(MP, share, part), 'mp', split_axis=0, conc...  8.5 us
  transfers between devices with their start and end apart: 20, of which 7 were waited for; matrix products, arithmetic and copies ran while one was open for 9% of the time, Pallas kernels for 26%

profile of v3, /device:TPU:0, one launch (start us, length us, event | category | flops | bytes accessed | tf_op | source)
XLA Modules:
  0.0 207.3 jit_solution(224342229452538755)
XLA Ops:
  11.8 3.3 %all-to-all-start = ((bf16[4,32,512]{2,1,0:T(8,128)(2,1)}), bf16[4,32,512]{2,1,0:T(8,128)(2,1)S(1)}, u32[]{:S(2)}, u32[]{:S(2)}) async-start(bf16[4,32,512]{2,1,0:T(8,128)(2,1)} %bitcast.77), calls=%async_computation | async-start | bytes 262144 | tf_op jit(solution)/shard_map/all_to_all | solution.py:426
  17.6 8.5 %all-to-all-done = bf16[4,32,512]{2,1,0:T(8,128)(2,1)S(1)} async-done(((bf16[4,32,512]{2,1,0:T(8,128)(2,1)}), bf16[4,32,512]{2,1,0:T(8,128)(2,1)S(1)}, u32[]{:S(2)}, u32[]{:S(2)}) %all-to-all-start) | async-done | bytes 131104 | tf_op jit(solution)/shard_map/all_to_all | solution.py:426
  28.3 2.1 %collective-permute-start = (bf16[512,512]{1,0:T(8,128)(2,1)S(1)}, bf16[512,512]{1,0:T(8,128)(2,1)S(1)}, u32[]{:S(2)}, u32[]{:S(2)}) collective-permute-start(bf16[512,512]{1,0:T(8,128)(2,1)S(1)} %get-tuple-element.31.own_ref), channel_id=1, source_target_pairs={{0,3},{1,0},{2,1},{3,2},{4,7},{5,4},{6,5},{7,6},{8,11},{9,8},{10,9... | collective-permute-start | bytes 1572872 | tf_op jit(solution)/shard_map/ppermute | solution.py:25
  31.8 3.2 %collective-permute-start.7 = (bf16[256,512]{1,0:T(8,128)(2,1)S(1)}, bf16[256,512]{1,0:T(8,128)(2,1)}, u32[]{:S(2)}, u32[]{:S(2)}) collective-permute-start(bf16[256,512]{1,0:T(8,128)(2,1)S(1)} %slice.97), channel_id=1, source_target_pairs={{0,3},{1,0},{2,1},{3,2},{4,7},{5,4},{6,5},{7,6},{8,11},{9,8},{10,9... | collective-permute-start | bytes 786440 | tf_op jit(solution)/shard_map/ppermute | solution.py:25
  35.3 7.9 %collective-permute-done.1.left_ref = bf16[512,512]{1,0:T(8,128)(2,1)S(1)} collective-permute-done((bf16[512,512]{1,0:T(8,128)(2,1)S(1)}, bf16[512,512]{1,0:T(8,128)(2,1)S(1)}, u32[]{:S(2)}, u32[]{:S(2)}) %collective-permute-start.1) | collective-permute-done | bytes 524320 | tf_op jit(solution)/shard_map/ppermute | solution.py:25
  43.4 3.3 %collective-permute-start.3 = (bf16[256,512]{1,0:T(8,128)(2,1)S(1)}, bf16[256,512]{1,0:T(8,128)(2,1)S(1)}, u32[]{:S(2)}, u32[]{:S(2)}) collective-permute-start(bf16[256,512]{1,0:T(8,128)(2,1)S(1)} %slice.95), channel_id=1, source_target_pairs={{0,3},{1,0},{2,1},{3,2},{4,7},{5,4},{6,5},{7,6},{8,11},{9,8},{10,9... | collective-permute-start | bytes 786440 | tf_op jit(solution)/shard_map/ppermute | solution.py:25
  46.6 2.3 %collective-permute-done.6.high_ref = bf16[256,512]{1,0:T(8,128)(2,1)} collective-permute-done((bf16[256,512]{1,0:T(8,128)(2,1)S(1)}, bf16[256,512]{1,0:T(8,128)(2,1)}, u32[]{:S(2)}, u32[]{:S(2)}) %collective-permute-start.6) | collective-permute-done | bytes 262176 | tf_op jit(solution)/shard_map/ppermute | solution.py:25
  49.0 14.9 %encode.2 = (bf16[1024,1792]{1,0:T(8,128)(2,1)}, bf16[1024,1792]{1,0:T(8,128)(2,1)}, bf16[1024,1792]{1,0:T(8,128)(2,1)}, f32[7,4,256]{2,1,0:T(4,128)S(1)}, f32[5...) custom-call(s32[1]{0:T(128)} %bitcast.m_ref, bf16[512,512]{1,0:T(8,128)(2,1)} %copy-done.8, ...), custom_call_target="tpu_custom_call" | custom-call | flops 7516192768 | bytes 22282240 | tf_op jit(solution)/shard_map/encode/pallas_call | solution.py:158
  64.7 14.9 %encode.3 = (bf16[1024,1792]{1,0:T(8,128)(2,1)}, bf16[1024,1792]{1,0:T(8,128)(2,1)}, bf16[1024,1792]{1,0:T(8,128)(2,1)}, f32[7,4,256]{2,1,0:T(4,128)S(1)}, f32[5...) custom-call(s32[1]{0:T(128)} %bitcast.m_ref, ...), custom_call_target="tpu_custom_call", output_to_operand_aliasing={{0}: (10, {}), {1}: (11, {}), {2}: (12, {})} | custom-call | flops 7516192768 | bytes 22282240 | tf_op jit(solution)/shard_map/encode/pallas_call | solution.py:158
  81.6 4.5 %all-to-all-start.1 = ((bf16[8,8,2048]{2,1,0:T(8,128)(2,1)}), bf16[8,8,2048]{2,1,0:T(8,128)(2,1)S(1)}, u32[]{:S(2)}, u32[]{:S(2)}) async-start(bf16[8,8,2048]{2,1,0:T(8,128)(2,1)} %broadcast_in_dim.19), calls=%async_computation.1 | async-start | bytes 524288 | tf_op jit(solution)/shard_map/all_to_all | solution.py:33
  86.2 6.8 %all-to-all-done.1 = bf16[8,8,2048]{2,1,0:T(8,128)(2,1)S(1)} async-done(((bf16[8,8,2048]{2,1,0:T(8,128)(2,1)}), bf16[8,8,2048]{2,1,0:T(8,128)(2,1)S(1)}, u32[]{:S(2)}, u32[]{:S(2)}) %all-to-all-start.1) | async-done | bytes 262176 | tf_op jit(solution)/shard_map/all_to_all | solution.py:33
  94.6 2.3 %fusion.20 = (f32[512]{0:T(512)S(1)}, f32[512]{0:T(512)S(1)}, f32[16,512]{1,0:T(8,128)S(1)}) fusion(f32[16]{0:T(128)S(1)} %rsqrt.32, f32[512]{0:T(512)S(1)} %get-tuple-element.61, f32[16]{0:T(128)S(1)} %fusion.26, f32[16]{0:T(128)S(1)} %fusion.30, f32[512]{0:T(512)S(1)} %get-tuple-element.62, bf16[512,2176]{1,0:T(8,128)(2,1)} %all-gather.3.cloned.1.call-done, ...), kind=kOutput, calls=%fused_computation.45 | convolution fusion | flops 33610752 | bytes 2203840 | tf_op jit(solution)/shard_map/dot_general | solution.py:195
  96.9 15.3 %all_to_all.25 = f32[16,8,128]{2,1,0:T(8,128)S(1)} all-to-all(f32[16,8,128]{2,1,0:T(8,128)S(1)} %broadcast_in_dim.20), channel_id=1, replica_groups=mesh['x'=4,'z'=4,'core'=2,'mp'=4] {'x','z'}, dimensions={0} | all-to-all | bytes 131072 | tf_op jit(solution)/shard_map/all_to_all | solution.py:33
  115.4 3.6 %all-to-all-start.3 = ((bf16[8,8,2176]{2,1,0:T(8,128)(2,1)}), bf16[8,8,2176]{2,1,0:T(8,128)(2,1)S(1)}, u32[]{:S(2)}, u32[]{:S(2)}) async-start(bf16[8,8,2176]{2,1,0:T(8,128)(2,1)} %bitcast.19), calls=%async_computation.3 | async-start | bytes 557056 | tf_op jit(solution)/shard_map/all_to_all | solution.py:515
  121.0 4.8 %all-to-all-done.3 = bf16[8,8,2176]{2,1,0:T(8,128)(2,1)S(1)} async-done(((bf16[8,8,2176]{2,1,0:T(8,128)(2,1)}), bf16[8,8,2176]{2,1,0:T(8,128)(2,1)S(1)}, u32[]{:S(2)}, u32[]{:S(2)}) %all-to-all-start.3) | async-done | bytes 278560 | tf_op jit(solution)/shard_map/all_to_all | solution.py:515
  126.1 5.1 %convert_convert_fusion = (f32[8,1792]{1,0:T(8,128)S(1)}, f32[8,1792]{1,0:T(8,128)S(1)}) fusion(bf16[8,2048]{1,0:T(8,128)(2,1)S(1)} %fusion.12, bf16[1792,2048]{1,0:T(8,128)(2,1)} %param.17), kind=kOutput, calls=%fused_computation.43 | convolution fusion | flops 58763264 | bytes 7487488 | tf_op jit(solution)/shard_map/dot_general | solution.py:195
  131.2 11.6 %back_far.1 = (bf16[512,512]{1,0:T(8,128)(2,1)S(1)}, bf16[512,512]{1,0:T(8,128)(2,1)S(1)}, f32[1024,1]{1,0:T(8,128)S(1)}, bf16[1024,3584]{1,0:T(8,128)(2,1)}) custom-call(s32[1]{0:T(128)} %bitcast.m_ref, bf16[1024,1792]{1,0:T(8,128)(2,1)} %get-tuple-element.35.a_ref, bf16[1024,1792]{1,0:T(8,128)(2,1)} %get-tuple-element.36.b_ref, ...), custom_call_target="tpu_custom_call" | custom-call | flops 1 | bytes 1 | tf_op jit(solution)/shard_map/back_far/pallas_call | solution.py:279
  146.1 12.4 %back_near.2 = (bf16[512,512]{1,0:T(8,128)(2,1)}, bf16[512,512]{1,0:T(8,128)(2,1)}, bf16[512,512]{1,0:T(8,128)(2,1)}, bf16[512,512]{1,0:T(8,128)(2,1)}) custom-call(s32[1]{0:T(128)} %bitcast.m_ref, bf16[1024,3584]{1,0:T(8,128)(2,1)} %get-tuple-element.48.d_ref, bf16[2048,1792]{1,0:T(8,128)(2,1)} %wg_ref.9, bf16[2048,1792]{1,0:T(8,128)(2,1)} %wu_ref.9), custom_call_target="tpu_custom_call" | custom-call | flops 1 | bytes 1 | tf_op jit(solution)/shard_map/back_near/pallas_call | solution.py:355
  158.5 3.0 %collective-permute-start.13 = (bf16[512,512]{1,0:T(8,128)(2,1)}, bf16[512,512]{1,0:T(8,128)(2,1)}, u32[]{:S(2)}, u32[]{:S(2)}) collective-permute-start(bf16[512,512]{1,0:T(8,128)(2,1)} %get-tuple-element.58), channel_id=1, source_target_pairs={{0,3},{1,0},{2,1},{3,2},{4,7},{5,4},{6,5},{7,6},{8,11},{9,8},{10,9... | collective-permute-start | bytes 1572872 | tf_op jit(solution)/shard_map/ppermute | solution.py:25
  166.3 8.3 %back_near.3 = (bf16[512,512]{1,0:T(8,128)(2,1)}, bf16[512,512]{1,0:T(8,128)(2,1)}) custom-call(s32[1]{0:T(128)} %bitcast.m_ref, bf16[1024,3584]{1,0:T(8,128)(2,1)} %get-tuple-element.48.d_ref, bf16[2048,1792]{1,0:T(8,128)(2,1)} %wg_ref.9, bf16[2048,1792]{1,0:T(8,128)(2,1)} %wu_ref.9), custom_call_target="tpu_custom_call" | custom-call | flops 274877906944 | bytes 1 | tf_op jit(solution)/shard_map/back_near/pallas_call | solution.py:355
  175.2 4.5 %all-to-all-start.4 = ((f32[4,16,128]{2,1,0:T(8,128)}), f32[4,16,128]{2,1,0:T(8,128)S(1)}, u32[]{:S(2)}, u32[]{:S(2)}) async-start(f32[4,16,128]{2,1,0:T(8,128)} %broadcast_in_dim.46), calls=%async_computation.4 | async-start | bytes 65536 | tf_op jit(solution)/shard_map/all_to_all | solution.py:33
  187.1 6.3 %collective-permute-done.14.two_ref = bf16[512,512]{1,0:T(8,128)(2,1)S(1)} collective-permute-done((bf16[512,512]{1,0:T(8,128)(2,1)S(1)}, bf16[512,512]{1,0:T(8,128)(2,1)S(1)}, u32[]{:S(2)}, u32[]{:S(2)}) %collective-permute-start.14) | collective-permute-done | bytes 524320 | tf_op jit(solution)/shard_map/ppermute | solution.py:25
  194.1 2.7 %finish.2.refs_0_ = bf16[1024,512]{1,0:T(8,128)(2,1)} custom-call(bf16[1024,512]{1,0:T(8,128)(2,1)} %x_ref.3, bf16[512,512]{1,0:T(8,128)(2,1)} %get-tuple-element.57.own_ref, bf16[512,512]{1,0:T(8,128)(2,1)} %collective-permute-done.13.one_ref, bf16[512,512]{1,0:T(8,128)(2,1)} %copy-done.7, f32[1024,1]{1,0:T(8,128)} %copy.51.rms_ref, ...), custom_call_target="tpu_custom_call" | custom-call | tf_op jit(solution)/shard_map/finish/pallas_call | solution.py:394
  197.7 2.7 %finish.3 = bf16[1024,512]{1,0:T(8,128)(2,1)} custom-call(bf16[1024,512]{1,0:T(8,128)(2,1)} %x_ref.3, bf16[512,512]{1,0:T(8,128)(2,1)} %get-tuple-element.52.own_ref, bf16[512,512]{1,0:T(8,128)(2,1)} %copy-done.5, bf16[512,512]{1,0:T(8,128)(2,1)} %collective-permute-done.12.two_ref, f32[1024,1]{1,0:T(8,128)} %copy.51.rms_ref, ...), custom_call_target="tpu_custom_call", output_to_operand_aliasing={{}: (9, {})} | custom-call | tf_op jit(solution)/shard_map/finish/pallas_call | solution.py:394
  (138 shorter events, 38.4 us)
Async XLA Ops:
  7.2 41.8 %copy-start = (f32[2048]{0:T(1024)S(1)}, f32[2048]{0:T(1024)}, u32[]{:S(2)}) copy-start(f32[2048]{0:T(1024)} %param.14) | copy-start | bytes 24580
  8.4 40.5 %copy-start.8 = (bf16[512,512]{1,0:T(8,128)(2,1)}, bf16[512,512]{1,0:T(8,128)(2,1)S(1)}, u32[]{:S(2)}) copy-start(bf16[512,512]{1,0:T(8,128)(2,1)S(1)} %get-tuple-element.73.own_ref) | copy-start | bytes 1572868
  8.5 55.4 %copy-start.1 = (bf16[512,512]{1,0:T(8,128)(2,1)}, bf16[512,512]{1,0:T(8,128)(2,1)S(1)}, u32[]{:S(2)}) copy-start(bf16[512,512]{1,0:T(8,128)(2,1)S(1)} %get-tuple-element.31.own_ref) | copy-start | bytes 1572868
  8.5 22.1 %collective-permute-start.5 = (bf16[512,512]{1,0:T(8,128)(2,1)S(1)}, bf16[512,512]{1,0:T(8,128)(2,1)S(1)}, u32[]{:S(2)}, u32[]{:S(2)}) collective-permute-start(bf16[512,512]{1,0:T(8,128)(2,1)S(1)} %get-tuple-element.73.own_ref), channel_id=1, source_target_pairs={{0,1},{1,2},{2,3},{3,0},{4,5},{5,6},{6,7},{7,4},{8,9},{9,10},{10,1... | collective-permute-start | bytes 1572872 | tf_op jit(solution)/shard_map/ppermute | solution.py:25
  10.2 20.5 %collective-permute-start.4 = (bf16[512,512]{1,0:T(8,128)(2,1)S(1)}, bf16[512,512]{1,0:T(8,128)(2,1)}, u32[]{:S(2)}, u32[]{:S(2)}) collective-permute-start(bf16[512,512]{1,0:T(8,128)(2,1)S(1)} %get-tuple-element.73.own_ref), channel_id=1, source_target_pairs={{0,3},{1,0},{2,1},{3,2},{4,7},{5,4},{6,5},{7,6},{8,11},{9,8},{10,9... | collective-permute-start | bytes 1572872 | tf_op jit(solution)/shard_map/ppermute | solution.py:25
  11.8 14.4 %all-to-all-start = ((bf16[4,32,512]{2,1,0:T(8,128)(2,1)}), bf16[4,32,512]{2,1,0:T(8,128)(2,1)S(1)}, u32[]{:S(2)}, u32[]{:S(2)}) async-start(bf16[4,32,512]{2,1,0:T(8,128)(2,1)} %bitcast.77), calls=%async_computation | async-start | bytes 262144 | tf_op jit(solution)/shard_map/all_to_all | solution.py:426
  15.1 78.1 %all-gather.3.cloned.1.call-start = ((), (), s32[]{:S(2)}) async-start(), calls=%async_computation.5 | async-start | bytes 2367488 | tf_op jit(solution)/shard_map/all_gather | solution.py:446
  16.0 70.1 %collective-permute-start.8 = (s32[8]{0:T(128)S(1)}, s32[8]{0:T(128)S(1)}, u32[]{:S(2)}, u32[]{:S(2)}) collective-permute-start(s32[8]{0:T(128)S(1)} %get-tuple-element.69), channel_id=1, source_target_pairs={{0,4},{4,0},{1,5},{5,1},{2,6},{6,2},{3,7},{7,3},{8,12},{12,8},{9,1... | collective-permute-start | bytes 104 | tf_op jit(solution)/shard_map/ppermute | solution.py:29
  27.1 16.1 %collective-permute-start.1 = (bf16[512,512]{1,0:T(8,128)(2,1)S(1)}, bf16[512,512]{1,0:T(8,128)(2,1)S(1)}, u32[]{:S(2)}, u32[]{:S(2)}) collective-permute-start(bf16[512,512]{1,0:T(8,128)(2,1)S(1)} %get-tuple-element.31.own_ref), channel_id=1, source_target_pairs={{0,1},{1,2},{2,3},{3,0},{4,5},{5,6},{6,7},{7,4},{8,9},{9,10},{10,1... | collective-permute-start | bytes 1572872 | tf_op jit(solution)/shard_map/ppermute | solution.py:25
  28.3 15.0 %collective-permute-start = (bf16[512,512]{1,0:T(8,128)(2,1)S(1)}, bf16[512,512]{1,0:T(8,128)(2,1)S(1)}, u32[]{:S(2)}, u32[]{:S(2)}) collective-permute-start(bf16[512,512]{1,0:T(8,128)(2,1)S(1)} %get-tuple-element.31.own_ref), channel_id=1, source_target_pairs={{0,3},{1,0},{2,1},{3,2},{4,7},{5,4},{6,5},{7,6},{8,11},{9,8},{10,9... | collective-permute-start | bytes 1572872 | tf_op jit(solution)/shard_map/ppermute | solution.py:25
  30.6 18.3 %collective-permute-start.6 = (bf16[256,512]{1,0:T(8,128)(2,1)S(1)}, bf16[256,512]{1,0:T(8,128)(2,1)}, u32[]{:S(2)}, u32[]{:S(2)}) collective-permute-start(bf16[256,512]{1,0:T(8,128)(2,1)S(1)} %slice.96), channel_id=1, source_target_pairs={{0,1},{1,2},{2,3},{3,0},{4,5},{5,6},{6,7},{7,4},{8,9},{9,10},{10,1... | collective-permute-start | bytes 786440 | tf_op jit(solution)/shard_map/ppermute | solution.py:25
  31.8 17.2 %collective-permute-start.7 = (bf16[256,512]{1,0:T(8,128)(2,1)S(1)}, bf16[256,512]{1,0:T(8,128)(2,1)}, u32[]{:S(2)}, u32[]{:S(2)}) collective-permute-start(bf16[256,512]{1,0:T(8,128)(2,1)S(1)} %slice.97), channel_id=1, source_target_pairs={{0,3},{1,0},{2,1},{3,2},{4,7},{5,4},{6,5},{7,6},{8,11},{9,8},{10,9... | collective-permute-start | bytes 786440 | tf_op jit(solution)/shard_map/ppermute | solution.py:25
  43.2 20.7 %collective-permute-start.2 = (bf16[256,512]{1,0:T(8,128)(2,1)S(1)}, bf16[256,512]{1,0:T(8,128)(2,1)S(1)}, u32[]{:S(2)}, u32[]{:S(2)}) collective-permute-start(bf16[256,512]{1,0:T(8,128)(2,1)S(1)} %slice.94), channel_id=1, source_target_pairs={{0,1},{1,2},{2,3},{3,0},{4,5},{5,6},{6,7},{7,4},{8,9},{9,10},{10,1... | collective-permute-start | bytes 786440 | tf_op jit(solution)/shard_map/ppermute | solution.py:25
  43.4 20.6 %collective-permute-start.3 = (bf16[256,512]{1,0:T(8,128)(2,1)S(1)}, bf16[256,512]{1,0:T(8,128)(2,1)S(1)}, u32[]{:S(2)}, u32[]{:S(2)}) collective-permute-start(bf16[256,512]{1,0:T(8,128)(2,1)S(1)} %slice.95), channel_id=1, source_target_pairs={{0,3},{1,0},{2,1},{3,2},{4,7},{5,4},{6,5},{7,6},{8,11},{9,8},{10,9... | collective-permute-start | bytes 786440 | tf_op jit(solution)/shard_map/ppermute | solution.py:25
  48.9 30.7 %slice-start = ((s8[7340032]{0:T(1024)(128)(4,1)}), s8[4194304]{0:T(1024)(128)(4,1)S(1)}, s32[]{:S(2)}) async-start(s8[7340032]{0:T(1024)(128)(4,1)} %bitcast.71), calls=%async_computation.6 | async-start | bytes 8388608
  81.6 11.4 %all-to-all-start.1 = ((bf16[8,8,2048]{2,1,0:T(8,128)(2,1)}), bf16[8,8,2048]{2,1,0:T(8,128)(2,1)S(1)}, u32[]{:S(2)}, u32[]{:S(2)}) async-start(bf16[8,8,2048]{2,1,0:T(8,128)(2,1)} %broadcast_in_dim.19), calls=%async_computation.1 | async-start | bytes 524288 | tf_op jit(solution)/shard_map/all_to_all | solution.py:33
  115.4 10.4 %all-to-all-start.3 = ((bf16[8,8,2176]{2,1,0:T(8,128)(2,1)}), bf16[8,8,2176]{2,1,0:T(8,128)(2,1)S(1)}, u32[]{:S(2)}, u32[]{:S(2)}) async-start(bf16[8,8,2176]{2,1,0:T(8,128)(2,1)} %bitcast.19), calls=%async_computation.3 | async-start | bytes 557056 | tf_op jit(solution)/shard_map/all_to_all | solution.py:515
  142.9 19.5 %collective-permute-start.10 = (bf16[512,512]{1,0:T(8,128)(2,1)S(1)}, bf16[512,512]{1,0:T(8,128)(2,1)S(1)}, u32[]{:S(2)}, u32[]{:S(2)}) collective-permute-start(bf16[512,512]{1,0:T(8,128)(2,1)S(1)} %get-tuple-element.47), channel_id=1, source_target_pairs={{0,3},{1,0},{2,1},{3,2},{4,7},{5,4},{6,5},{7,6},{8,11},{9,8},{10,9... | collective-permute-start | bytes 1572872 | tf_op jit(solution)/shard_map/ppermute | solution.py:25
  145.7 18.6 %collective-permute-start.9 = (bf16[512,512]{1,0:T(8,128)(2,1)S(1)}, bf16[512,512]{1,0:T(8,128)(2,1)S(1)}, u32[]{:S(2)}, u32[]{:S(2)}) collective-permute-start(bf16[512,512]{1,0:T(8,128)(2,1)S(1)} %get-tuple-element.45), channel_id=1, source_target_pairs={{0,1},{1,2},{2,3},{3,0},{4,5},{5,6},{6,7},{7,4},{8,9},{9,10},{10,1... | collective-permute-start | bytes 1572872 | tf_op jit(solution)/shard_map/ppermute | solution.py:25
  158.5 28.6 %collective-permute-start.13 = (bf16[512,512]{1,0:T(8,128)(2,1)}, bf16[512,512]{1,0:T(8,128)(2,1)}, u32[]{:S(2)}, u32[]{:S(2)}) collective-permute-start(bf16[512,512]{1,0:T(8,128)(2,1)} %get-tuple-element.58), channel_id=1, source_target_pairs={{0,3},{1,0},{2,1},{3,2},{4,7},{5,4},{6,5},{7,6},{8,11},{9,8},{10,9... | collective-permute-start | bytes 1572872 | tf_op jit(solution)/shard_map/ppermute | solution.py:25
  161.5 35.3 %collective-permute-start.12 = (bf16[512,512]{1,0:T(8,128)(2,1)}, bf16[512,512]{1,0:T(8,128)(2,1)}, u32[]{:S(2)}, u32[]{:S(2)}) collective-permute-start(bf16[512,512]{1,0:T(8,128)(2,1)} %get-tuple-element.54), channel_id=1, source_target_pairs={{0,1},{1,2},{2,3},{3,0},{4,5},{5,6},{6,7},{7,4},{8,9},{9,10},{10,1... | collective-permute-start | bytes 1572872 | tf_op jit(solution)/shard_map/ppermute | solution.py:25
  175.2 10.2 %all-to-all-start.4 = ((f32[4,16,128]{2,1,0:T(8,128)}), f32[4,16,128]{2,1,0:T(8,128)S(1)}, u32[]{:S(2)}, u32[]{:S(2)}) async-start(f32[4,16,128]{2,1,0:T(8,128)} %broadcast_in_dim.46), calls=%async_computation.4 | async-start | bytes 65536 | tf_op jit(solution)/shard_map/all_to_all | solution.py:33
  179.7 13.6 %collective-permute-start.14 = (bf16[512,512]{1,0:T(8,128)(2,1)S(1)}, bf16[512,512]{1,0:T(8,128)(2,1)S(1)}, u32[]{:S(2)}, u32[]{:S(2)}) collective-permute-start(bf16[512,512]{1,0:T(8,128)(2,1)S(1)} %copy-done.6), channel_id=1, source_target_pairs={{0,1},{1,2},{2,3},{3,0},{4,5},{5,6},{6,7},{7,4},{8,9},{9,10},{10,1... | collective-permute-start | bytes 1572872 | tf_op jit(solution)/shard_map/ppermute | solution.py:25
  181.7 15.1 %collective-permute-start.11 = (bf16[512,512]{1,0:T(8,128)(2,1)S(1)}, bf16[512,512]{1,0:T(8,128)(2,1)S(1)}, u32[]{:S(2)}, u32[]{:S(2)}) collective-permute-start(bf16[512,512]{1,0:T(8,128)(2,1)S(1)} %copy-done.4), channel_id=1, source_target_pairs={{0,3},{1,0},{2,1},{3,2},{4,7},{5,4},{6,5},{7,6},{8,11},{9,8},{10,9... | collective-permute-start | bytes 1572872 | tf_op jit(solution)/shard_map/ppermute | solution.py:25
  (12 other events, 106.0 us)
Sparse Core Ops, SparseCore 0:
  30.5 45.3 all-gather.2

commit v4 on v3

--- a/solution.py
+++ b/solution.py
@@ -15,7 +15,7 @@
 unit_epsilon = 1e-06
 MP = 4
 FT = 256
-ROW_STEP = 512
+SCOPED = 40 << 20
 CHUNKS = (512, 512)
 bf16 = jnp.bfloat16
 f32 = jnp.float32
@@ -25,6 +25,11 @@
     return lax.ppermute(x, "mp", [(i, (i + by) % MP) for i in range(MP)])
 
 
+def across(left, right):
+    half = left.shape[0] // 2
+    return shifted(left[:half], 1), shifted(right[half:], -1)
+
+
 def swapped(x):
     return lax.ppermute(x, "core", [(0, 1), (1, 0)])
 
@@ -37,6 +42,25 @@
 
 def in_hbm(x):
     return pltpu.with_memory_space_constraint(x, pltpu.HBM)
+
+
+def contract_rows(left, right):
+    return lax.dot_general(
+        left, right, (((1,), (1,)), ((), ())), preferred_element_type=f32
+    )
+
+
+def each(count, body):
+    def step(n, carry):
+        body(n)
+        return carry
+
+    lax.fori_loop(0, count, step, 0)
+
+
+anywhere = pl.BlockSpec(memory_space=pl.ANY)
+vmem = pl.BlockSpec(memory_space=pltpu.VMEM)
+smem = pl.BlockSpec(memory_space=pltpu.SMEM)
 
 
 def encode_kernel(
@@ -83,13 +107,6 @@
             for i, out in enumerate((a_out, b_out, c_out))
         ]
 
-    def each(count, body):
-        def step(n, carry):
-            body(n)
-            return carry
-
-        lax.fori_loop(0, count, step, 0)
-
     def start_weights(n):
         for copy in weight_copies(n):
             copy.start()
@@ -119,8 +136,8 @@
     def multiply(n):
         for copy in weight_copies(n):
             copy.wait()
-        for r in range(0, rows, ROW_STEP):
-            at = slice(r, r + ROW_STEP)
+        for r in range(0, rows, rows):
+            at = slice(r, r + rows)
             both = jnp.dot(xs[at], w[n], preferred_element_type=f32)
             gate, up = both[:, :FT], both[:, FT:]
             mask = mask_ref[at]
@@ -129,7 +146,7 @@
             b = gate * sig
             bu = b * up
             act = bu.astype(bf16).astype(f32)
-            for p in range(ROW_STEP // L):
+            for p in range(rows // L):
                 q = r // L + p
                 pool_ref[n, q : q + 1] = jnp.sum(act[p * L : (p + 1) * L], axis=0, keepdims=True)
             a = up * (sig + b * (1.0 - sig))
@@ -153,11 +170,9 @@
     width, ff = w_gate.shape
     passes = rows // L
     tiles = ff // FT
-    anywhere = pl.BlockSpec(memory_space=pl.ANY)
-    vmem = pl.BlockSpec(memory_space=pltpu.VMEM)
     return pl.pallas_call(
         functools.partial(encode_kernel, chunk, len(before)),
-        in_specs=[pl.BlockSpec(memory_space=pltpu.SMEM)]
+        in_specs=[smem]
         + [anywhere] * 5
         + [vmem, vmem, anywhere, anywhere]
         + [anywhere] * len(before),
@@ -191,12 +206,6 @@
     )
 
 
-def contract_rows(left, right):
-    return lax.dot_general(
-        left, right, (((1,), (1,)), ((), ())), preferred_element_type=f32
-    )
-
-
 def load_weights(m, steps, wg_ref, wu_ref, w, sem):
     part, ff = w.shape[1], wg_ref.shape[1]
     copies = []
@@ -211,200 +220,176 @@
     return copies
 
 
-def back_far_kernel(m_ref, a_ref, b_ref, c_ref, g_ref, wg_ref, wu_ref, *refs):
-    high_ref, low_ref, s_ref, d_out = refs[:4]
-    abc, d, w, in_sem, w_sem, out_sem = refs[4:]
+def back_kernel(steps, first, m_ref, a_ref, b_ref, c_ref, g_in, gs_ref, wg_ref, wu_ref, *refs):
+    if first:
+        wd_ref, *refs = refs
+    count = 2 * len(steps)
+    outs = refs[:count]
+    last = not first and len(steps) == 1
+    if first:
+        g_ref, ab, w, in_sem, w_sem = refs[count:]
+    elif last:
+        s_ref, c, ab, w, in_sem, w_sem = refs[count:]
+    else:
+        ab, w, in_sem, w_sem = refs[count:]
+    part = outs[0].shape[1]
     ff = a_ref.shape[1]
-    tiles, _, rt, _ = abc.shape
-    weights = load_weights(m_ref[0], (2,), wg_ref, wu_ref, w, w_sem)
-    half = tiles // 2
-    passes = g_ref.shape[0] // 2
+    tiles, rt, _ = ab.shape
+    here = tiles // 2
+    weights = load_weights(m_ref[0], steps, wg_ref, wu_ref, w, w_sem)
+    passes = g_in.shape[0]
 
     def arriving(r):
         at = pl.ds(pl.multiple_of(r * rt, rt), rt)
-        return [
-            pltpu.make_async_copy(ref.at[at], abc.at[r, i], in_sem.at[r, i])
-            for i, ref in enumerate((a_ref, b_ref, c_ref))
+        copies = [
+            pltpu.make_async_copy(ref.at[at], ab.at[r, :, pl.ds(i * ff, ff)], in_sem.at[r, i])
+            for i, ref in enumerate((a_ref, b_ref))
         ]
-
-    def leaving(r):
-        at = pl.ds(pl.multiple_of(r * rt, rt), rt)
-        return pltpu.make_async_copy(d.at[r], d_out.at[at], out_sem.at[r])
-
-    for copy in arriving(0) + weights + sum((arriving(r) for r in range(1, tiles)), []):
+        if last:
+            copies.append(pltpu.make_async_copy(c_ref.at[at], c.at[r], in_sem.at[r, 2]))
+        return copies
+
+    for copy in arriving(0) + weights[:2]:
         copy.start()
-    for copy in weights:
-        copy.wait()
-
-    def step(r, carry):
+    for r in range(1, tiles):
+        for copy in arriving(r):
+            copy.start()
+    for copy in weights[2:]:
+        copy.start()
+
+    if first:
+
+        def dact_tile(n):
+            at = pl.ds(pl.multiple_of(n * FT, FT), FT)
+            g_ref[:, at] = contract_rows(wd_ref[at], g_in[...]).T
+
+        each(ff // FT, dact_tile)
+        source = g_ref
+    else:
+        source = g_in
+
+    def scale(r):
         for copy in arriving(r):
             copy.wait()
-        sums = contract_rows(abc[r, 2], g_ref[...].astype(bf16))
         lane = lax.broadcasted_iota(jnp.int32, (L, 2 * passes), 1)
         for p in range(rt // L):
-            part = slice(p * L, (p + 1) * L)
+            at = slice(p * L, (p + 1) * L)
             q = r * (rt // L) + p
-            dact = g_ref[pl.ds(q, 1)].astype(bf16)
-            d[r, part, :ff] = dact * abc[r, 0, part]
-            d[r, part, ff:] = dact * abc[r, 1, part]
-            mine = (lane == q) | (lane == q + passes)
-            s_ref[pl.ds(pl.multiple_of(q * L, L), L)] = jnp.sum(
-                jnp.where(mine, sums[part], 0.0), axis=1, keepdims=True
-            )
-        leaving(r).start()
-        out = contract_rows(d[r], w[0]).astype(bf16)
-
-        @pl.when(r < half)
+            dact = source[pl.ds(q, 1)].astype(bf16)
+            ab[r, at, :ff] = dact * ab[r, at, :ff]
+            ab[r, at, ff:] = dact * ab[r, at, ff:]
+            if last:
+                sums = contract_rows(c[r, at], gs_ref[...])
+                mine = (lane == q) | (lane == q + passes)
+                s_ref[pl.ds(pl.multiple_of(q * L, L), L)] = jnp.sum(
+                    jnp.where(mine, sums, 0.0), axis=1, keepdims=True
+                )
+
+    def multiply(j):
+        k, r = j // tiles, lax.rem(j, tiles)
+
+        @pl.when(k == 0)
         def _():
-            high_ref[pl.ds(pl.multiple_of(r * rt, rt), rt)] = out
-
-        @pl.when(r >= half)
-        def _():
-            low_ref[pl.ds(pl.multiple_of((r - half) * rt, rt), rt)] = out
-
-        return carry
-
-    lax.fori_loop(0, tiles, step, 0)
-    for r in range(tiles):
-        leaving(r).wait()
-
-
-def back_far(m, a, b, c, g, w_gate, w_up):
-    rows, ff = a.shape
-    part = w_gate.shape[0] // MP
-    rt = 256
-    tiles = rows // rt
-    anywhere = pl.BlockSpec(memory_space=pl.ANY)
-    vmem = pl.BlockSpec(memory_space=pltpu.VMEM)
-    return pl.pallas_call(
-        back_far_kernel,
-        in_specs=[pl.BlockSpec(memory_space=pltpu.SMEM)]
-        + [anywhere] * 3
-        + [vmem, anywhere, anywhere],
-        out_specs=[vmem, vmem, vmem, anywhere],
-        out_shape=[
-            jax.ShapeDtypeStruct((rows // 2, part), bf16),
-            jax.ShapeDtypeStruct((rows // 2, part), bf16),
-            jax.ShapeDtypeStruct((rows, 1), f32),
-            pltpu.HBM((rows, 2 * ff), bf16),
-        ],
-        scratch_shapes=[
-            pltpu.VMEM((tiles, 3, rt, ff), bf16),
-            pltpu.VMEM((tiles, rt, 2 * ff), bf16),
-            pltpu.VMEM((1, part, 2 * ff), bf16),
-            pltpu.SemaphoreType.DMA((tiles, 3)),
-            pltpu.SemaphoreType.DMA((1, 2)),
-            pltpu.SemaphoreType.DMA((tiles,)),
-        ],
-        compiler_params=pltpu.CompilerParams(vmem_limit_bytes=44 << 20),
-        cost_estimate=pl.CostEstimate(flops=1, transcendentals=0, bytes_accessed=1),
-        name="back_far",
-    )(m, *map(in_hbm, (a, b, c)), g, in_hbm(w_gate), in_hbm(w_up))
-
-
-def back_near_kernel(steps, m_ref, d_ref, wg_ref, wu_ref, *refs):
-    count = 2 * len(steps)
-    outs = refs[:count]
-    d, w, out, in_sem, w_sem, out_sem = refs[count:]
-    tiles, rt, _ = d.shape
-    half = wg_ref.shape[1]
-    weights = load_weights(m_ref[0], steps, wg_ref, wu_ref, w, w_sem)
-
-    def arriving(r):
-        at = pl.ds(pl.multiple_of(r * rt, rt), rt)
-        return pltpu.make_async_copy(d_ref.at[at], d.at[r], in_sem.at[r])
-
-    for copy in weights[:2] + [arriving(r) for r in range(tiles)] + weights[2:]:
-        copy.start()
-
-    def step(j, carry):
-        k, r = j // tiles, lax.rem(j, tiles)
+            scale(r)
 
         @pl.when(r == 0)
         def _():
             for i in range(2):
                 pltpu.make_async_copy(
-                    wg_ref.at[pl.ds(0, w.shape[1])], w.at[k, :, pl.ds(i * half, half)], w_sem.at[k, i]
+                    wg_ref.at[pl.ds(0, part)], w.at[k, :, pl.ds(i * ff, ff)], w_sem.at[k, i]
                 ).wait()
 
-        @pl.when(k == 0)
-        def _():
-            arriving(r).wait()
-
-        out[j] = contract_rows(d[r], w[k]).astype(bf16)
+        out = contract_rows(ab[r], w[k]).astype(bf16)
+        at = pl.ds(pl.multiple_of(lax.rem(j, here) * rt, rt), rt)
         for i, ref in enumerate(outs):
 
-            @pl.when(j == i)
+            @pl.when(j // here == i)
             def _():
-                pltpu.make_async_copy(out.at[j], ref, out_sem.at[i]).start()
-
-        return carry
-
-    lax.fori_loop(0, count, step, 0)
-    for i, ref in enumerate(outs):
-        pltpu.make_async_copy(out.at[i], ref, out_sem.at[i]).wait()
-
-
-def back_near(m, steps, d, w_gate, w_up, flops):
-    rows, ff2 = d.shape
-    part = w_gate.shape[0] // MP
-    tiles = 2
-    count = tiles * len(steps)
-    rt = rows // tiles
-    anywhere = pl.BlockSpec(memory_space=pl.ANY)
+                ref[at] = out
+
+    each(len(steps) * tiles, multiply)
+
+
+def back(m, steps, rt, first, a, b, c, g, gs, w_gate, w_up, w_down):
+    rows, ff = a.shape
+    width = w_gate.shape[0]
+    part = width // MP
+    tiles = rows // rt
+    last = not first and len(steps) == 1
+    out = pltpu.HBM((rows // 2, part), bf16)
+    more = []
+    scratch = []
+    if first:
+        more = [jax.ShapeDtypeStruct((g.shape[0], ff), f32)]
+    elif last:
+        more = [jax.ShapeDtypeStruct((rows, 1), f32)]
+        scratch = [pltpu.VMEM((tiles, rt, ff), bf16)]
     return pl.pallas_call(
-        functools.partial(back_near_kernel, steps),
-        in_specs=[pl.BlockSpec(memory_space=pltpu.SMEM)] + [anywhere] * 3,
-        out_specs=[anywhere] * count,
-        out_shape=[pltpu.HBM((rt, part), bf16)] * count,
-        scratch_shapes=[
-            pltpu.VMEM((tiles, rt, ff2), bf16),
-            pltpu.VMEM((len(steps), part, ff2), bf16),
-            pltpu.VMEM((count, rt, part), bf16),
-            pltpu.SemaphoreType.DMA((tiles,)),
+        functools.partial(back_kernel, steps, first),
+        in_specs=[smem] + [anywhere] * 3 + [vmem] * 2 + [anywhere] * 2 + [vmem] * first,
+        out_specs=[vmem] * (2 * len(steps) + len(more)),
+        out_shape=[out] * (2 * len(steps)) + more,
+        scratch_shapes=scratch
+        + [
+            pltpu.VMEM((tiles, rt, 2 * ff), bf16),
+            pltpu.VMEM((len(steps), part, 2 * ff), bf16),
+            pltpu.SemaphoreType.DMA((tiles, 3)),
             pltpu.SemaphoreType.DMA((len(steps), 2)),
-            pltpu.SemaphoreType.DMA((count,)),
         ],
-        compiler_params=pltpu.CompilerParams(vmem_limit_bytes=44 << 20),
-        cost_estimate=pl.CostEstimate(flops=flops, transcendentals=0, bytes_accessed=1),
-        name="back_near",
-    )(m, in_hbm(d), in_hbm(w_gate), in_hbm(w_up))
+        compiler_params=pltpu.CompilerParams(vmem_limit_bytes=SCOPED),
+        cost_estimate=pl.CostEstimate(flops=1, transcendentals=0, bytes_accessed=1),
+        name="back",
+    )(m, *map(in_hbm, (a, b, c)), g, gs, in_hbm(w_gate), in_hbm(w_up), *([w_down] if first else []))
 
 
 def finish_kernel(
-    count, x_ref, own_ref, one_ref, two_ref, rms_ref, inner_ref, mask_ref, token_ref, gain_ref, *refs
+    x_ref, high_ref, low_ref, one_ref, two_ref, rms_ref, inner_ref, mask_ref, token_ref, gain_ref, out_ref
 ):
-    out_ref = refs[count]
+    half = pl.num_programs(0) // 2
     rms = rms_ref[...]
-    normed = own_ref[...].astype(f32) + one_ref[...].astype(f32) + two_ref[...].astype(f32)
-    grad = rms * gain_ref[...] * normed - x_ref[...].astype(f32) * (rms * rms * inner_ref[...])
+    eye = lax.broadcasted_iota(jnp.int32, (L, L), 0) == lax.broadcasted_iota(jnp.int32, (L, L), 1)
+    inner = jnp.concatenate(
+        [
+            jnp.sum(jnp.where(eye, inner_ref[0, p : p + 1], 0.0), axis=1, keepdims=True)
+            for p in range(out_ref.shape[0] // L)
+        ],
+        axis=0,
+    )
+    own = jnp.where(pl.program_id(0) < half, high_ref[...], low_ref[...]).astype(f32)
+    normed = own + one_ref[...].astype(f32) + two_ref[...].astype(f32)
+    grad = rms * gain_ref[...] * normed - x_ref[...].astype(f32) * (rms * rms * inner)
     mask = mask_ref[...]
     for p in range(out_ref.shape[0] // L):
         part = slice(p * L, (p + 1) * L)
         out_ref[part] = (grad[part] + mask[part] * token_ref[0, p : p + 1]).astype(bf16)
 
 
-def finish(chunk, before, x, own, one, two, rms, inner, mask, token, gain):
-    rows, part = own.shape
+def finish(x, high, low, one, two, rms, inner, mask, token, gain):
+    rows, part = x.shape
     rt = 256
-    steps = rows // rt
-    here = pl.BlockSpec((rt, part), lambda r: (r, 0))
-    whole = pl.BlockSpec((rt, part), lambda r: (chunk * steps + r, 0))
-    column = pl.BlockSpec((rt, 1), lambda r: (chunk * steps + r, 0))
+    half = rows // (2 * rt)
+    whole = pl.BlockSpec((rt, part), lambda r: (r, 0))
+    column = pl.BlockSpec((rt, 1), lambda r: (r, 0))
     return pl.pallas_call(
-        functools.partial(finish_kernel, len(before)),
-        grid=(steps,),
-        in_specs=[whole, here, here, here, column, column, column]
-        + [
-            pl.BlockSpec((1, rt // L, part), lambda r: (chunk * steps + r, 0, 0)),
+        finish_kernel,
+        grid=(rows // rt,),
+        in_specs=[
+            whole,
+            pl.BlockSpec((rt, part), lambda r: (jnp.minimum(r, half - 1), 0)),
+            pl.BlockSpec((rt, part), lambda r: (jnp.maximum(r - half, 0), 0)),
+            whole,
+            whole,
+            column,
+            pl.BlockSpec((1, rt // L, L), lambda r: (r, 0, 0)),
+            column,
+            pl.BlockSpec((1, rt // L, part), lambda r: (r, 0, 0)),
             pl.BlockSpec((1, part), lambda r: (0, 0)),
-        ]
-        + [pl.BlockSpec(memory_space=pl.ANY)] * len(before),
+        ],
         out_specs=whole,
         out_shape=jax.ShapeDtypeStruct(x.shape, bf16),
-        input_output_aliases={9 + k: k for k in range(len(before))},
+        compiler_params=pltpu.CompilerParams(vmem_limit_bytes=16 << 20),
         name="finish",
-    )(x, own, one, two, rms, inner, mask, token.reshape(-1, rt // L, part), gain, *before)
+    )(*map(in_hbm, (x, high, low, one, two)), rms, inner, mask, token.reshape(-1, rt // L, part), gain)
 
 
 def per_device(
@@ -437,11 +422,13 @@
 
     chunks = []
     at = 0
-    for k, rows in enumerate(CHUNKS):
+    for rows in CHUNKS:
         own = hidden_in[at : at + rows]
-        if k == 1:
-            own, sent = lax.optimization_barrier((own, sent))
-        chunks.append((at, rows, own, shifted(own, 1), shifted(own, -1)))
+        if chunks:
+            own, sent, *last = lax.optimization_barrier((own, sent, *chunks[-1][1:]))
+            chunks[-1] = (chunks[-1][0], *last)
+        left, right = shifted(own, 1), shifted(own, -1)
+        chunks.append((at, own, right, left, *(across(left, right) if at == 0 else ())))
         at += rows
     all_q = lax.all_gather(sent, ("x", "z"), axis=0)
 
@@ -460,15 +447,13 @@
 
     done = []
     before = ()
-    for k, (at, rows, own, left, right) in enumerate(chunks):
-        half = rows // 2
-        high, low = shifted(left[:half], 1), shifted(right[half:], -1)
-        part_mask = mask[at : at + rows]
-        done.append(
-            encode(
-                m, k, row_count, before, own, right, left, high, low, part_mask, gain, w_gate, w_up
-            )
-        )
+    for k, (at, *pieces) in enumerate(chunks):
+        if k > 0:
+            pool, right, left = lax.optimization_barrier((done[-1][3], *pieces[1:]))
+            done[-1] = (*done[-1][:3], pool, *done[-1][4:])
+            pieces = (pieces[0], right, left, *across(left, right))
+        part_mask = mask[at : at + CHUNKS[k]]
+        done.append(encode(m, k, row_count, before, *pieces, part_mask, gain, w_gate, w_up))
         before = done[-1][:3]
     a, b, c = before
     pool = jnp.concatenate([d[3] for d in done], axis=1)
@@ -518,34 +503,35 @@
     scale = lax.dynamic_slice_in_dim(vec_scale, core * passes, passes)
     change = scale * grad[:, :width] - own_vec * (scale**3 * grad[:, width : width + 1])
     token_grad = (change / divisor).astype(bf16)
-    dact = contract_rows(token_grad, w_down)
-    dact_high = dact.astype(bf16).astype(f32)
-    dact = jnp.concatenate([dact_high, dact - dact_high], axis=0)
-
-    high, low, s, d = back_far(m, a, b, c, dact, w_gate, w_up)
+
+    tensors = (w_gate, w_up, w_down)
+    none = jnp.zeros((2 * passes, pool.shape[1]), bf16)
+    high, low, g = back(m, (2,), 256, True, a, b, c, token_grad, none, *tensors)
     from_right = shifted(high, -1)
     from_left = shifted(low, 1)
-    right_high, right_low, left_high, left_low = back_near(m, (1, 3), d, w_gate, w_up, 1)
-    left_low = shifted(left_low, -1)
-    right_high = shifted(right_high, 1)
+    right_high, right_low, left_high, left_low = back(
+        m, (1, 3), 512, False, a, b, c, g, none, *tensors
+    )
     right_low = (right_low.astype(f32) + from_left.astype(f32)).astype(bf16)
     left_high = (left_high.astype(f32) + from_right.astype(f32)).astype(bf16)
-    right_low, left_high, d = lax.optimization_barrier((right_low, left_high, d))
-    right_low = shifted(right_low, 1)
-    left_high = shifted(left_high, -1)
-    own_high, own_low = back_near(m, (0,), d, w_gate, w_up, 1 << 38)
+    right = jnp.concatenate([right_high, right_low], axis=0)
+    left = jnp.concatenate([left_high, left_low], axis=0)
+    right, left, g = lax.optimization_barrier((right, left, g))
+    right = shifted(right, 1)
+    left = shifted(left, -1)
+    g_high = g.astype(bf16)
+    gs = jnp.concatenate([g_high, (g - g_high.astype(f32)).astype(bf16)], axis=0)
+    own_high, own_low, s = back(m, (0,), 512, False, a, b, c, g, gs, *tensors)
     small = jnp.concatenate(
         [s.reshape(passes, L), jnp.pad(own_loss[None, :], ((0, 7), (0, L - share)))], axis=0
     )
-    own_high, small = lax.optimization_barrier((own_high, small))
     small = copies_to_all(small, "mp", MP)
-    inner = small[:, :passes].sum(axis=0).reshape(row_count, 1) / width
+    inner = small[:, :passes].sum(axis=0).reshape(passes // 2, 2, L) / width
     query_loss = small[:, passes, :share].reshape(MP * share)
     own_gain = lax.dynamic_slice_in_dim(norm_gain, mi * part, part)[None, :]
     own_token = lax.dynamic_slice_in_dim(token_grad, mi * part, part, axis=1).astype(f32)
     rest = (rms, inner, mask, own_token, own_gain)
-    hidden_grad = finish(1, (), hidden_in, own_low, left_low, right_low, *rest)
-    hidden_grad = finish(0, (hidden_grad,), hidden_in, own_high, left_high, right_high, *rest)
+    hidden_grad = finish(hidden_in, own_high, own_low, right, left, *rest)
     return query_loss, hidden_grad
 
 

time: 208 us -> 199 us (0.957)
  matrix products: 10.4 us -> 5.36 us
  starting transfers between devices: 37.6 us -> 33.9 us
  waiting for transfers between devices: 37.7 us -> 40.7 us
  local copies, waits for them, and re-layouts: 13.9 us -> 11.7 us
    ppermute x14 -> x12, waiting for transfers between devices: 16.5 us -> 8.11 us  [shifted(): return lax.ppermute(x, 'mp', [(i, (i + by) % MP) for i in range(MP)])]
    all_to_all x2, waiting for transfers between devices: 7.88 us -> 15.3 us  [copies_to_all(): lax.all_to_all(jnp.broadcast_to(x, (count, *x.shape)), axes, split_axis=0...]
    dot_general x2 -> x1, matrix products: 7.36 us -> 2.27 us  [contract_rows(): lax.dot_general(left, right, (((1,), (1,)), ((), ())), preferred_element_...]
    ppermute x14 -> x12, starting transfers between devices: 21.6 us -> 18.4 us  [shifted(): return lax.ppermute(x, 'mp', [(i, (i + by) % MP) for i in range(MP)])]
    concatenate x1 -> x3, other arithmetic: 0.02 us -> 3.19 us  [the longest x1 2.14 us: per_device(): left = jnp.concatenate([left_high, left_low], axis=0)]
    unnamed x36 -> x48, local copies, waits for them, and re-layouts: 2.55 us -> 4.36 us
    pallas_call x5 -> x4, Pallas kernels: 37.7 us -> 39.2 us  [the longest x3 34.7 us: back(): pl.pallas_call(functools.partial(back_kernel, steps, first), in_specs=[sm...]
  transfers between devices with their start and end apart: 20 -> 18, of which waited for: 7 -> 7; matrix products, arithmetic and copies ran while one was open for 9% -> 6% of each run, Pallas kernels for 26% -> 27%
where the time goes in v4:
time: 199 us
  Pallas kernels  68.8 us (35%)
  waiting for transfers between devices  40.7 us (20%)
  starting transfers between devices  33.9 us (17%)
  blocking collectives  15.3 us (8%)
  between operations  14.6 us (7%)
  local copies, waits for them, and re-layouts  11.7 us (6%)
  other arithmetic  8.29 us (4%)
  matrix products  5.36 us (3%)
    pallas_call x3, Pallas kernels, back(): pl.pallas_call(functools.partial(back_kernel, steps, first), in_specs=[sm...  34.7 us
    pallas_call x2, Pallas kernels, encode(): pl.pallas_call(functools.partial(encode_kernel, chunk, len(before)), in_s...  29.6 us
    ppermute x12, starting transfers between devices, shifted(): return lax.ppermute(x, 'mp', [(i, (i + by) % MP) for i in range(MP)])  18.4 us
    all_to_all x1, blocking collectives, copies_to_all(): lax.all_to_all(jnp.broadcast_to(x, (count, *x.shape)), axes, split_axis=0...  15.3 us
    all_to_all x2, waiting for transfers between devices, copies_to_all(): lax.all_to_all(jnp.broadcast_to(x, (count, *x.shape)), axes, split_axis=0...  15.3 us
    all_to_all x1, waiting for transfers between devices, per_device(): lax.all_to_all(queries.reshape(MP, share, part), 'mp', split_axis=0, conc...  10.5 us
    all_to_all x2, starting transfers between devices, copies_to_all(): lax.all_to_all(jnp.broadcast_to(x, (count, *x.shape)), axes, split_axis=0...  8.47 us
    ppermute x12, waiting for transfers between devices, shifted(): return lax.ppermute(x, 'mp', [(i, (i + by) % MP) for i in range(MP)])  8.11 us
  transfers between devices with their start and end apart: 18, of which 7 were waited for; matrix products, arithmetic and copies ran while one was open for 6% of the time, Pallas kernels for 27%

profile of v4, /device:TPU:0, one launch (start us, length us, event | category | flops | bytes accessed | tf_op | source)
XLA Modules:
  0.0 198.6 jit_solution(14326928855175375255)
XLA Ops:
  11.8 3.3 %all-to-all-start = ((bf16[4,32,512]{2,1,0:T(8,128)(2,1)}), bf16[4,32,512]{2,1,0:T(8,128)(2,1)S(1)}, u32[]{:S(2)}, u32[]{:S(2)}) async-start(bf16[4,32,512]{2,1,0:T(8,128)(2,1)} %bitcast.77), calls=%async_computation | async-start | bytes 262144 | tf_op jit(solution)/shard_map/all_to_all | solution.py:411
  15.7 10.5 %all-to-all-done = bf16[4,32,512]{2,1,0:T(8,128)(2,1)S(1)} async-done(((bf16[4,32,512]{2,1,0:T(8,128)(2,1)}), bf16[4,32,512]{2,1,0:T(8,128)(2,1)S(1)}, u32[]{:S(2)}, u32[]{:S(2)}) %all-to-all-start) | async-done | bytes 131104 | tf_op jit(solution)/shard_map/all_to_all | solution.py:411
  27.8 2.2 %collective-permute-start.3 = (bf16[256,512]{1,0:T(8,128)(2,1)S(1)}, bf16[256,512]{1,0:T(8,128)(2,1)S(1)}, u32[]{:S(2)}, u32[]{:S(2)}) collective-permute-start(bf16[256,512]{1,0:T(8,128)(2,1)S(1)} %slice.95), channel_id=1, source_target_pairs={{0,3},{1,0},{2,1},{3,2},{4,7},{5,4},{6,5},{7,6},{8,11},{9,8},{10,9... | collective-permute-start | bytes 786440 | tf_op jit(solution)/shard_map/ppermute | solution.py:25
  30.6 4.1 %collective-permute-done.2.high_ref = bf16[256,512]{1,0:T(8,128)(2,1)S(1)} collective-permute-done((bf16[256,512]{1,0:T(8,128)(2,1)S(1)}, bf16[256,512]{1,0:T(8,128)(2,1)S(1)}, u32[]{:S(2)}, u32[]{:S(2)}) %collective-permute-start.2) | collective-permute-done | bytes 262176 | tf_op jit(solution)/shard_map/ppermute | solution.py:25
  35.1 3.1 %collective-permute-start.4 = (bf16[512,512]{1,0:T(8,128)(2,1)S(1)}, bf16[512,512]{1,0:T(8,128)(2,1)S(1)}, u32[]{:S(2)}, u32[]{:S(2)}) collective-permute-start(bf16[512,512]{1,0:T(8,128)(2,1)S(1)} %get-tuple-element.37.own_ref), channel_id=1, source_target_pairs={{0,3},{1,0},{2,1},{3,2},{4,7},{5,4},{6,5},{7,6},{8,11},{9,8},{10,9... | collective-permute-start | bytes 1572872 | tf_op jit(solution)/shard_map/ppermute | solution.py:25
  38.2 14.7 %encode.2 = (bf16[1024,1792]{1,0:T(8,128)(2,1)}, bf16[1024,1792]{1,0:T(8,128)(2,1)}, bf16[1024,1792]{1,0:T(8,128)(2,1)}, f32[7,4,256]{2,1,0:T(4,128)S(1)}, f32[5...) custom-call(s32[1]{0:T(128)} %bitcast.m_ref, bf16[512,512]{1,0:T(8,128)(2,1)} %copy-done.11, bf16[512,512]{1,0:T(8,128)(2,1)} %copy-done.14, ...), custom_call_target="tpu_custom_call" | custom-call | flops 7516192768 | bytes 22282240 | tf_op jit(solution)/shard_map/encode/pallas_call | solution.py:173
  54.7 3.2 %collective-permute-start.7 = (bf16[256,512]{1,0:T(8,128)(2,1)}, bf16[256,512]{1,0:T(8,128)(2,1)}, u32[]{:S(2)}, u32[]{:S(2)}) collective-permute-start(bf16[256,512]{1,0:T(8,128)(2,1)} %slice.78), channel_id=1, source_target_pairs={{0,3},{1,0},{2,1},{3,2},{4,7},{5,4},{6,5},{7,6},{8,11},{9,8},{10,9... | collective-permute-start | bytes 786440 | tf_op jit(solution)/shard_map/ppermute | solution.py:25
  58.1 3.7 %collective-permute-done.6.high_ref = bf16[256,512]{1,0:T(8,128)(2,1)} collective-permute-done((bf16[256,512]{1,0:T(8,128)(2,1)}, bf16[256,512]{1,0:T(8,128)(2,1)}, u32[]{:S(2)}, u32[]{:S(2)}) %collective-permute-start.6) | collective-permute-done | bytes 262176 | tf_op jit(solution)/shard_map/ppermute | solution.py:25
  62.1 14.9 %encode.3 = (bf16[1024,1792]{1,0:T(8,128)(2,1)}, bf16[1024,1792]{1,0:T(8,128)(2,1)}, bf16[1024,1792]{1,0:T(8,128)(2,1)}, f32[7,4,256]{2,1,0:T(4,128)S(1)}, f32[5...) custom-call(s32[1]{0:T(128)} %bitcast.m_ref, ...), custom_call_target="tpu_custom_call", output_to_operand_aliasing={{0}: (10, {}), {1}: (11, {}), {2}: (12, {})} | custom-call | flops 7516192768 | bytes 22282240 | tf_op jit(solution)/shard_map/encode/pallas_call | solution.py:173
  79.0 5.2 %all-to-all-start.1 = ((bf16[8,8,2048]{2,1,0:T(8,128)(2,1)}), bf16[8,8,2048]{2,1,0:T(8,128)(2,1)S(1)}, u32[]{:S(2)}, u32[]{:S(2)}) async-start(bf16[8,8,2048]{2,1,0:T(8,128)(2,1)} %broadcast_in_dim.21), calls=%async_computation.1 | async-start | bytes 524288 | tf_op jit(solution)/shard_map/all_to_all | solution.py:38
  84.3 6.8 %all-to-all-done.1 = bf16[8,8,2048]{2,1,0:T(8,128)(2,1)S(1)} async-done(((bf16[8,8,2048]{2,1,0:T(8,128)(2,1)}), bf16[8,8,2048]{2,1,0:T(8,128)(2,1)S(1)}, u32[]{:S(2)}, u32[]{:S(2)}) %all-to-all-start.1) | async-done | bytes 262176 | tf_op jit(solution)/shard_map/all_to_all | solution.py:38
  92.7 2.3 %fusion.19 = (f32[512]{0:T(512)S(1)}, f32[512]{0:T(512)S(1)}, f32[16,512]{1,0:T(8,128)S(1)}) fusion(f32[16]{0:T(128)S(1)} %rsqrt.32, f32[512]{0:T(512)S(1)} %get-tuple-element.73, f32[16]{0:T(128)S(1)} %fusion.25, f32[16]{0:T(128)S(1)} %fusion.29, f32[512]{0:T(512)S(1)} %get-tuple-element.74, bf16[512,2176]{1,0:T(8,128)(2,1)} %all-gather.3.cloned.1.call-done, ...), kind=kOutput, calls=%fused_computation.46 | convolution fusion | flops 33610752 | bytes 2203840 | tf_op jit(solution)/shard_map/dot_general | solution.py:48
  95.0 15.3 %all_to_all.25 = f32[16,8,128]{2,1,0:T(8,128)S(1)} all-to-all(f32[16,8,128]{2,1,0:T(8,128)S(1)} %broadcast_in_dim.44), channel_id=1, replica_groups=mesh['x'=4,'z'=4,'core'=2,'mp'=4] {'x','z'}, dimensions={0} | all-to-all | bytes 131072 | tf_op jit(solution)/shard_map/all_to_all | solution.py:38
  113.5 3.6 %all-to-all-start.3 = ((bf16[8,8,2176]{2,1,0:T(8,128)(2,1)}), bf16[8,8,2176]{2,1,0:T(8,128)(2,1)S(1)}, u32[]{:S(2)}, u32[]{:S(2)}) async-start(bf16[8,8,2176]{2,1,0:T(8,128)(2,1)} %bitcast.19), calls=%async_computation.3 | async-start | bytes 557056 | tf_op jit(solution)/shard_map/all_to_all | solution.py:500
  117.2 6.8 %all-to-all-done.3 = bf16[8,8,2176]{2,1,0:T(8,128)(2,1)S(1)} async-done(((bf16[8,8,2176]{2,1,0:T(8,128)(2,1)}), bf16[8,8,2176]{2,1,0:T(8,128)(2,1)S(1)}, u32[]{:S(2)}, u32[]{:S(2)}) %all-to-all-start.3) | async-done | bytes 278560 | tf_op jit(solution)/shard_map/all_to_all | solution.py:500
  124.3 3.1 %copy-done = bf16[1792,2048]{1,0:T(8,128)(2,1)S(1)} copy-done((bf16[1792,2048]{1,0:T(8,128)(2,1)S(1)}, bf16[1792,2048]{1,0:T(8,128)(2,1)}, u32[]{:S(2)}) %copy-start) | copy-done | bytes 7340056
  127.4 10.3 %back.3 = (bf16[512,512]{1,0:T(8,128)(2,1)}, bf16[512,512]{1,0:T(8,128)(2,1)}, f32[8,1792]{1,0:T(8,128)S(1)}) custom-call(s32[1]{0:T(128)} %bitcast.m_ref, bf16[1024,1792]{1,0:T(8,128)(2,1)} %get-tuple-element.49.a_ref, bf16[1024,1792]{1,0:T(8,128)(2,1)} %get-tuple-element.50.b_ref, bf16[1024,1792]{1,0:T(8,128)(2,1)} %get-tuple-element.51.c_ref, ...), custom_call_target="tpu_custom_call" | custom-call | flops 1 | bytes 1 | tf_op jit(solution)/shard_map/back/pallas_call | solution.py:327
  140.6 13.5 %back.4 = (bf16[512,512]{1,0:T(8,128)(2,1)}, bf16[512,512]{1,0:T(8,128)(2,1)}, bf16[512,512]{1,0:T(8,128)(2,1)}, bf16[512,512]{1,0:T(8,128)(2,1)}) custom-call(s32[1]{0:T(128)} %bitcast.m_ref, bf16[1024,1792]{1,0:T(8,128)(2,1)} %get-tuple-element.49.a_ref, bf16[1024,1792]{1,0:T(8,128)(2,1)} %get-tuple-element.50.b_ref, ...), custom_call_target="tpu_custom_call" | custom-call | flops 1 | bytes 1 | tf_op jit(solution)/shard_map/back/pallas_call | solution.py:327
  155.4 2.1 %pad_maximum_fusion.1 = bf16[1024,512]{1,0:T(8,128)(2,1)} fusion(bf16[512,512]{1,0:T(8,128)(2,1)} %get-tuple-element.63, bf16[512,512]{1,0:T(8,128)(2,1)S(1)} %add_convert_fusion), kind=kLoop, calls=%fused_computation.6 | loop fusion | flops 2097152 | bytes 2097152 | tf_op jit(solution)/shard_map/concatenate | solution.py:518
  159.6 2.4 %collective-permute-start.12 = (bf16[1024,512]{1,0:T(8,128)(2,1)}, bf16[1024,512]{1,0:T(8,128)(2,1)}, u32[]{:S(2)}, u32[]{:S(2)}) collective-permute-start(bf16[1024,512]{1,0:T(8,128)(2,1)} %pad_maximum_fusion.1), channel_id=1, source_target_pairs={{0,3},{1,0},{2,1},{3,2},{4,7},{5,4},{6,5},{7,6},{8,11},{9,8},{10,9... | collective-permute-start | bytes 3145736 | tf_op jit(solution)/shard_map/ppermute | solution.py:25
  162.1 10.9 %back.5 = (bf16[512,512]{1,0:T(8,128)(2,1)}, bf16[512,512]{1,0:T(8,128)(2,1)}, f32[1024,1]{1,0:T(8,128)S(1)}) custom-call(s32[1]{0:T(128)} %bitcast.m_ref, bf16[1024,1792]{1,0:T(8,128)(2,1)} %get-tuple-element.49.a_ref, bf16[1024,1792]{1,0:T(8,128)(2,1)} %get-tuple-element.50.b_ref, bf16[1024,1792]{1,0:T(8,128)(2,1)} %get-tuple-element.51.c_ref, ...), custom_call_target="tpu_custom_call" | custom-call | flops 1 | bytes 1 | tf_op jit(solution)/shard_map/back/pallas_call | solution.py:327
  173.9 3.3 %all-to-all-start.4 = ((f32[4,16,128]{2,1,0:T(8,128)}), f32[4,16,128]{2,1,0:T(8,128)S(1)}, u32[]{:S(2)}, u32[]{:S(2)}) async-start(f32[4,16,128]{2,1,0:T(8,128)} %broadcast_in_dim.50), calls=%async_computation.4 | async-start | bytes 65536 | tf_op jit(solution)/shard_map/all_to_all | solution.py:38
  177.2 8.5 %all-to-all-done.4 = f32[4,16,128]{2,1,0:T(8,128)S(1)} async-done(((f32[4,16,128]{2,1,0:T(8,128)}), f32[4,16,128]{2,1,0:T(8,128)S(1)}, u32[]{:S(2)}, u32[]{:S(2)}) %all-to-all-start.4) | async-done | bytes 32800 | tf_op jit(solution)/shard_map/all_to_all | solution.py:38
  187.3 4.5 %finish.1 = bf16[1024,512]{1,0:T(8,128)(2,1)} custom-call(bf16[1024,512]{1,0:T(8,128)(2,1)} %x_ref.1, bf16[512,512]{1,0:T(8,128)(2,1)} %get-tuple-element.66.high_ref, bf16[512,512]{1,0:T(8,128)(2,1)} %get-tuple-element.67.low_ref, bf16[1024,512]{1,0:T(8,128)(2,1)} %copy-done.9, bf16[1024,512]{1,0:T(8,128)(2,1)} %collective-permute-done.12.two_ref, ...), custom_call_target="tpu_custom_call" | custom-call | tf_op jit(solution)/shard_map/finish/pallas_call | solution.py:373
  (147 shorter events, 25.7 us)
Async XLA Ops:
  7.2 31.0 %copy-start.5 = (f32[2048]{0:T(1024)S(1)}, f32[2048]{0:T(1024)}, u32[]{:S(2)}) copy-start(f32[2048]{0:T(1024)} %param.14) | copy-start | bytes 24580
  8.5 29.7 %copy-start.11 = (bf16[512,512]{1,0:T(8,128)(2,1)}, bf16[512,512]{1,0:T(8,128)(2,1)S(1)}, u32[]{:S(2)}) copy-start(bf16[512,512]{1,0:T(8,128)(2,1)S(1)} %get-tuple-element.38.own_ref) | copy-start | bytes 1572868
  8.5 44.4 %copy-start.6 = (bf16[512,512]{1,0:T(8,128)(2,1)}, bf16[512,512]{1,0:T(8,128)(2,1)S(1)}, u32[]{:S(2)}) copy-start(bf16[512,512]{1,0:T(8,128)(2,1)S(1)} %get-tuple-element.37.own_ref) | copy-start | bytes 1572868
  8.5 18.0 %collective-permute-start.1 = (bf16[512,512]{1,0:T(8,128)(2,1)S(1)}, bf16[512,512]{1,0:T(8,128)(2,1)S(1)}, u32[]{:S(2)}, u32[]{:S(2)}) collective-permute-start(bf16[512,512]{1,0:T(8,128)(2,1)S(1)} %get-tuple-element.38.own_ref), channel_id=1, source_target_pairs={{0,1},{1,2},{2,3},{3,0},{4,5},{5,6},{6,7},{7,4},{8,9},{9,10},{10,1... | collective-permute-start | bytes 1572872 | tf_op jit(solution)/shard_map/ppermute | solution.py:25
  10.2 17.5 %collective-permute-start = (bf16[512,512]{1,0:T(8,128)(2,1)S(1)}, bf16[512,512]{1,0:T(8,128)(2,1)S(1)}, u32[]{:S(2)}, u32[]{:S(2)}) collective-permute-start(bf16[512,512]{1,0:T(8,128)(2,1)S(1)} %get-tuple-element.38.own_ref), channel_id=1, source_target_pairs={{0,3},{1,0},{2,1},{3,2},{4,7},{5,4},{6,5},{7,6},{8,11},{9,8},{10,9... | collective-permute-start | bytes 1572872 | tf_op jit(solution)/shard_map/ppermute | solution.py:25
  11.8 14.4 %all-to-all-start = ((bf16[4,32,512]{2,1,0:T(8,128)(2,1)}), bf16[4,32,512]{2,1,0:T(8,128)(2,1)S(1)}, u32[]{:S(2)}, u32[]{:S(2)}) async-start(bf16[4,32,512]{2,1,0:T(8,128)(2,1)} %bitcast.77), calls=%async_computation | async-start | bytes 262144 | tf_op jit(solution)/shard_map/all_to_all | solution.py:411
  15.2 76.2 %all-gather.3.cloned.1.call-start = ((), (), s32[]{:S(2)}) async-start(), calls=%async_computation.5 | async-start | bytes 2367488 | tf_op jit(solution)/shard_map/all_gather | solution.py:433
  15.4 68.8 %collective-permute-start.8 = (s32[8]{0:T(128)S(1)}, s32[8]{0:T(128)S(1)}, u32[]{:S(2)}, u32[]{:S(2)}) collective-permute-start(s32[8]{0:T(128)S(1)} %get-tuple-element.83), channel_id=1, source_target_pairs={{0,4},{4,0},{1,5},{5,1},{2,6},{6,2},{3,7},{7,3},{8,12},{12,8},{9,1... | collective-permute-start | bytes 104 | tf_op jit(solution)/shard_map/ppermute | solution.py:34
  26.5 8.2 %collective-permute-start.2 = (bf16[256,512]{1,0:T(8,128)(2,1)S(1)}, bf16[256,512]{1,0:T(8,128)(2,1)S(1)}, u32[]{:S(2)}, u32[]{:S(2)}) collective-permute-start(bf16[256,512]{1,0:T(8,128)(2,1)S(1)} %slice.94), channel_id=1, source_target_pairs={{0,1},{1,2},{2,3},{3,0},{4,5},{5,6},{6,7},{7,4},{8,9},{9,10},{10,1... | collective-permute-start | bytes 786440 | tf_op jit(solution)/shard_map/ppermute | solution.py:25
  27.8 6.9 %collective-permute-start.3 = (bf16[256,512]{1,0:T(8,128)(2,1)S(1)}, bf16[256,512]{1,0:T(8,128)(2,1)S(1)}, u32[]{:S(2)}, u32[]{:S(2)}) collective-permute-start(bf16[256,512]{1,0:T(8,128)(2,1)S(1)} %slice.95), channel_id=1, source_target_pairs={{0,3},{1,0},{2,1},{3,2},{4,7},{5,4},{6,5},{7,6},{8,11},{9,8},{10,9... | collective-permute-start | bytes 786440 | tf_op jit(solution)/shard_map/ppermute | solution.py:25
  35.1 17.9 %collective-permute-start.4 = (bf16[512,512]{1,0:T(8,128)(2,1)S(1)}, bf16[512,512]{1,0:T(8,128)(2,1)S(1)}, u32[]{:S(2)}, u32[]{:S(2)}) collective-permute-start(bf16[512,512]{1,0:T(8,128)(2,1)S(1)} %get-tuple-element.37.own_ref), channel_id=1, source_target_pairs={{0,3},{1,0},{2,1},{3,2},{4,7},{5,4},{6,5},{7,6},{8,11},{9,8},{10,9... | collective-permute-start | bytes 1572872 | tf_op jit(solution)/shard_map/ppermute | solution.py:25
  38.2 14.8 %collective-permute-start.5 = (bf16[512,512]{1,0:T(8,128)(2,1)S(1)}, bf16[512,512]{1,0:T(8,128)(2,1)S(1)}, u32[]{:S(2)}, u32[]{:S(2)}) collective-permute-start(bf16[512,512]{1,0:T(8,128)(2,1)S(1)} %get-tuple-element.37.own_ref), channel_id=1, source_target_pairs={{0,1},{1,2},{2,3},{3,0},{4,5},{5,6},{6,7},{7,4},{8,9},{9,10},{10,1... | collective-permute-start | bytes 1572872 | tf_op jit(solution)/shard_map/ppermute | solution.py:25
  53.9 7.9 %collective-permute-start.6 = (bf16[256,512]{1,0:T(8,128)(2,1)}, bf16[256,512]{1,0:T(8,128)(2,1)}, u32[]{:S(2)}, u32[]{:S(2)}) collective-permute-start(bf16[256,512]{1,0:T(8,128)(2,1)} %slice.77), channel_id=1, source_target_pairs={{0,1},{1,2},{2,3},{3,0},{4,5},{5,6},{6,7},{7,4},{8,9},{9,10},{10,1... | collective-permute-start | bytes 786440 | tf_op jit(solution)/shard_map/ppermute | solution.py:25
  53.9 23.1 %slice-start = ((s8[7340032]{0:T(1024)(128)(4,1)}), s8[3145728]{0:T(1024)(128)(4,1)S(1)}, s32[]{:S(2)}) async-start(s8[7340032]{0:T(1024)(128)(4,1)} %bitcast.65), calls=%async_computation.6 | async-start | bytes 6291456
  54.7 7.4 %collective-permute-start.7 = (bf16[256,512]{1,0:T(8,128)(2,1)}, bf16[256,512]{1,0:T(8,128)(2,1)}, u32[]{:S(2)}, u32[]{:S(2)}) collective-permute-start(bf16[256,512]{1,0:T(8,128)(2,1)} %slice.78), channel_id=1, source_target_pairs={{0,3},{1,0},{2,1},{3,2},{4,7},{5,4},{6,5},{7,6},{8,11},{9,8},{10,9... | collective-permute-start | bytes 786440 | tf_op jit(solution)/shard_map/ppermute | solution.py:25
  62.1 15.0 %slice-start.1 = ((s8[7340032]{0:T(1024)(128)(4,1)}), s8[4194304]{0:T(1024)(128)(4,1)S(1)}, s32[]{:S(2)}) async-start(s8[7340032]{0:T(1024)(128)(4,1)} %bitcast.65), calls=%async_computation.7 | async-start | bytes 8388608
  79.0 12.1 %all-to-all-start.1 = ((bf16[8,8,2048]{2,1,0:T(8,128)(2,1)}), bf16[8,8,2048]{2,1,0:T(8,128)(2,1)S(1)}, u32[]{:S(2)}, u32[]{:S(2)}) async-start(bf16[8,8,2048]{2,1,0:T(8,128)(2,1)} %broadcast_in_dim.21), calls=%async_computation.1 | async-start | bytes 524288 | tf_op jit(solution)/shard_map/all_to_all | solution.py:38
  113.5 10.4 %all-to-all-start.3 = ((bf16[8,8,2176]{2,1,0:T(8,128)(2,1)}), bf16[8,8,2176]{2,1,0:T(8,128)(2,1)S(1)}, u32[]{:S(2)}, u32[]{:S(2)}) async-start(bf16[8,8,2176]{2,1,0:T(8,128)(2,1)} %bitcast.19), calls=%async_computation.3 | async-start | bytes 557056 | tf_op jit(solution)/shard_map/all_to_all | solution.py:500
  127.4 12.6 %copy-start.4 = (f32[512,1]{1,0:T(8,128)S(1)}, f32[512,1]{1,0:T(8,128)}, u32[]{:S(2)}) copy-start(f32[512,1]{1,0:T(8,128)} %copy-done.3) | copy-start | bytes 6148
  137.7 16.5 %collective-permute-start.10 = (bf16[512,512]{1,0:T(8,128)(2,1)}, bf16[512,512]{1,0:T(8,128)(2,1)S(1)}, u32[]{:S(2)}, u32[]{:S(2)}) collective-permute-start(bf16[512,512]{1,0:T(8,128)(2,1)} %get-tuple-element.62), channel_id=1, source_target_pairs={{0,3},{1,0},{2,1},{3,2},{4,7},{5,4},{6,5},{7,6},{8,11},{9,8},{10,9... | collective-permute-start | bytes 1572872 | tf_op jit(solution)/shard_map/ppermute | solution.py:25
  140.3 17.3 %collective-permute-start.9 = (bf16[512,512]{1,0:T(8,128)(2,1)}, bf16[512,512]{1,0:T(8,128)(2,1)S(1)}, u32[]{:S(2)}, u32[]{:S(2)}) collective-permute-start(bf16[512,512]{1,0:T(8,128)(2,1)} %get-tuple-element.60), channel_id=1, source_target_pairs={{0,1},{1,2},{2,3},{3,0},{4,5},{5,6},{6,7},{7,4},{8,9},{9,10},{10,1... | collective-permute-start | bytes 1572872 | tf_op jit(solution)/shard_map/ppermute | solution.py:25
  158.8 27.6 %collective-permute-start.11 = (bf16[1024,512]{1,0:T(8,128)(2,1)}, bf16[1024,512]{1,0:T(8,128)(2,1)S(1)}, u32[]{:S(2)}, u32[]{:S(2)}) collective-permute-start(bf16[1024,512]{1,0:T(8,128)(2,1)} %pad_maximum_fusion), channel_id=1, source_target_pairs={{0,1},{1,2},{2,3},{3,0},{4,5},{5,6},{6,7},{7,4},{8,9},{9,10},{10,1... | collective-permute-start | bytes 3145736 | tf_op jit(solution)/shard_map/ppermute | solution.py:25
  159.6 26.8 %collective-permute-start.12 = (bf16[1024,512]{1,0:T(8,128)(2,1)}, bf16[1024,512]{1,0:T(8,128)(2,1)}, u32[]{:S(2)}, u32[]{:S(2)}) collective-permute-start(bf16[1024,512]{1,0:T(8,128)(2,1)} %pad_maximum_fusion.1), channel_id=1, source_target_pairs={{0,3},{1,0},{2,1},{3,2},{4,7},{5,4},{6,5},{7,6},{8,11},{9,8},{10,9... | collective-permute-start | bytes 3145736 | tf_op jit(solution)/shard_map/ppermute | solution.py:25
  173.9 11.8 %all-to-all-start.4 = ((f32[4,16,128]{2,1,0:T(8,128)}), f32[4,16,128]{2,1,0:T(8,128)S(1)}, u32[]{:S(2)}, u32[]{:S(2)}) async-start(f32[4,16,128]{2,1,0:T(8,128)} %broadcast_in_dim.50), calls=%async_computation.4 | async-start | bytes 65536 | tf_op jit(solution)/shard_map/all_to_all | solution.py:38
  (16 other events, 88.2 us)
Sparse Core Ops, SparseCore 0:
  34.8 47.9 all-gather.2

commit v5 on v4

--- a/solution.py
+++ b/solution.py
@@ -16,7 +16,6 @@
 MP = 4
 FT = 256
 SCOPED = 40 << 20
-CHUNKS = (512, 512)
 bf16 = jnp.bfloat16
 f32 = jnp.float32
 
@@ -63,82 +62,163 @@
 smem = pl.BlockSpec(memory_space=pltpu.SMEM)
 
 
-def encode_kernel(
-    chunk, count, m_ref, own_ref, right_ref, left_ref, high_ref, low_ref, mask_ref, gain_ref, wg_ref, wu_ref, *refs
+def loop_copies(copies, count):
+    def start(n):
+        for copy in copies(n):
+            copy.start()
+
+    each(count, start)
+
+
+def weight_tiles(m, steps, part, wg_ref, wu_ref, w, sem):
+    def copies(n):
+        columns = pl.ds(pl.multiple_of(n * FT, FT), FT)
+        return [
+            pltpu.make_async_copy(
+                ref.at[pl.ds(pl.multiple_of(lax.rem(m + step, MP) * part, part), part), columns],
+                w.at[n, pl.ds(k * part, part), pl.ds(i * FT, FT)],
+                sem.at[n, 2 * k + i],
+            )
+            for k, step in enumerate(steps)
+            for i, ref in enumerate((wg_ref, wu_ref))
+        ]
+
+    return copies
+
+
+NEAR = (0, 1, 3)
+
+
+def encode_near_kernel(
+    m_ref, own_ref, right_ref, left_ref, mask_ref, gain_ref, wg_ref, wu_ref,
+    acc_out, square_ref, xpool_ref, xin, xs, w, acc, in_sem, w_sem, out_sem,
 ):
-    a_out, b_out, c_out, pool_ref, rms_ref, xpool_ref = refs[count : count + 6]
-    xin, xs, w, results, in_sem, w_sem, out_sem = refs[count + 6 :]
     rows, part = own_ref.shape
+    tiles = w.shape[0]
+    m = m_ref[0]
+    arriving = [
+        pltpu.make_async_copy(ref, xin.at[k], in_sem.at[k])
+        for k, ref in enumerate((own_ref, right_ref, left_ref))
+    ]
+    for copy in arriving:
+        copy.start()
+    weights = weight_tiles(m, NEAR, part, wg_ref, wu_ref, w, w_sem)
+    loop_copies(weights, tiles)
+    for copy in arriving:
+        copy.wait()
+
+    def scale(p):
+        at = pl.ds(pl.multiple_of(p * L, L), L)
+        total = None
+        for k, step in enumerate(NEAR):
+            v = xin[k, at].astype(f32)
+            square = jnp.sum(v * v, axis=1, keepdims=True)
+            total = square if total is None else total + square
+            xs[at, k * part : (k + 1) * part] = (v * gain_ref[lax.rem(m + step, MP)]).astype(bf16)
+            if k == 0:
+                xpool_ref[pl.ds(p, 1)] = jnp.sum(v * mask_ref[at], axis=0, keepdims=True)
+        square_ref[at] = total
+
+    each(rows // L, scale)
+
+    def leaving(n):
+        return pltpu.make_async_copy(acc.at[lax.rem(n, 2)], acc_out.at[n], out_sem.at[n])
+
+    def multiply(n):
+        for copy in weights(n):
+            copy.wait()
+
+        @pl.when(n >= 2)
+        def _():
+            leaving(n - 2).wait()
+
+        acc[lax.rem(n, 2)] = jnp.dot(xs[...], w[n], preferred_element_type=f32)
+        leaving(n).start()
+
+    each(tiles, multiply)
+    leaving(tiles - 2).wait()
+    leaving(tiles - 1).wait()
+
+
+def encode_near(m, own, right, left, mask, gain, w_gate, w_up):
+    rows, part = own.shape
+    width, ff = w_gate.shape
+    tiles = ff // FT
+    return pl.pallas_call(
+        encode_near_kernel,
+        in_specs=[smem] + [anywhere] * 3 + [vmem, vmem, anywhere, anywhere],
+        out_specs=[anywhere, vmem, vmem],
+        out_shape=[
+            pltpu.HBM((tiles, rows, 2 * FT), f32),
+            jax.ShapeDtypeStruct((rows, 1), f32),
+            jax.ShapeDtypeStruct((rows // L, part), f32),
+        ],
+        scratch_shapes=[
+            pltpu.VMEM((len(NEAR), rows, part), bf16),
+            pltpu.VMEM((rows, len(NEAR) * part), bf16),
+            pltpu.VMEM((tiles, len(NEAR) * part, 2 * FT), bf16),
+            pltpu.VMEM((2, rows, 2 * FT), f32),
+            pltpu.SemaphoreType.DMA((len(NEAR),)),
+            pltpu.SemaphoreType.DMA((tiles, 2 * len(NEAR))),
+            pltpu.SemaphoreType.DMA((tiles,)),
+        ],
+        compiler_params=pltpu.CompilerParams(vmem_limit_bytes=SCOPED),
+        cost_estimate=pl.CostEstimate(
+            flops=3 * rows * width * ff, transcendentals=0, bytes_accessed=4 * rows * width
+        ),
+        name="encode_near",
+    )(m, *map(in_hbm, (own, right, left)), mask, gain, in_hbm(w_gate), in_hbm(w_up))
+
+
+def encode_far_kernel(
+    m_ref, high_ref, low_ref, acc_ref, square_ref, mask_ref, gain_ref, wg_ref, wu_ref,
+    a_out, b_out, c_out, pool_ref, rms_ref, xin, xs, w, acc, results, in_sem, w_sem, acc_sem, out_sem,
+):
+    rows, part = xin.shape
     half = rows // 2
     tiles = w.shape[0]
     m = m_ref[0]
-    sources = [
-        (own_ref, xin.at[0]),
-        (right_ref, xin.at[1]),
-        (left_ref, xin.at[3]),
-        (high_ref, xin.at[2, pl.ds(0, half)]),
-        (low_ref, xin.at[2, pl.ds(half, half)]),
+    arriving = [
+        pltpu.make_async_copy(ref, xin.at[pl.ds(k * half, half)], in_sem.at[k])
+        for k, ref in enumerate((high_ref, low_ref))
     ]
-    arriving = [pltpu.make_async_copy(a, b, in_sem.at[k]) for k, (a, b) in enumerate(sources)]
     for copy in arriving:
         copy.start()
-    def weight_copies(n):
-        columns = pl.ds(pl.multiple_of(n * FT, FT), FT)
-        copies = []
-        for k in range(MP):
-            at = pl.multiple_of(lax.rem(m + k, MP) * part, part)
-            for i, ref in enumerate((wg_ref, wu_ref)):
-                copies.append(
-                    pltpu.make_async_copy(
-                        ref.at[pl.ds(at, part), columns],
-                        w.at[n, pl.ds(k * part, part), pl.ds(i * FT, FT)],
-                        w_sem.at[n, 2 * k + i],
-                    )
-                )
-        return copies
-
-    def result_copies(n):
+    weights = weight_tiles(m, (2,), part, wg_ref, wu_ref, w, w_sem)
+
+    def inputs(n):
+        return [*weights(n), pltpu.make_async_copy(acc_ref.at[n], acc.at[n], acc_sem.at[n])]
+
+    loop_copies(inputs, tiles)
+    for copy in arriving:
+        copy.wait()
+
+    def scale(p):
+        at = pl.ds(pl.multiple_of(p * L, L), L)
+        v = xin[at].astype(f32)
+        total = square_ref[at] + jnp.sum(v * v, axis=1, keepdims=True)
+        rms_ref[at] = lax.rsqrt(total / (MP * part) + norm_epsilon)
+        xs[at] = (v * gain_ref[lax.rem(m + 2, MP)]).astype(bf16)
+
+    each(rows // L, scale)
+
+    def leaving(n):
         return [
             pltpu.make_async_copy(
                 results.at[n, i],
-                out.at[pl.ds(chunk * rows, rows), pl.ds(pl.multiple_of(n * FT, FT), FT)],
+                out.at[:, pl.ds(pl.multiple_of(n * FT, FT), FT)],
                 out_sem.at[n, i],
             )
             for i, out in enumerate((a_out, b_out, c_out))
         ]
 
-    def start_weights(n):
-        for copy in weight_copies(n):
-            copy.start()
-
-    each(tiles, start_weights)
-    for copy in arriving:
-        copy.wait()
-
-    def normalise(p):
-        at = pl.ds(pl.multiple_of(p * L, L), L)
-        mask = mask_ref[at]
-        total = None
-        for k in range(MP):
-            v = xin[k, at].astype(f32)
-            square = jnp.sum(v * v, axis=1, keepdims=True)
-            total = square if total is None else total + square
-        rms = lax.rsqrt(total / (MP * part) + norm_epsilon)
-        rms_ref[at] = rms
-        for k in range(MP):
-            j = lax.rem(m + k, MP)
-            v = xin[k, at].astype(f32)
-            xs[at, k * part : (k + 1) * part] = (v * rms * gain_ref[j]).astype(bf16)
-            xpool_ref[p, pl.ds(j, 1)] = jnp.sum(v * mask, axis=0, keepdims=True)
-
-    each(rows // L, normalise)
-
     def multiply(n):
-        for copy in weight_copies(n):
+        for copy in inputs(n):
             copy.wait()
-        for r in range(0, rows, rows):
-            at = slice(r, r + rows)
-            both = jnp.dot(xs[at], w[n], preferred_element_type=f32)
+        for r in range(2):
+            at = slice(r * half, (r + 1) * half)
+            both = acc[n, at] + jnp.dot(xs[at], w[n], preferred_element_type=f32)
+            both *= rms_ref[at]
             gate, up = both[:, :FT], both[:, FT:]
             mask = mask_ref[at]
             sig = jax.nn.sigmoid(gate)
@@ -146,64 +226,56 @@
             b = gate * sig
             bu = b * up
             act = bu.astype(bf16).astype(f32)
-            for p in range(rows // L):
-                q = r // L + p
+            for p in range(half // L):
+                q = r * (half // L) + p
                 pool_ref[n, q : q + 1] = jnp.sum(act[p * L : (p + 1) * L], axis=0, keepdims=True)
             a = up * (sig + b * (1.0 - sig))
             results[n, 0, at] = a.astype(bf16)
             results[n, 1, at] = (b * mask).astype(bf16)
             results[n, 2, at] = (a * gate + bu).astype(bf16)
-        for copy in result_copies(n):
+        for copy in leaving(n):
             copy.start()
 
     each(tiles, multiply)
 
-    def wait_results(n):
-        for copy in result_copies(n):
+    def wait(n):
+        for copy in leaving(n):
             copy.wait()
 
-    each(tiles, wait_results)
-
-
-def encode(m, chunk, total, before, own, right, left, high, low, mask, gain, w_gate, w_up):
-    rows, part = own.shape
+    each(tiles, wait)
+
+
+def encode_far(m, high, low, acc, square, mask, gain, w_gate, w_up):
+    half, part = high.shape
+    rows = 2 * half
     width, ff = w_gate.shape
-    passes = rows // L
     tiles = ff // FT
     return pl.pallas_call(
-        functools.partial(encode_kernel, chunk, len(before)),
-        in_specs=[smem]
-        + [anywhere] * 5
-        + [vmem, vmem, anywhere, anywhere]
-        + [anywhere] * len(before),
-        out_specs=[anywhere] * 3 + [vmem] * 3,
-        out_shape=[pltpu.HBM((total, ff), bf16)] * 3
+        encode_far_kernel,
+        in_specs=[smem] + [anywhere] * 3 + [vmem] * 3 + [anywhere] * 2,
+        out_specs=[anywhere] * 3 + [vmem] * 2,
+        out_shape=[pltpu.HBM((rows, ff), bf16)] * 3
         + [
-            jax.ShapeDtypeStruct((tiles, passes, FT), f32),
+            jax.ShapeDtypeStruct((tiles, rows // L, FT), f32),
             jax.ShapeDtypeStruct((rows, 1), f32),
-            jax.ShapeDtypeStruct((passes, MP, part), f32),
         ],
         scratch_shapes=[
-            pltpu.VMEM((MP, rows, part), bf16),
-            pltpu.VMEM((rows, width), bf16),
-            pltpu.VMEM((tiles, width, 2 * FT), bf16),
+            pltpu.VMEM((rows, part), bf16),
+            pltpu.VMEM((rows, part), bf16),
+            pltpu.VMEM((tiles, part, 2 * FT), bf16),
+            pltpu.VMEM((tiles, rows, 2 * FT), f32),
             pltpu.VMEM((tiles, 3, rows, FT), bf16),
-            pltpu.SemaphoreType.DMA((5,)),
-            pltpu.SemaphoreType.DMA((tiles, 2 * MP)),
+            pltpu.SemaphoreType.DMA((2,)),
+            pltpu.SemaphoreType.DMA((tiles, 2)),
+            pltpu.SemaphoreType.DMA((tiles,)),
             pltpu.SemaphoreType.DMA((tiles, 3)),
         ],
-        compiler_params=pltpu.CompilerParams(vmem_limit_bytes=44 << 20),
+        compiler_params=pltpu.CompilerParams(vmem_limit_bytes=SCOPED),
         cost_estimate=pl.CostEstimate(
-            flops=4 * rows * width * ff,
-            transcendentals=rows * ff,
-            bytes_accessed=4 * width * ff + 2 * rows * width + 6 * rows * ff,
+            flops=rows * width * ff, transcendentals=rows * ff, bytes_accessed=6 * rows * ff
         ),
-        input_output_aliases={10 + k: k for k in range(len(before))},
-        name="encode",
-    )(
-        m, *map(in_hbm, (own, right, left, high, low)), mask, gain,
-        in_hbm(w_gate), in_hbm(w_up), *map(in_hbm, before),
-    )
+        name="encode_far",
+    )(m, *map(in_hbm, (high, low, acc)), square, mask, gain, in_hbm(w_gate), in_hbm(w_up))
 
 
 def load_weights(m, steps, wg_ref, wu_ref, w, sem):
@@ -223,7 +295,7 @@
 def back_kernel(steps, first, m_ref, a_ref, b_ref, c_ref, g_in, gs_ref, wg_ref, wu_ref, *refs):
     if first:
         wd_ref, *refs = refs
-    count = 2 * len(steps)
+    count = 2 if first else len(steps)
     outs = refs[:count]
     last = not first and len(steps) == 1
     if first:
@@ -235,7 +307,7 @@
     part = outs[0].shape[1]
     ff = a_ref.shape[1]
     tiles, rt, _ = ab.shape
-    here = tiles // 2
+    here = tiles // 2 if first else tiles
     weights = load_weights(m_ref[0], steps, wg_ref, wu_ref, w, w_sem)
     passes = g_in.shape[0]
 
@@ -316,7 +388,9 @@
     part = width // MP
     tiles = rows // rt
     last = not first and len(steps) == 1
-    out = pltpu.HBM((rows // 2, part), bf16)
+    outs = [pltpu.HBM((rows // 2, part), bf16)] * 2
+    if not first:
+        outs = [pltpu.HBM((rows, part), bf16)] * len(steps)
     more = []
     scratch = []
     if first:
@@ -327,8 +401,8 @@
     return pl.pallas_call(
         functools.partial(back_kernel, steps, first),
         in_specs=[smem] + [anywhere] * 3 + [vmem] * 2 + [anywhere] * 2 + [vmem] * first,
-        out_specs=[vmem] * (2 * len(steps) + len(more)),
-        out_shape=[out] * (2 * len(steps)) + more,
+        out_specs=[vmem] * (len(outs) + len(more)),
+        out_shape=outs + more,
         scratch_shapes=scratch
         + [
             pltpu.VMEM((tiles, rt, 2 * ff), bf16),
@@ -343,9 +417,8 @@
 
 
 def finish_kernel(
-    x_ref, high_ref, low_ref, one_ref, two_ref, rms_ref, inner_ref, mask_ref, token_ref, gain_ref, out_ref
+    x_ref, own_ref, one_ref, two_ref, rms_ref, inner_ref, mask_ref, token_ref, gain_ref, out_ref
 ):
-    half = pl.num_programs(0) // 2
     rms = rms_ref[...]
     eye = lax.broadcasted_iota(jnp.int32, (L, L), 0) == lax.broadcasted_iota(jnp.int32, (L, L), 1)
     inner = jnp.concatenate(
@@ -355,8 +428,7 @@
         ],
         axis=0,
     )
-    own = jnp.where(pl.program_id(0) < half, high_ref[...], low_ref[...]).astype(f32)
-    normed = own + one_ref[...].astype(f32) + two_ref[...].astype(f32)
+    normed = own_ref[...].astype(f32) + one_ref[...].astype(f32) + two_ref[...].astype(f32)
     grad = rms * gain_ref[...] * normed - x_ref[...].astype(f32) * (rms * rms * inner)
     mask = mask_ref[...]
     for p in range(out_ref.shape[0] // L):
@@ -364,10 +436,9 @@
         out_ref[part] = (grad[part] + mask[part] * token_ref[0, p : p + 1]).astype(bf16)
 
 
-def finish(x, high, low, one, two, rms, inner, mask, token, gain):
+def finish(x, own, one, two, rms, inner, mask, token, gain):
     rows, part = x.shape
     rt = 256
-    half = rows // (2 * rt)
     whole = pl.BlockSpec((rt, part), lambda r: (r, 0))
     column = pl.BlockSpec((rt, 1), lambda r: (r, 0))
     return pl.pallas_call(
@@ -375,8 +446,7 @@
         grid=(rows // rt,),
         in_specs=[
             whole,
-            pl.BlockSpec((rt, part), lambda r: (jnp.minimum(r, half - 1), 0)),
-            pl.BlockSpec((rt, part), lambda r: (jnp.maximum(r - half, 0), 0)),
+            whole,
             whole,
             whole,
             column,
@@ -389,7 +459,7 @@
         out_shape=jax.ShapeDtypeStruct(x.shape, bf16),
         compiler_params=pltpu.CompilerParams(vmem_limit_bytes=16 << 20),
         name="finish",
-    )(*map(in_hbm, (x, high, low, one, two)), rms, inner, mask, token.reshape(-1, rt // L, part), gain)
+    )(*map(in_hbm, (x, own, one, two)), rms, inner, mask, token.reshape(-1, rt // L, part), gain)
 
 
 def per_device(
@@ -420,16 +490,10 @@
     extra = jnp.pad(extra, ((0, 0), (0, L - 3)))
     sent = jnp.concatenate([mine, extra], axis=1)
 
-    chunks = []
-    at = 0
-    for rows in CHUNKS:
-        own = hidden_in[at : at + rows]
-        if chunks:
-            own, sent, *last = lax.optimization_barrier((own, sent, *chunks[-1][1:]))
-            chunks[-1] = (chunks[-1][0], *last)
-        left, right = shifted(own, 1), shifted(own, -1)
-        chunks.append((at, own, right, left, *(across(left, right) if at == 0 else ())))
-        at += rows
+    right, left = shifted(hidden_in, -1), shifted(hidden_in, 1)
+    right, left, sent = lax.optimization_barrier((right, left, sent))
+    half = row_count // 2
+    high, low = shifted(left[:half], 1), shifted(right[half:], -1)
     all_q = lax.all_gather(sent, ("x", "z"), axis=0)
 
     live_pass = jnp.arange(passes, dtype=jnp.int32) % most < jnp.repeat(passage_counts, most)
@@ -445,26 +509,15 @@
     divisor = jnp.maximum(jnp.sum(live_float, axis=1), 1.0)[:, None]
     gain = norm_gain.reshape(MP, 1, part)
 
-    done = []
-    before = ()
-    for k, (at, *pieces) in enumerate(chunks):
-        if k > 0:
-            pool, right, left = lax.optimization_barrier((done[-1][3], *pieces[1:]))
-            done[-1] = (*done[-1][:3], pool, *done[-1][4:])
-            pieces = (pieces[0], right, left, *across(left, right))
-        part_mask = mask[at : at + CHUNKS[k]]
-        done.append(encode(m, k, row_count, before, *pieces, part_mask, gain, w_gate, w_up))
-        before = done[-1][:3]
-    a, b, c = before
-    pool = jnp.concatenate([d[3] for d in done], axis=1)
+    weights = (gain, w_gate, w_up)
+    acc, square, own_x = encode_near(m, hidden_in, right, left, mask, *weights)
+    a, b, c, pool, rms = encode_far(m, high, low, acc, square, mask, *weights)
     pool = jnp.moveaxis(pool, 0, 1).reshape(passes, -1)
-    rms = jnp.concatenate([d[4] for d in done], axis=0)
-    xpool = jnp.concatenate([d[5] for d in done], axis=0)
 
     high = pool.astype(bf16)
     low = (pool - high.astype(f32)).astype(bf16)
     branch = jnp.dot(jnp.concatenate([high, low], 0), w_down, preferred_element_type=f32)
-    own_x = (jnp.arange(MP) == mi)[None, :, None].astype(f32) * xpool
+    own_x = (jnp.arange(MP) == mi)[None, :, None].astype(f32) * own_x[:, None, :]
     summed = (branch[:passes] + branch[passes:] + own_x.reshape(passes, width)) / divisor
     summed = copies_to_all(summed.astype(bf16), ("core", "mp"), cores * MP)
     summed = summed.reshape(cores, MP, passes, width).astype(f32).sum(axis=1)
@@ -509,19 +562,15 @@
     high, low, g = back(m, (2,), 256, True, a, b, c, token_grad, none, *tensors)
     from_right = shifted(high, -1)
     from_left = shifted(low, 1)
-    right_high, right_low, left_high, left_low = back(
-        m, (1, 3), 512, False, a, b, c, g, none, *tensors
-    )
-    right_low = (right_low.astype(f32) + from_left.astype(f32)).astype(bf16)
-    left_high = (left_high.astype(f32) + from_right.astype(f32)).astype(bf16)
-    right = jnp.concatenate([right_high, right_low], axis=0)
-    left = jnp.concatenate([left_high, left_low], axis=0)
+    right, left = back(m, (1, 3), 512, False, a, b, c, g, none, *tensors)
+    right = right.at[half:].set((right[half:].astype(f32) + from_left.astype(f32)).astype(bf16))
+    left = left.at[:half].set((left[:half].astype(f32) + from_right.astype(f32)).astype(bf16))
     right, left, g = lax.optimization_barrier((right, left, g))
     right = shifted(right, 1)
     left = shifted(left, -1)
     g_high = g.astype(bf16)
     gs = jnp.concatenate([g_high, (g - g_high.astype(f32)).astype(bf16)], axis=0)
-    own_high, own_low, s = back(m, (0,), 512, False, a, b, c, g, gs, *tensors)
+    own, s = back(m, (0,), 512, False, a, b, c, g, gs, *tensors)
     small = jnp.concatenate(
         [s.reshape(passes, L), jnp.pad(own_loss[None, :], ((0, 7), (0, L - share)))], axis=0
     )
@@ -531,7 +580,7 @@
     own_gain = lax.dynamic_slice_in_dim(norm_gain, mi * part, part)[None, :]
     own_token = lax.dynamic_slice_in_dim(token_grad, mi * part, part, axis=1).astype(f32)
     rest = (rms, inner, mask, own_token, own_gain)
-    hidden_grad = finish(hidden_in, own_high, own_low, right, left, *rest)
+    hidden_grad = finish(hidden_in, own, right, left, *rest)
     return query_loss, hidden_grad
 
 

time: 199 us -> 191 us (0.960)
  starting transfers between devices: 33.9 us -> 26.5 us
  local copies, waits for them, and re-layouts: 11.7 us -> 9.52 us
  waiting for transfers between devices: 40.7 us -> 42.7 us
    all_to_all x1, waiting for transfers between devices: 10.5 us -> 20.4 us  [per_device(): lax.all_to_all(queries.reshape(MP, share, part), 'mp', split_axis=0, conc...]
    ppermute x12 -> x8, waiting for transfers between devices: 8.11 us -> 0.02 us  [shifted(): return lax.ppermute(x, 'mp', [(i, (i + by) % MP) for i in range(MP)])]
    ppermute x12 -> x8, starting transfers between devices: 18.4 us -> 11.9 us  [shifted(): return lax.ppermute(x, 'mp', [(i, (i + by) % MP) for i in range(MP)])]
    scatter x0 -> x2, other arithmetic: none -> 3.94 us  [the longest x1 1.97 us: per_device(): right.at[half:]]
    concatenate x4 -> x0, other arithmetic: 3.21 us -> none  [the longest x1 2.14 us: per_device(): left = jnp.concatenate([left_high, left_low], axis=0)]
    slice x8 -> x2, local copies, waits for them, and re-layouts: 3.14 us -> 0.07 us  [per_device(): high, low = (shifted(left[:half], 1), shifted(right[half:], -1))]
    unnamed x48 -> x22, local copies, waits for them, and re-layouts: 4.36 us -> 5.1 us
  transfers between devices with their start and end apart: 18 -> 14, of which waited for: 7 -> 4; matrix products, arithmetic and copies ran while one was open for 6% -> 5% of each run, Pallas kernels for 27% -> 29%
where the time goes in v5:
time: 191 us; the launch traced here: 190 us
  Pallas kernels  69.3 us (36%)
  waiting for transfers between devices  42.7 us (22%)
  starting transfers between devices  26.5 us (14%)
  blocking collectives  15.3 us (8%)
  between operations  14.4 us (8%)
  local copies, waits for them, and re-layouts  9.52 us (5%)
  other arithmetic  9.07 us (5%)
  matrix products  3.77 us (2%)
    pallas_call x3, Pallas kernels, back(): pl.pallas_call(functools.partial(back_kernel, steps, first), in_specs=[sm...  34.7 us
    all_to_all x1, waiting for transfers between devices, per_device(): lax.all_to_all(queries.reshape(MP, share, part), 'mp', split_axis=0, conc...  20.4 us
    pallas_call x1, Pallas kernels, encode_near(): pl.pallas_call(encode_near_kernel, in_specs=[smem] + [anywhere] * 3 + [vm...  18.1 us
    all_to_all x1, blocking collectives, copies_to_all(): lax.all_to_all(jnp.broadcast_to(x, (count, *x.shape)), axes, split_axis=0...  15.3 us
    all_to_all x2, waiting for transfers between devices, copies_to_all(): lax.all_to_all(jnp.broadcast_to(x, (count, *x.shape)), axes, split_axis=0...  15.3 us
    pallas_call x1, Pallas kernels, encode_far(): pl.pallas_call(encode_far_kernel, in_specs=[smem] + [anywhere] * 3 + [vme...  12.1 us
    ppermute x8, starting transfers between devices, shifted(): return lax.ppermute(x, 'mp', [(i, (i + by) % MP) for i in range(MP)])  11.9 us
    all_to_all x1, waiting for transfers between devices, per_device(): lax.all_to_all(grad, ('core', 'mp'), split_axis=0, concat_axis=0, tiled=T...  6.94 us
  transfers between devices with their start and end apart: 14, of which 4 were waited for; matrix products, arithmetic and copies ran while one was open for 5% of the time, Pallas kernels for 29%

profile of v5, /device:TPU:0, one launch (start us, length us, event | category | flops | bytes accessed | tf_op | source)
XLA Modules:
  0.0 190.5 jit_solution(15379463213759655452)
XLA Ops:
  7.2 3.2 %collective-permute-start = (bf16[1024,512]{1,0:T(8,128)(2,1)}, bf16[1024,512]{1,0:T(8,128)(2,1)S(1)}, u32[]{:S(2)}, u32[]{:S(2)}) collective-permute-start(bf16[1024,512]{1,0:T(8,128)(2,1)} %x_ref.1), channel_id=1, source_target_pairs={{0,3},{1,0},{2,1},{3,2},{4,7},{5,4},{6,5},{7,6},{8,11},{9,8},{10,9... | collective-permute-start | bytes 3145736 | tf_op jit(solution)/shard_map/ppermute | solution.py:24
  10.3 4.5 %all-to-all-start = ((bf16[4,32,512]{2,1,0:T(8,128)(2,1)}), bf16[4,32,512]{2,1,0:T(8,128)(2,1)S(1)}, u32[]{:S(2)}, u32[]{:S(2)}) async-start(bf16[4,32,512]{2,1,0:T(8,128)(2,1)} %bitcast.69), calls=%async_computation | async-start | bytes 262144 | tf_op jit(solution)/shard_map/all_to_all | solution.py:481
  17.4 20.4 %all-to-all-done = bf16[4,32,512]{2,1,0:T(8,128)(2,1)S(1)} async-done(((bf16[4,32,512]{2,1,0:T(8,128)(2,1)}), bf16[4,32,512]{2,1,0:T(8,128)(2,1)S(1)}, u32[]{:S(2)}, u32[]{:S(2)}) %all-to-all-start) | async-done | bytes 131104 | tf_op jit(solution)/shard_map/all_to_all | solution.py:481
  39.3 3.3 %collective-permute-start.3 = (bf16[512,512]{1,0:T(8,128)(2,1)S(1)}, bf16[512,512]{1,0:T(8,128)(2,1)S(1)}, u32[]{:S(2)}, u32[]{:S(2)}) collective-permute-start(bf16[512,512]{1,0:T(8,128)(2,1)S(1)} %slice.88), channel_id=1, source_target_pairs={{0,3},{1,0},{2,1},{3,2},{4,7},{5,4},{6,5},{7,6},{8,11},{9,8},{10,9... | collective-permute-start | bytes 1572872 | tf_op jit(solution)/shard_map/ppermute | solution.py:24
  42.6 18.1 %encode_near.1 = (f32[7,1024,512]{2,1,0:T(8,128)}, f32[1024,1]{1,0:T(8,128)S(1)}, f32[8,512]{1,0:T(8,128)S(1)}) custom-call(s32[1]{0:T(128)} %bitcast.m_ref, bf16[1024,512]{1,0:T(8,128)(2,1)} %x_ref.1, bf16[1024,512]{1,0:T(8,128)(2,1)} %copy-done.5, bf16[1024,512]{1,0:T(8,128)(2,1)} %copy-done.6, f32[1024,1]{1,0:T(8,128)S(1)} %copy.29.mask_ref, ...), custom_call_target="tpu_custom_call" | custom-call | flops 11274289152 | bytes 8388608 | tf_op jit(solution)/shard_map/encode_near/pallas_call | solution.py:147
  61.6 12.1 %encode_far.1 = (bf16[1024,1792]{1,0:T(8,128)(2,1)}, bf16[1024,1792]{1,0:T(8,128)(2,1)}, bf16[1024,1792]{1,0:T(8,128)(2,1)}, f32[7,8,256]{2,1,0:T(8,128)S(1)}, f32[1024,1]{1,0:T(8,128)S(1)}) custom-call(s32[1]{0:T(128)} %bitcast.m_ref, bf16[512,512]{1,0:T(8,128)(2,1)} %copy-done.3, bf16[512,512]{1,0:T(8,128)(2,1)} %copy-done.4, ...), custom_call_target="tpu_custom_call" | custom-call | flops 3758096384 | bytes 11010048 | tf_op jit(solution)/shard_map/encode_far/pallas_call | solution.py:253
  75.6 3.4 %all-to-all-start.1 = ((bf16[8,8,2048]{2,1,0:T(8,128)(2,1)}), bf16[8,8,2048]{2,1,0:T(8,128)(2,1)S(1)}, u32[]{:S(2)}, u32[]{:S(2)}) async-start(bf16[8,8,2048]{2,1,0:T(8,128)(2,1)} %broadcast_in_dim.21), calls=%async_computation.1 | async-start | bytes 524288 | tf_op jit(solution)/shard_map/all_to_all | solution.py:37
  79.2 6.7 %all-to-all-done.1 = bf16[8,8,2048]{2,1,0:T(8,128)(2,1)S(1)} async-done(((bf16[8,8,2048]{2,1,0:T(8,128)(2,1)}), bf16[8,8,2048]{2,1,0:T(8,128)(2,1)S(1)}, u32[]{:S(2)}, u32[]{:S(2)}) %all-to-all-start.1) | async-done | bytes 262176 | tf_op jit(solution)/shard_map/all_to_all | solution.py:37
  86.1 1.1 slice_convert_fusion
  87.7 2.3 %fusion.21 = (f32[512]{0:T(512)S(1)}, f32[512]{0:T(512)S(1)}, f32[16,512]{1,0:T(8,128)S(1)}) fusion(f32[16]{0:T(128)S(1)} %rsqrt.32, f32[512]{0:T(512)S(1)} %get-tuple-element.69, f32[16]{0:T(128)S(1)} %fusion.26, f32[16]{0:T(128)S(1)} %fusion.29, f32[512]{0:T(512)S(1)} %get-tuple-element.70, bf16[512,2176]{1,0:T(8,128)(2,1)} %all-gather.3.cloned.1.call-done, ...), kind=kOutput, calls=%fused_computation.44 | convolution fusion | flops 33610752 | bytes 2203840 | tf_op jit(solution)/shard_map/dot_general | solution.py:47
  90.0 15.3 %all_to_all.25 = f32[16,8,128]{2,1,0:T(8,128)S(1)} all-to-all(f32[16,8,128]{2,1,0:T(8,128)S(1)} %broadcast_in_dim.22), channel_id=1, replica_groups=mesh['x'=4,'z'=4,'core'=2,'mp'=4] {'x','z'}, dimensions={0} | all-to-all | bytes 131072 | tf_op jit(solution)/shard_map/all_to_all | solution.py:37
  106.9 3.4 %all-to-all-start.3 = ((bf16[8,8,2176]{2,1,0:T(8,128)(2,1)}), bf16[8,8,2176]{2,1,0:T(8,128)(2,1)S(1)}, u32[]{:S(2)}, u32[]{:S(2)}) async-start(bf16[8,8,2176]{2,1,0:T(8,128)(2,1)} %bitcast.20), calls=%async_computation.3 | async-start | bytes 557056 | tf_op jit(solution)/shard_map/all_to_all | solution.py:553
  110.4 6.9 %all-to-all-done.3 = bf16[8,8,2176]{2,1,0:T(8,128)(2,1)S(1)} async-done(((bf16[8,8,2176]{2,1,0:T(8,128)(2,1)}), bf16[8,8,2176]{2,1,0:T(8,128)(2,1)S(1)}, u32[]{:S(2)}, u32[]{:S(2)}) %all-to-all-start.3) | async-done | bytes 278560 | tf_op jit(solution)/shard_map/all_to_all | solution.py:553
  117.7 3.1 %copy-done = bf16[1792,2048]{1,0:T(8,128)(2,1)S(1)} copy-done((bf16[1792,2048]{1,0:T(8,128)(2,1)S(1)}, bf16[1792,2048]{1,0:T(8,128)(2,1)}, u32[]{:S(2)}) %copy-start) | copy-done | bytes 7340056
  120.7 10.3 %back.3 = (bf16[512,512]{1,0:T(8,128)(2,1)}, bf16[512,512]{1,0:T(8,128)(2,1)}, f32[8,1792]{1,0:T(8,128)S(1)}) custom-call(s32[1]{0:T(128)} %bitcast.m_ref, bf16[1024,1792]{1,0:T(8,128)(2,1)} %get-tuple-element.51.a_ref, bf16[1024,1792]{1,0:T(8,128)(2,1)} %get-tuple-element.52.b_ref, bf16[1024,1792]{1,0:T(8,128)(2,1)} %get-tuple-element.53.c_ref, ...), custom_call_target="tpu_custom_call" | custom-call | flops 1 | bytes 1 | tf_op jit(solution)/shard_map/back/pallas_call | solution.py:401
  131.0 1.8 collective-permute-start.6
  133.2 13.5 %back.4 = (bf16[1024,512]{1,0:T(8,128)(2,1)}, bf16[1024,512]{1,0:T(8,128)(2,1)}) custom-call(s32[1]{0:T(128)} %bitcast.m_ref, bf16[1024,1792]{1,0:T(8,128)(2,1)} %get-tuple-element.51.a_ref, bf16[1024,1792]{1,0:T(8,128)(2,1)} %get-tuple-element.52.b_ref, bf16[1024,1792]{1,0:T(8,128)(2,1)} %get-tuple-element.53.c_ref, f32[8,1792]{1,0:T(8,128)S(1)} %get-tuple-element.62.g_in, ...), custom_call_target="tpu_custom_call" | custom-call | flops 1 | bytes 1 | tf_op jit(solution)/shard_map/back/pallas_call | solution.py:401
  146.7 2.0 %fusion.5 = bf16[1024,512]{1,0:T(8,128)(2,1)} fusion(bf16[1024,512]{1,0:T(8,128)(2,1)} %get-tuple-element.60, bf16[512,512]{1,0:T(8,128)(2,1)S(1)} %collective-permute-done.6), kind=kLoop, calls=%fused_computation.9 | loop fusion | flops 1048576 | bytes 1572864 | tf_op jit(solution)/shard_map/scatter | solution.py:567
  148.7 2.0 %fusion.4 = bf16[1024,512]{1,0:T(8,128)(2,1)} fusion(bf16[1024,512]{1,0:T(8,128)(2,1)} %get-tuple-element.58, bf16[512,512]{1,0:T(8,128)(2,1)S(1)} %collective-permute-done.5), kind=kLoop, calls=%fused_computation.8 | loop fusion | flops 1048576 | bytes 1572864 | tf_op jit(solution)/shard_map/scatter | solution.py:566
  151.4 2.4 %collective-permute-start.8 = (bf16[1024,512]{1,0:T(8,128)(2,1)}, bf16[1024,512]{1,0:T(8,128)(2,1)}, u32[]{:S(2)}, u32[]{:S(2)}) collective-permute-start(bf16[1024,512]{1,0:T(8,128)(2,1)} %fusion.5), channel_id=1, source_target_pairs={{0,3},{1,0},{2,1},{3,2},{4,7},{5,4},{6,5},{7,6},{8,11},{9,8},{10,9... | collective-permute-start | bytes 3145736 | tf_op jit(solution)/shard_map/ppermute | solution.py:24
  154.0 10.9 %back.5 = (bf16[1024,512]{1,0:T(8,128)(2,1)}, f32[1024,1]{1,0:T(8,128)S(1)}) custom-call(s32[1]{0:T(128)} %bitcast.m_ref, bf16[1024,1792]{1,0:T(8,128)(2,1)} %get-tuple-element.51.a_ref, bf16[1024,1792]{1,0:T(8,128)(2,1)} %get-tuple-element.52.b_ref, bf16[1024,1792]{1,0:T(8,128)(2,1)} %get-tuple-element.53.c_ref, f32[8,1792]{1,0:T(8,128)S(1)} %get-tuple-element.62.g_in, ...), custom_call_target="tpu_custom_call" | custom-call | flops 1 | bytes 1 | tf_op jit(solution)/shard_map/back/pallas_call | solution.py:401
  165.7 3.3 %all-to-all-start.4 = ((f32[4,16,128]{2,1,0:T(8,128)}), f32[4,16,128]{2,1,0:T(8,128)S(1)}, u32[]{:S(2)}, u32[]{:S(2)}) async-start(f32[4,16,128]{2,1,0:T(8,128)} %broadcast_in_dim.51), calls=%async_computation.4 | async-start | bytes 65536 | tf_op jit(solution)/shard_map/all_to_all | solution.py:37
  169.1 8.5 %all-to-all-done.4 = f32[4,16,128]{2,1,0:T(8,128)S(1)} async-done(((f32[4,16,128]{2,1,0:T(8,128)}), f32[4,16,128]{2,1,0:T(8,128)S(1)}, u32[]{:S(2)}, u32[]{:S(2)}) %all-to-all-start.4) | async-done | bytes 32800 | tf_op jit(solution)/shard_map/all_to_all | solution.py:37
  179.2 4.4 %finish.1 = bf16[1024,512]{1,0:T(8,128)(2,1)} custom-call(bf16[1024,512]{1,0:T(8,128)(2,1)} %x_ref.1, bf16[1024,512]{1,0:T(8,128)(2,1)} %get-tuple-element.64.own_ref, bf16[1024,512]{1,0:T(8,128)(2,1)} %copy-done.2, bf16[1024,512]{1,0:T(8,128)(2,1)} %collective-permute-done.8.two_ref, f32[1024,1]{1,0:T(8,128)S(1)} %get-tuple-element.67.rms_ref, ...), custom_call_target="tpu_custom_call" | custom-call | tf_op jit(solution)/shard_map/finish/pallas_call | solution.py:444
  (100 shorter events, 13.2 us)
Async XLA Ops:
  7.2 35.4 %copy-start.1 = (f32[2048]{0:T(1024)S(1)}, f32[2048]{0:T(1024)}, u32[]{:S(2)}) copy-start(f32[2048]{0:T(1024)} %param.18) | copy-start | bytes 24580
  7.2 31.6 %collective-permute-start = (bf16[1024,512]{1,0:T(8,128)(2,1)}, bf16[1024,512]{1,0:T(8,128)(2,1)S(1)}, u32[]{:S(2)}, u32[]{:S(2)}) collective-permute-start(bf16[1024,512]{1,0:T(8,128)(2,1)} %x_ref.1), channel_id=1, source_target_pairs={{0,3},{1,0},{2,1},{3,2},{4,7},{5,4},{6,5},{7,6},{8,11},{9,8},{10,9... | collective-permute-start | bytes 3145736 | tf_op jit(solution)/shard_map/ppermute | solution.py:24
  10.3 28.4 %collective-permute-start.1 = (bf16[1024,512]{1,0:T(8,128)(2,1)}, bf16[1024,512]{1,0:T(8,128)(2,1)S(1)}, u32[]{:S(2)}, u32[]{:S(2)}) collective-permute-start(bf16[1024,512]{1,0:T(8,128)(2,1)} %x_ref.1), channel_id=1, source_target_pairs={{0,1},{1,2},{2,3},{3,0},{4,5},{5,6},{6,7},{7,4},{8,9},{9,10},{10,1... | collective-permute-start | bytes 3145736 | tf_op jit(solution)/shard_map/ppermute | solution.py:24
  10.3 27.4 %all-to-all-start = ((bf16[4,32,512]{2,1,0:T(8,128)(2,1)}), bf16[4,32,512]{2,1,0:T(8,128)(2,1)S(1)}, u32[]{:S(2)}, u32[]{:S(2)}) async-start(bf16[4,32,512]{2,1,0:T(8,128)(2,1)} %bitcast.69), calls=%async_computation | async-start | bytes 262144 | tf_op jit(solution)/shard_map/all_to_all | solution.py:481
  14.8 71.3 %all-gather.3.cloned.1.call-start = ((), (), s32[]{:S(2)}) async-start(), calls=%async_computation.5 | async-start | bytes 2367488 | tf_op jit(solution)/shard_map/all_gather | solution.py:497
  15.7 63.4 %collective-permute-start.4 = (s32[8]{0:T(128)S(1)}, s32[8]{0:T(128)S(1)}, u32[]{:S(2)}, u32[]{:S(2)}) collective-permute-start(s32[8]{0:T(128)S(1)} %get-tuple-element.77), channel_id=1, source_target_pairs={{0,4},{4,0},{1,5},{5,1},{2,6},{6,2},{3,7},{7,3},{8,12},{12,8},{9,1... | collective-permute-start | bytes 104 | tf_op jit(solution)/shard_map/ppermute | solution.py:33
  38.7 3.8 %copy-start.5 = (bf16[1024,512]{1,0:T(8,128)(2,1)}, bf16[1024,512]{1,0:T(8,128)(2,1)S(1)}, u32[]{:S(2)}) copy-start(bf16[1024,512]{1,0:T(8,128)(2,1)S(1)} %collective-permute-done.right_ref) | copy-start | bytes 3145732
  38.7 3.8 %copy-start.6 = (bf16[1024,512]{1,0:T(8,128)(2,1)}, bf16[1024,512]{1,0:T(8,128)(2,1)S(1)}, u32[]{:S(2)}) copy-start(bf16[1024,512]{1,0:T(8,128)(2,1)S(1)} %collective-permute-done.1.left_ref) | copy-start | bytes 3145732
  39.2 21.5 %collective-permute-start.2 = (bf16[512,512]{1,0:T(8,128)(2,1)S(1)}, bf16[512,512]{1,0:T(8,128)(2,1)S(1)}, u32[]{:S(2)}, u32[]{:S(2)}) collective-permute-start(bf16[512,512]{1,0:T(8,128)(2,1)S(1)} %slice.87), channel_id=1, source_target_pairs={{0,1},{1,2},{2,3},{3,0},{4,5},{5,6},{6,7},{7,4},{8,9},{9,10},{10,1... | collective-permute-start | bytes 1572872 | tf_op jit(solution)/shard_map/ppermute | solution.py:24
  39.2 34.5 %slice-start = ((s8[7340032]{0:T(1024)(128)(4,1)}), s8[4194304]{0:T(1024)(128)(4,1)S(1)}, s32[]{:S(2)}) async-start(s8[7340032]{0:T(1024)(128)(4,1)} %bitcast.58), calls=%async_computation.6 | async-start | bytes 8388608
  39.3 21.4 %collective-permute-start.3 = (bf16[512,512]{1,0:T(8,128)(2,1)S(1)}, bf16[512,512]{1,0:T(8,128)(2,1)S(1)}, u32[]{:S(2)}, u32[]{:S(2)}) collective-permute-start(bf16[512,512]{1,0:T(8,128)(2,1)S(1)} %slice.88), channel_id=1, source_target_pairs={{0,3},{1,0},{2,1},{3,2},{4,7},{5,4},{6,5},{7,6},{8,11},{9,8},{10,9... | collective-permute-start | bytes 1572872 | tf_op jit(solution)/shard_map/ppermute | solution.py:24
  42.6 31.2 %slice-start.1 = ((s8[7340032]{0:T(1024)(128)(4,1)}), s8[3145728]{0:T(1024)(128)(4,1)S(1)}, s32[]{:S(2)}) async-start(s8[7340032]{0:T(1024)(128)(4,1)} %bitcast.58), calls=%async_computation.7 | async-start | bytes 6291456
  60.7 0.8 copy-start.3
  60.7 0.9 copy-start.4
  75.6 10.3 %all-to-all-start.1 = ((bf16[8,8,2048]{2,1,0:T(8,128)(2,1)}), bf16[8,8,2048]{2,1,0:T(8,128)(2,1)S(1)}, u32[]{:S(2)}, u32[]{:S(2)}) async-start(bf16[8,8,2048]{2,1,0:T(8,128)(2,1)} %broadcast_in_dim.21), calls=%async_computation.1 | async-start | bytes 524288 | tf_op jit(solution)/shard_map/all_to_all | solution.py:37
  86.1 19.5 %copy-start.7 = (bf16[512,2176]{1,0:T(8,128)(2,1)S(1)}, bf16[512,2176]{1,0:T(8,128)(2,1)}, u32[]{:S(2)}) copy-start(bf16[512,2176]{1,0:T(8,128)(2,1)} %all-gather.3.cloned.1.call-done) | copy-start | bytes 6684676
  106.9 10.4 %all-to-all-start.3 = ((bf16[8,8,2176]{2,1,0:T(8,128)(2,1)}), bf16[8,8,2176]{2,1,0:T(8,128)(2,1)S(1)}, u32[]{:S(2)}, u32[]{:S(2)}) async-start(bf16[8,8,2176]{2,1,0:T(8,128)(2,1)} %bitcast.20), calls=%async_computation.3 | async-start | bytes 557056 | tf_op jit(solution)/shard_map/all_to_all | solution.py:553
  117.7 3.1 %copy-start = (bf16[1792,2048]{1,0:T(8,128)(2,1)S(1)}, bf16[1792,2048]{1,0:T(8,128)(2,1)}, u32[]{:S(2)}) copy-start(bf16[1792,2048]{1,0:T(8,128)(2,1)} %refs_0_.1) | copy-start | bytes 22020100
  131.0 15.7 %collective-permute-start.6 = (bf16[512,512]{1,0:T(8,128)(2,1)}, bf16[512,512]{1,0:T(8,128)(2,1)S(1)}, u32[]{:S(2)}, u32[]{:S(2)}) collective-permute-start(bf16[512,512]{1,0:T(8,128)(2,1)} %get-tuple-element.61), channel_id=1, source_target_pairs={{0,3},{1,0},{2,1},{3,2},{4,7},{5,4},{6,5},{7,6},{8,11},{9,8},{10,9... | collective-permute-start | bytes 1572872 | tf_op jit(solution)/shard_map/ppermute | solution.py:24
  132.9 15.8 %collective-permute-start.5 = (bf16[512,512]{1,0:T(8,128)(2,1)}, bf16[512,512]{1,0:T(8,128)(2,1)S(1)}, u32[]{:S(2)}, u32[]{:S(2)}) collective-permute-start(bf16[512,512]{1,0:T(8,128)(2,1)} %get-tuple-element.59), channel_id=1, source_target_pairs={{0,1},{1,2},{2,3},{3,0},{4,5},{5,6},{6,7},{7,4},{8,9},{9,10},{10,1... | collective-permute-start | bytes 1572872 | tf_op jit(solution)/shard_map/ppermute | solution.py:24
  150.6 27.6 %collective-permute-start.7 = (bf16[1024,512]{1,0:T(8,128)(2,1)}, bf16[1024,512]{1,0:T(8,128)(2,1)S(1)}, u32[]{:S(2)}, u32[]{:S(2)}) collective-permute-start(bf16[1024,512]{1,0:T(8,128)(2,1)} %fusion.4), channel_id=1, source_target_pairs={{0,1},{1,2},{2,3},{3,0},{4,5},{5,6},{6,7},{7,4},{8,9},{9,10},{10,1... | collective-permute-start | bytes 3145736 | tf_op jit(solution)/shard_map/ppermute | solution.py:24
  151.4 26.8 %collective-permute-start.8 = (bf16[1024,512]{1,0:T(8,128)(2,1)}, bf16[1024,512]{1,0:T(8,128)(2,1)}, u32[]{:S(2)}, u32[]{:S(2)}) collective-permute-start(bf16[1024,512]{1,0:T(8,128)(2,1)} %fusion.5), channel_id=1, source_target_pairs={{0,3},{1,0},{2,1},{3,2},{4,7},{5,4},{6,5},{7,6},{8,11},{9,8},{10,9... | collective-permute-start | bytes 3145736 | tf_op jit(solution)/shard_map/ppermute | solution.py:24
  165.7 11.8 %all-to-all-start.4 = ((f32[4,16,128]{2,1,0:T(8,128)}), f32[4,16,128]{2,1,0:T(8,128)S(1)}, u32[]{:S(2)}, u32[]{:S(2)}) async-start(f32[4,16,128]{2,1,0:T(8,128)} %broadcast_in_dim.51), calls=%async_computation.4 | async-start | bytes 65536 | tf_op jit(solution)/shard_map/all_to_all | solution.py:37
  178.2 1.0 copy-start.2
Sparse Core Ops, SparseCore 0:
  38.9 45.3 all-gather.2

commit v6 on v5

--- a/solution.py
+++ b/solution.py
@@ -86,88 +86,95 @@
     return copies
 
 
-NEAR = (0, 1, 3)
-
-
-def encode_near_kernel(
-    m_ref, own_ref, right_ref, left_ref, mask_ref, gain_ref, wg_ref, wu_ref,
-    acc_out, square_ref, xpool_ref, xin, xs, w, acc, in_sem, w_sem, out_sem,
-):
-    rows, part = own_ref.shape
+def encode_near_kernel(steps, m_ref, *refs):
+    count = len(steps)
+    pieces, (gain_ref, wg_ref, wu_ref), refs = refs[:count], refs[count : count + 3], refs[count + 3 :]
+    own = count == 1
+    if own:
+        mask_ref, acc_out, square_ref, xpool_ref = refs[:4]
+        xin, xs, w, acc, in_sem, w_sem, out_sem = refs[4:]
+    else:
+        acc_in, square_in, acc_out, square_ref = refs[:4]
+        xin, xs, w, acc, in_sem, w_sem, out_sem, acc_sem = refs[4:]
+    rows, part = pieces[0].shape
     tiles = w.shape[0]
     m = m_ref[0]
-    arriving = [
-        pltpu.make_async_copy(ref, xin.at[k], in_sem.at[k])
-        for k, ref in enumerate((own_ref, right_ref, left_ref))
-    ]
+    arriving = [pltpu.make_async_copy(ref, xin.at[k], in_sem.at[k]) for k, ref in enumerate(pieces)]
     for copy in arriving:
         copy.start()
-    weights = weight_tiles(m, NEAR, part, wg_ref, wu_ref, w, w_sem)
-    loop_copies(weights, tiles)
+    weights = weight_tiles(m, steps, part, wg_ref, wu_ref, w, w_sem)
+
+    def inputs(n):
+        more = [] if own else [pltpu.make_async_copy(acc_in.at[n], acc.at[n], acc_sem.at[n])]
+        return weights(n) + more
+
+    loop_copies(inputs, tiles)
     for copy in arriving:
         copy.wait()
 
     def scale(p):
         at = pl.ds(pl.multiple_of(p * L, L), L)
-        total = None
-        for k, step in enumerate(NEAR):
+        total = None if own else square_in[at]
+        for k, step in enumerate(steps):
             v = xin[k, at].astype(f32)
             square = jnp.sum(v * v, axis=1, keepdims=True)
             total = square if total is None else total + square
             xs[at, k * part : (k + 1) * part] = (v * gain_ref[lax.rem(m + step, MP)]).astype(bf16)
-            if k == 0:
+            if own:
                 xpool_ref[pl.ds(p, 1)] = jnp.sum(v * mask_ref[at], axis=0, keepdims=True)
         square_ref[at] = total
 
     each(rows // L, scale)
 
     def leaving(n):
-        return pltpu.make_async_copy(acc.at[lax.rem(n, 2)], acc_out.at[n], out_sem.at[n])
+        return pltpu.make_async_copy(acc.at[n], acc_out.at[n], out_sem.at[n])
 
     def multiply(n):
-        for copy in weights(n):
+        for copy in inputs(n):
             copy.wait()
-
-        @pl.when(n >= 2)
-        def _():
-            leaving(n - 2).wait()
-
-        acc[lax.rem(n, 2)] = jnp.dot(xs[...], w[n], preferred_element_type=f32)
+        product = jnp.dot(xs[...], w[n], preferred_element_type=f32)
+        acc[n] = product if own else acc[n] + product
         leaving(n).start()
 
     each(tiles, multiply)
-    leaving(tiles - 2).wait()
-    leaving(tiles - 1).wait()
-
-
-def encode_near(m, own, right, left, mask, gain, w_gate, w_up):
-    rows, part = own.shape
+    each(tiles, lambda n: leaving(n).wait())
+
+
+def encode_near(m, steps, pieces, gain, w_gate, w_up, *rest):
+    own = len(steps) == 1
+    rows, part = pieces[0].shape
     width, ff = w_gate.shape
     tiles = ff // FT
+    count = len(steps)
+    rest = rest if own else (in_hbm(rest[0]), rest[1])
     return pl.pallas_call(
-        encode_near_kernel,
-        in_specs=[smem] + [anywhere] * 3 + [vmem, vmem, anywhere, anywhere],
-        out_specs=[anywhere, vmem, vmem],
+        functools.partial(encode_near_kernel, steps),
+        in_specs=[smem]
+        + [anywhere] * count
+        + [vmem, anywhere, anywhere]
+        + ([vmem] if own else [anywhere, vmem]),
+        out_specs=[anywhere, vmem] + [vmem] * own,
         out_shape=[
             pltpu.HBM((tiles, rows, 2 * FT), f32),
             jax.ShapeDtypeStruct((rows, 1), f32),
-            jax.ShapeDtypeStruct((rows // L, part), f32),
-        ],
+        ]
+        + [jax.ShapeDtypeStruct((rows // L, part), f32)] * own,
         scratch_shapes=[
-            pltpu.VMEM((len(NEAR), rows, part), bf16),
-            pltpu.VMEM((rows, len(NEAR) * part), bf16),
-            pltpu.VMEM((tiles, len(NEAR) * part, 2 * FT), bf16),
-            pltpu.VMEM((2, rows, 2 * FT), f32),
-            pltpu.SemaphoreType.DMA((len(NEAR),)),
-            pltpu.SemaphoreType.DMA((tiles, 2 * len(NEAR))),
+            pltpu.VMEM((count, rows, part), bf16),
+            pltpu.VMEM((rows, count * part), bf16),
+            pltpu.VMEM((tiles, count * part, 2 * FT), bf16),
+            pltpu.VMEM((tiles, rows, 2 * FT), f32),
+            pltpu.SemaphoreType.DMA((count,)),
+            pltpu.SemaphoreType.DMA((tiles, 2 * count)),
             pltpu.SemaphoreType.DMA((tiles,)),
-        ],
+        ]
+        + [pltpu.SemaphoreType.DMA((tiles,))] * (not own),
         compiler_params=pltpu.CompilerParams(vmem_limit_bytes=SCOPED),
         cost_estimate=pl.CostEstimate(
-            flops=3 * rows * width * ff, transcendentals=0, bytes_accessed=4 * rows * width
+            flops=count * rows * width * ff, transcendentals=0, bytes_accessed=4 * rows * width
         ),
         name="encode_near",
-    )(m, *map(in_hbm, (own, right, left)), mask, gain, in_hbm(w_gate), in_hbm(w_up))
+    )(m, *map(in_hbm, pieces), gain, in_hbm(w_gate), in_hbm(w_up), *rest)
 
 
 def encode_far_kernel(
@@ -416,6 +423,29 @@
     )(m, *map(in_hbm, (a, b, c)), g, gs, in_hbm(w_gate), in_hbm(w_up), *([w_down] if first else []))
 
 
+def add_kernel(right_ref, left_ref, from_left_ref, from_right_ref, right_out, left_out):
+    right_out[...] = (right_ref[...].astype(f32) + from_left_ref[...].astype(f32)).astype(bf16)
+    left_out[...] = (left_ref[...].astype(f32) + from_right_ref[...].astype(f32)).astype(bf16)
+
+
+def add_halves(right, left, from_left, from_right):
+    half, part = from_left.shape
+    rt = half // 2
+    upper = pl.BlockSpec((rt, part), lambda r: (r, 0))
+    lower = pl.BlockSpec((rt, part), lambda r: (r + 2, 0))
+    return pl.pallas_call(
+        add_kernel,
+        grid=(2,),
+        in_specs=[lower, upper, upper, upper],
+        out_specs=[lower, upper],
+        out_shape=[pltpu.HBM(right.shape, bf16)] * 2,
+        input_output_aliases={0: 0, 1: 1},
+        compiler_params=pltpu.CompilerParams(vmem_limit_bytes=8 << 20),
+        cost_estimate=pl.CostEstimate(flops=1, transcendentals=0, bytes_accessed=1),
+        name="add_halves",
+    )(in_hbm(right), in_hbm(left), from_left, from_right)
+
+
 def finish_kernel(
     x_ref, own_ref, one_ref, two_ref, rms_ref, inner_ref, mask_ref, token_ref, gain_ref, out_ref
 ):
@@ -459,7 +489,7 @@
         out_shape=jax.ShapeDtypeStruct(x.shape, bf16),
         compiler_params=pltpu.CompilerParams(vmem_limit_bytes=16 << 20),
         name="finish",
-    )(*map(in_hbm, (x, own, one, two)), rms, inner, mask, token.reshape(-1, rt // L, part), gain)
+    )(in_hbm(x), in_hbm(own), one, two, rms, inner, mask, token.reshape(-1, rt // L, part), gain)
 
 
 def per_device(
@@ -491,26 +521,26 @@
     sent = jnp.concatenate([mine, extra], axis=1)
 
     right, left = shifted(hidden_in, -1), shifted(hidden_in, 1)
-    right, left, sent = lax.optimization_barrier((right, left, sent))
+    live_pass = jnp.arange(passes, dtype=jnp.int32) % most < jnp.repeat(passage_counts, most)
+    token_live = (token_ids.reshape(passes, L) != pad_token) & live_pass[:, None]
+    live_float = token_live.astype(f32)
+    mask = live_float.reshape(row_count, 1)
+    weights = (norm_gain.reshape(MP, 1, part), w_gate, w_up)
+    acc, square, own_x = encode_near(m, (0,), (hidden_in,), *weights, mask)
+    right, left, sent, acc = lax.optimization_barrier((right, left, sent, acc))
     half = row_count // 2
     high, low = shifted(left[:half], 1), shifted(right[half:], -1)
     all_q = lax.all_gather(sent, ("x", "z"), axis=0)
 
-    live_pass = jnp.arange(passes, dtype=jnp.int32) % most < jnp.repeat(passage_counts, most)
     other_live = swapped(live_pass.astype(jnp.int32)) > 0
     live = jnp.where(
         core == 0,
         jnp.concatenate([live_pass, other_live]),
         jnp.concatenate([other_live, live_pass]),
     ).astype(f32)[:, None]
-    token_live = (token_ids.reshape(passes, L) != pad_token) & live_pass[:, None]
-    live_float = token_live.astype(f32)
-    mask = live_float.reshape(row_count, 1)
     divisor = jnp.maximum(jnp.sum(live_float, axis=1), 1.0)[:, None]
-    gain = norm_gain.reshape(MP, 1, part)
-
-    weights = (gain, w_gate, w_up)
-    acc, square, own_x = encode_near(m, hidden_in, right, left, mask, *weights)
+
+    acc, square = encode_near(m, (1, 3), (right, left), *weights, acc, square)
     a, b, c, pool, rms = encode_far(m, high, low, acc, square, mask, *weights)
     pool = jnp.moveaxis(pool, 0, 1).reshape(passes, -1)
 
@@ -563,8 +593,7 @@
     from_right = shifted(high, -1)
     from_left = shifted(low, 1)
     right, left = back(m, (1, 3), 512, False, a, b, c, g, none, *tensors)
-    right = right.at[half:].set((right[half:].astype(f32) + from_left.astype(f32)).astype(bf16))
-    left = left.at[:half].set((left[:half].astype(f32) + from_right.astype(f32)).astype(bf16))
+    right, left = add_halves(right, left, from_left, from_right)
     right, left, g = lax.optimization_barrier((right, left, g))
     right = shifted(right, 1)
     left = shifted(left, -1)

time: 191 us -> 185 us (0.969)
  waiting for transfers between devices: 42.7 us -> 33 us
  Pallas kernels: 69.3 us -> 76.3 us
  other arithmetic: 9.07 us -> 5.51 us
    all_to_all x1, waiting for transfers between devices: 20.4 us -> 11.4 us  [per_device(): lax.all_to_all(queries.reshape(MP, share, part), 'mp', split_axis=0, conc...]
    pallas_call x1 -> x3, Pallas kernels: 18.1 us -> 25.7 us  [the longest x2 23.6 us: encode_near(): pl.pallas_call(functools.partial(encode_near_kernel, steps), in_specs=[sm...]
    scatter x2 -> x0, other arithmetic: 3.94 us -> none  [the longest x1 1.97 us: per_device(): right.at[half:]]
    all_to_all x2, waiting for transfers between devices: 15.3 us -> 12.9 us  [copies_to_all(): lax.all_to_all(jnp.broadcast_to(x, (count, *x.shape)), axes, split_axis=0...]
    unnamed x22 -> x26, local copies, waits for them, and re-layouts: 5.1 us -> 5.69 us
  transfers between devices with their start and end apart: 14 -> 14, of which waited for: 4 -> 5; matrix products, arithmetic and copies ran while one was open for 5% -> 4% of each run, Pallas kernels for 29% -> 32%
where the time goes in v6:
time: 185 us; the launch traced here: 184 us
  Pallas kernels  76.3 us (41%)
  waiting for transfers between devices  33 us (18%)
  starting transfers between devices  27.7 us (15%)
  between operations  14.4 us (8%)
  blocking collectives  13.5 us (7%)
  local copies, waits for them, and re-layouts  10.1 us (5%)
  other arithmetic  5.51 us (3%)
  matrix products  3.77 us (2%)
    pallas_call x3, Pallas kernels, back(): pl.pallas_call(functools.partial(back_kernel, steps, first), in_specs=[sm...  34.7 us
    pallas_call x2, Pallas kernels, encode_near(): pl.pallas_call(functools.partial(encode_near_kernel, steps), in_specs=[sm...  23.6 us
    all_to_all x1, blocking collectives, copies_to_all(): lax.all_to_all(jnp.broadcast_to(x, (count, *x.shape)), axes, split_axis=0...  13.5 us
    ppermute x8, starting transfers between devices, shifted(): return lax.ppermute(x, 'mp', [(i, (i + by) % MP) for i in range(MP)])  13.1 us
    all_to_all x2, waiting for transfers between devices, copies_to_all(): lax.all_to_all(jnp.broadcast_to(x, (count, *x.shape)), axes, split_axis=0...  12.9 us
    pallas_call x1, Pallas kernels, encode_far(): pl.pallas_call(encode_far_kernel, in_specs=[smem] + [anywhere] * 3 + [vme...  11.8 us
    all_to_all x1, waiting for transfers between devices, per_device(): lax.all_to_all(queries.reshape(MP, share, part), 'mp', split_axis=0, conc...  11.4 us
    all_to_all x1, waiting for transfers between devices, per_device(): lax.all_to_all(grad, ('core', 'mp'), split_axis=0, concat_axis=0, tiled=T...  6.94 us
  transfers between devices with their start and end apart: 14, of which 5 were waited for; matrix products, arithmetic and copies ran while one was open for 4% of the time, Pallas kernels for 32%

profile of v6, /device:TPU:0, one launch (start us, length us, event | category | flops | bytes accessed | tf_op | source)
XLA Modules:
  0.0 184.4 jit_solution(11490302728224193724)
XLA Ops:
  7.2 3.2 %collective-permute-start = (bf16[1024,512]{1,0:T(8,128)(2,1)}, bf16[1024,512]{1,0:T(8,128)(2,1)S(1)}, u32[]{:S(2)}, u32[]{:S(2)}) collective-permute-start(bf16[1024,512]{1,0:T(8,128)(2,1)} %x_ref.1), channel_id=1, source_target_pairs={{0,3},{1,0},{2,1},{3,2},{4,7},{5,4},{6,5},{7,6},{8,11},{9,8},{10,9... | collective-permute-start | bytes 3145736 | tf_op jit(solution)/shard_map/ppermute | solution.py:24
  10.3 4.5 %all-to-all-start = ((bf16[4,32,512]{2,1,0:T(8,128)(2,1)}), bf16[4,32,512]{2,1,0:T(8,128)(2,1)S(1)}, u32[]{:S(2)}, u32[]{:S(2)}) async-start(bf16[4,32,512]{2,1,0:T(8,128)(2,1)} %bitcast.70), calls=%async_computation | async-start | bytes 262144 | tf_op jit(solution)/shard_map/all_to_all | solution.py:511
  17.5 8.7 %encode_near.2 = (f32[7,1024,512]{2,1,0:T(8,128)}, f32[1024,1]{1,0:T(8,128)S(1)}, f32[8,512]{1,0:T(8,128)S(1)}) custom-call(s32[1]{0:T(128)} %bitcast.m_ref, bf16[1024,512]{1,0:T(8,128)(2,1)} %x_ref.1, f32[4,1,512]{2,1,0:T(1,128)S(1)} %bitcast.60, bf16[2048,1792]{1,0:T(8,128)(2,1)} %wg_ref.7, bf16[2048,1792]{1,0:T(8,128)(2,1)} %wu_ref.7, ...), custom_call_target="tpu_custom_call" | custom-call | flops 3758096384 | bytes 8388608 | tf_op jit(solution)/shard_map/encode_near/pallas_call | solution.py:150
  26.3 11.4 %all-to-all-done = bf16[4,32,512]{2,1,0:T(8,128)(2,1)S(1)} async-done(((bf16[4,32,512]{2,1,0:T(8,128)(2,1)}), bf16[4,32,512]{2,1,0:T(8,128)(2,1)S(1)}, u32[]{:S(2)}, u32[]{:S(2)}) %all-to-all-start) | async-done | bytes 131104 | tf_op jit(solution)/shard_map/all_to_all | solution.py:511
  39.1 3.3 %collective-permute-start.3 = (bf16[512,512]{1,0:T(8,128)(2,1)S(1)}, bf16[512,512]{1,0:T(8,128)(2,1)S(1)}, u32[]{:S(2)}, u32[]{:S(2)}) collective-permute-start(bf16[512,512]{1,0:T(8,128)(2,1)S(1)} %slice.48), channel_id=1, source_target_pairs={{0,3},{1,0},{2,1},{3,2},{4,7},{5,4},{6,5},{7,6},{8,11},{9,8},{10,9... | collective-permute-start | bytes 1572872 | tf_op jit(solution)/shard_map/ppermute | solution.py:24
  42.4 14.9 %encode_near.3 = (f32[7,1024,512]{2,1,0:T(8,128)}, f32[1024,1]{1,0:T(8,128)S(1)}) custom-call(s32[1]{0:T(128)} %bitcast.m_ref, bf16[1024,512]{1,0:T(8,128)(2,1)} %copy-done.4, bf16[1024,512]{1,0:T(8,128)(2,1)} %copy-done.5, f32[4,1,512]{2,1,0:T(1,128)S(1)} %bitcast.61, bf16[2048,1792]{1,0:T(8,128)(2,1)} %wg_ref.7, bf16[2048,1792]{1,0:T(8,128)(2,1)} %wu_ref.7, ...), custom_call_target="tpu_custom_call" | custom-call | flops 7516192768 | bytes 8388608 | tf_op jit(solution)/shard_map/encode_near/pallas_call | solution.py:150
  58.4 11.8 %encode_far.1 = (bf16[1024,1792]{1,0:T(8,128)(2,1)}, bf16[1024,1792]{1,0:T(8,128)(2,1)}, bf16[1024,1792]{1,0:T(8,128)(2,1)}, f32[7,8,256]{2,1,0:T(8,128)S(1)}, f32[1024,1]{1,0:T(8,128)S(1)}) custom-call(s32[1]{0:T(128)} %bitcast.m_ref, bf16[512,512]{1,0:T(8,128)(2,1)} %copy-done.6, bf16[512,512]{1,0:T(8,128)(2,1)} %copy-done.7, ...), custom_call_target="tpu_custom_call" | custom-call | flops 3758096384 | bytes 11010048 | tf_op jit(solution)/shard_map/encode_far/pallas_call | solution.py:260
  72.1 3.4 %all-to-all-start.1 = ((bf16[8,8,2048]{2,1,0:T(8,128)(2,1)}), bf16[8,8,2048]{2,1,0:T(8,128)(2,1)S(1)}, u32[]{:S(2)}, u32[]{:S(2)}) async-start(bf16[8,8,2048]{2,1,0:T(8,128)(2,1)} %broadcast_in_dim.21), calls=%async_computation.1 | async-start | bytes 524288 | tf_op jit(solution)/shard_map/all_to_all | solution.py:37
  75.6 6.7 %all-to-all-done.1 = bf16[8,8,2048]{2,1,0:T(8,128)(2,1)S(1)} async-done(((bf16[8,8,2048]{2,1,0:T(8,128)(2,1)}), bf16[8,8,2048]{2,1,0:T(8,128)(2,1)S(1)}, u32[]{:S(2)}, u32[]{:S(2)}) %all-to-all-start.1) | async-done | bytes 262176 | tf_op jit(solution)/shard_map/all_to_all | solution.py:37
  82.6 1.7 all-gather.3.cloned.1.call-done
  85.8 2.3 %fusion.19 = (f32[512]{0:T(512)S(1)}, f32[512]{0:T(512)S(1)}, f32[16,512]{1,0:T(8,128)S(1)}) fusion(f32[16]{0:T(128)S(1)} %rsqrt.32, f32[512]{0:T(512)S(1)} %get-tuple-element.55, f32[16]{0:T(128)S(1)} %fusion.24, f32[16]{0:T(128)S(1)} %fusion.27, f32[512]{0:T(512)S(1)} %get-tuple-element.56, bf16[512,2176]{1,0:T(8,128)(2,1)} %all-gather.3.cloned.1.call-done, ...), kind=kOutput, calls=%fused_computation.40 | convolution fusion | flops 33610752 | bytes 2203840 | tf_op jit(solution)/shard_map/dot_general | solution.py:47
  88.2 13.5 %all_to_all.25 = f32[16,8,128]{2,1,0:T(8,128)S(1)} all-to-all(f32[16,8,128]{2,1,0:T(8,128)S(1)} %broadcast_in_dim.22), channel_id=1, replica_groups=mesh['x'=4,'z'=4,'core'=2,'mp'=4] {'x','z'}, dimensions={0} | all-to-all | bytes 131072 | tf_op jit(solution)/shard_map/all_to_all | solution.py:37
  103.3 3.4 %all-to-all-start.3 = ((bf16[8,8,2176]{2,1,0:T(8,128)(2,1)}), bf16[8,8,2176]{2,1,0:T(8,128)(2,1)S(1)}, u32[]{:S(2)}, u32[]{:S(2)}) async-start(bf16[8,8,2176]{2,1,0:T(8,128)(2,1)} %bitcast.20), calls=%async_computation.3 | async-start | bytes 557056 | tf_op jit(solution)/shard_map/all_to_all | solution.py:583
  106.8 6.9 %all-to-all-done.3 = bf16[8,8,2176]{2,1,0:T(8,128)(2,1)S(1)} async-done(((bf16[8,8,2176]{2,1,0:T(8,128)(2,1)}), bf16[8,8,2176]{2,1,0:T(8,128)(2,1)S(1)}, u32[]{:S(2)}, u32[]{:S(2)}) %all-to-all-start.3) | async-done | bytes 278560 | tf_op jit(solution)/shard_map/all_to_all | solution.py:583
  114.0 3.1 %copy-done = bf16[1792,2048]{1,0:T(8,128)(2,1)S(1)} copy-done((bf16[1792,2048]{1,0:T(8,128)(2,1)S(1)}, bf16[1792,2048]{1,0:T(8,128)(2,1)}, u32[]{:S(2)}) %copy-start) | copy-done | bytes 7340056
  117.1 10.3 %back.3 = (bf16[512,512]{1,0:T(8,128)(2,1)}, bf16[512,512]{1,0:T(8,128)(2,1)}, f32[8,1792]{1,0:T(8,128)S(1)}) custom-call(s32[1]{0:T(128)} %bitcast.m_ref, bf16[1024,1792]{1,0:T(8,128)(2,1)} %get-tuple-element.35.a_ref, bf16[1024,1792]{1,0:T(8,128)(2,1)} %get-tuple-element.36.b_ref, bf16[1024,1792]{1,0:T(8,128)(2,1)} %get-tuple-element.37.c_ref, ...), custom_call_target="tpu_custom_call" | custom-call | flops 1 | bytes 1 | tf_op jit(solution)/shard_map/back/pallas_call | solution.py:408
  128.3 2.4 %collective-permute-start.6 = (bf16[512,512]{1,0:T(8,128)(2,1)}, bf16[512,512]{1,0:T(8,128)(2,1)S(1)}, u32[]{:S(2)}, u32[]{:S(2)}) collective-permute-start(bf16[512,512]{1,0:T(8,128)(2,1)} %get-tuple-element.45), channel_id=1, source_target_pairs={{0,3},{1,0},{2,1},{3,2},{4,7},{5,4},{6,5},{7,6},{8,11},{9,8},{10,9... | collective-permute-start | bytes 1572872 | tf_op jit(solution)/shard_map/ppermute | solution.py:24
  130.8 13.5 %back.4 = (bf16[1024,512]{1,0:T(8,128)(2,1)}, bf16[1024,512]{1,0:T(8,128)(2,1)}) custom-call(s32[1]{0:T(128)} %bitcast.m_ref, bf16[1024,1792]{1,0:T(8,128)(2,1)} %get-tuple-element.35.a_ref, bf16[1024,1792]{1,0:T(8,128)(2,1)} %get-tuple-element.36.b_ref, bf16[1024,1792]{1,0:T(8,128)(2,1)} %get-tuple-element.37.c_ref, f32[8,1792]{1,0:T(8,128)S(1)} %get-tuple-element.48.g_in, ...), custom_call_target="tpu_custom_call" | custom-call | flops 1 | bytes 1 | tf_op jit(solution)/shard_map/back/pallas_call | solution.py:408
  144.3 2.1 %add_halves.1 = (bf16[1024,512]{1,0:T(8,128)(2,1)}, bf16[1024,512]{1,0:T(8,128)(2,1)}) custom-call(bf16[1024,512]{1,0:T(8,128)(2,1)} %get-tuple-element.42.right_ref, bf16[1024,512]{1,0:T(8,128)(2,1)} %get-tuple-element.43.left_ref, bf16[512,512]{1,0:T(8,128)(2,1)S(1)} %collective-permute-done.5.from_left_ref, ...), custom_call_target="tpu_custom_call", output_to_operand_aliasing={{0}: (0, {}), {1}: (1, {})} | custom-call | flops 1 | bytes 1 | tf_op jit(solution)/shard_map/add_halves/pallas_call | solution.py:436
  146.4 3.2 %collective-permute-start.8 = (bf16[1024,512]{1,0:T(8,128)(2,1)}, bf16[1024,512]{1,0:T(8,128)(2,1)S(1)}, u32[]{:S(2)}, u32[]{:S(2)}) collective-permute-start(bf16[1024,512]{1,0:T(8,128)(2,1)} %get-tuple-element.52), channel_id=1, source_target_pairs={{0,3},{1,0},{2,1},{3,2},{4,7},{5,4},{6,5},{7,6},{8,11},{9,8},{10,9... | collective-permute-start | bytes 3145736 | tf_op jit(solution)/shard_map/ppermute | solution.py:24
  149.8 10.9 %back.5 = (bf16[1024,512]{1,0:T(8,128)(2,1)}, f32[1024,1]{1,0:T(8,128)S(1)}) custom-call(s32[1]{0:T(128)} %bitcast.m_ref, bf16[1024,1792]{1,0:T(8,128)(2,1)} %get-tuple-element.35.a_ref, bf16[1024,1792]{1,0:T(8,128)(2,1)} %get-tuple-element.36.b_ref, bf16[1024,1792]{1,0:T(8,128)(2,1)} %get-tuple-element.37.c_ref, f32[8,1792]{1,0:T(8,128)S(1)} %get-tuple-element.48.g_in, ...), custom_call_target="tpu_custom_call" | custom-call | flops 1 | bytes 1 | tf_op jit(solution)/shard_map/back/pallas_call | solution.py:408
  163.4 3.3 %all-to-all-start.4 = ((f32[4,16,128]{2,1,0:T(8,128)}), f32[4,16,128]{2,1,0:T(8,128)S(1)}, u32[]{:S(2)}, u32[]{:S(2)}) async-start(f32[4,16,128]{2,1,0:T(8,128)} %broadcast_in_dim.51), calls=%async_computation.4 | async-start | bytes 65536 | tf_op jit(solution)/shard_map/all_to_all | solution.py:37
  166.7 6.2 %all-to-all-done.4 = f32[4,16,128]{2,1,0:T(8,128)S(1)} async-done(((f32[4,16,128]{2,1,0:T(8,128)}), f32[4,16,128]{2,1,0:T(8,128)S(1)}, u32[]{:S(2)}, u32[]{:S(2)}) %all-to-all-start.4) | async-done | bytes 32800 | tf_op jit(solution)/shard_map/all_to_all | solution.py:37
  173.5 4.1 %finish.1 = bf16[1024,512]{1,0:T(8,128)(2,1)} custom-call(bf16[1024,512]{1,0:T(8,128)(2,1)} %x_ref.1, bf16[1024,512]{1,0:T(8,128)(2,1)} %get-tuple-element.50.own_ref, bf16[1024,512]{1,0:T(8,128)(2,1)S(1)} %collective-permute-done.7.one_ref, bf16[1024,512]{1,0:T(8,128)(2,1)S(1)} %collective-permute-done.8.two_ref, f32[1024,1]{1,0:T(8,128)S(1)} %get-tuple-element.53.rms_ref, ...), custom_call_target="tpu_custom_call" | custom-call | tf_op jit(solution)/shard_map/finish/pallas_call | solution.py:474
  (104 shorter events, 15.1 us)
Async XLA Ops:
  7.2 31.6 %collective-permute-start = (bf16[1024,512]{1,0:T(8,128)(2,1)}, bf16[1024,512]{1,0:T(8,128)(2,1)S(1)}, u32[]{:S(2)}, u32[]{:S(2)}) collective-permute-start(bf16[1024,512]{1,0:T(8,128)(2,1)} %x_ref.1), channel_id=1, source_target_pairs={{0,3},{1,0},{2,1},{3,2},{4,7},{5,4},{6,5},{7,6},{8,11},{9,8},{10,9... | collective-permute-start | bytes 3145736 | tf_op jit(solution)/shard_map/ppermute | solution.py:24
  10.3 28.4 %collective-permute-start.1 = (bf16[1024,512]{1,0:T(8,128)(2,1)}, bf16[1024,512]{1,0:T(8,128)(2,1)S(1)}, u32[]{:S(2)}, u32[]{:S(2)}) collective-permute-start(bf16[1024,512]{1,0:T(8,128)(2,1)} %x_ref.1), channel_id=1, source_target_pairs={{0,1},{1,2},{2,3},{3,0},{4,5},{5,6},{6,7},{7,4},{8,9},{9,10},{10,1... | collective-permute-start | bytes 3145736 | tf_op jit(solution)/shard_map/ppermute | solution.py:24
  10.3 27.4 %all-to-all-start = ((bf16[4,32,512]{2,1,0:T(8,128)(2,1)}), bf16[4,32,512]{2,1,0:T(8,128)(2,1)S(1)}, u32[]{:S(2)}, u32[]{:S(2)}) async-start(bf16[4,32,512]{2,1,0:T(8,128)(2,1)} %bitcast.70), calls=%async_computation | async-start | bytes 262144 | tf_op jit(solution)/shard_map/all_to_all | solution.py:511
  14.8 69.5 %all-gather.3.cloned.1.call-start = ((), (), s32[]{:S(2)}) async-start(), calls=%async_computation.5 | async-start | bytes 2367488 | tf_op jit(solution)/shard_map/all_gather | solution.py:533
  17.5 8.7 %copy-start.9 = (s32[128]{0:T(128)S(1)}, s32[128]{0:T(128)}, u32[]{:S(2)}) copy-start(s32[128]{0:T(128)} %param.12) | copy-start | bytes 1540
  17.5 24.9 %copy-start.3 = (f32[2048]{0:T(1024)S(1)}, f32[2048]{0:T(1024)}, u32[]{:S(2)}) copy-start(f32[2048]{0:T(1024)} %param.14) | copy-start | bytes 24580
  38.7 3.7 %copy-start.4 = (bf16[1024,512]{1,0:T(8,128)(2,1)}, bf16[1024,512]{1,0:T(8,128)(2,1)S(1)}, u32[]{:S(2)}) copy-start(bf16[1024,512]{1,0:T(8,128)(2,1)S(1)} %collective-permute-done.refs_0_) | copy-start | bytes 3145732
  38.7 3.7 %copy-start.5 = (bf16[1024,512]{1,0:T(8,128)(2,1)}, bf16[1024,512]{1,0:T(8,128)(2,1)S(1)}, u32[]{:S(2)}) copy-start(bf16[1024,512]{1,0:T(8,128)(2,1)S(1)} %collective-permute-done.1.refs_1_) | copy-start | bytes 3145732
  38.8 36.8 %collective-permute-start.4 = (s32[8]{0:T(128)S(1)}, s32[8]{0:T(128)S(1)}, u32[]{:S(2)}, u32[]{:S(2)}) collective-permute-start(s32[8]{0:T(128)S(1)} %get-tuple-element.63), channel_id=1, source_target_pairs={{0,4},{4,0},{1,5},{5,1},{2,6},{6,2},{3,7},{7,3},{8,12},{12,8},{9,1... | collective-permute-start | bytes 104 | tf_op jit(solution)/shard_map/ppermute | solution.py:33
  39.0 18.4 %collective-permute-start.2 = (bf16[512,512]{1,0:T(8,128)(2,1)S(1)}, bf16[512,512]{1,0:T(8,128)(2,1)S(1)}, u32[]{:S(2)}, u32[]{:S(2)}) collective-permute-start(bf16[512,512]{1,0:T(8,128)(2,1)S(1)} %slice.47), channel_id=1, source_target_pairs={{0,1},{1,2},{2,3},{3,0},{4,5},{5,6},{6,7},{7,4},{8,9},{9,10},{10,1... | collective-permute-start | bytes 1572872 | tf_op jit(solution)/shard_map/ppermute | solution.py:24
  39.1 31.1 %slice-start = ((s8[7340032]{0:T(1024)(128)(4,1)}), s8[4194304]{0:T(1024)(128)(4,1)S(1)}, s32[]{:S(2)}) async-start(s8[7340032]{0:T(1024)(128)(4,1)} %bitcast.58), calls=%async_computation.6 | async-start | bytes 8388608
  39.1 18.3 %collective-permute-start.3 = (bf16[512,512]{1,0:T(8,128)(2,1)S(1)}, bf16[512,512]{1,0:T(8,128)(2,1)S(1)}, u32[]{:S(2)}, u32[]{:S(2)}) collective-permute-start(bf16[512,512]{1,0:T(8,128)(2,1)S(1)} %slice.48), channel_id=1, source_target_pairs={{0,3},{1,0},{2,1},{3,2},{4,7},{5,4},{6,5},{7,6},{8,11},{9,8},{10,9... | collective-permute-start | bytes 1572872 | tf_op jit(solution)/shard_map/ppermute | solution.py:24
  42.4 27.8 %slice-start.1 = ((s8[7340032]{0:T(1024)(128)(4,1)}), s8[3145728]{0:T(1024)(128)(4,1)S(1)}, s32[]{:S(2)}) async-start(s8[7340032]{0:T(1024)(128)(4,1)} %bitcast.58), calls=%async_computation.7 | async-start | bytes 6291456
  57.4 1.0 copy-start.7
  72.1 10.3 %all-to-all-start.1 = ((bf16[8,8,2048]{2,1,0:T(8,128)(2,1)}), bf16[8,8,2048]{2,1,0:T(8,128)(2,1)S(1)}, u32[]{:S(2)}, u32[]{:S(2)}) async-start(bf16[8,8,2048]{2,1,0:T(8,128)(2,1)} %broadcast_in_dim.21), calls=%async_computation.1 | async-start | bytes 524288 | tf_op jit(solution)/shard_map/all_to_all | solution.py:37
  84.3 17.7 %copy-start.8 = (bf16[512,2176]{1,0:T(8,128)(2,1)S(1)}, bf16[512,2176]{1,0:T(8,128)(2,1)}, u32[]{:S(2)}) copy-start(bf16[512,2176]{1,0:T(8,128)(2,1)} %all-gather.3.cloned.1.call-done) | copy-start | bytes 6684676
  103.3 10.4 %all-to-all-start.3 = ((bf16[8,8,2176]{2,1,0:T(8,128)(2,1)}), bf16[8,8,2176]{2,1,0:T(8,128)(2,1)S(1)}, u32[]{:S(2)}, u32[]{:S(2)}) async-start(bf16[8,8,2176]{2,1,0:T(8,128)(2,1)} %bitcast.20), calls=%async_computation.3 | async-start | bytes 557056 | tf_op jit(solution)/shard_map/all_to_all | solution.py:583
  114.0 3.1 %copy-start = (bf16[1792,2048]{1,0:T(8,128)(2,1)S(1)}, bf16[1792,2048]{1,0:T(8,128)(2,1)}, u32[]{:S(2)}) copy-start(bf16[1792,2048]{1,0:T(8,128)(2,1)} %refs_0_.3) | copy-start | bytes 22020100
  127.4 16.9 %collective-permute-start.5 = (bf16[512,512]{1,0:T(8,128)(2,1)}, bf16[512,512]{1,0:T(8,128)(2,1)S(1)}, u32[]{:S(2)}, u32[]{:S(2)}) collective-permute-start(bf16[512,512]{1,0:T(8,128)(2,1)} %get-tuple-element.44), channel_id=1, source_target_pairs={{0,1},{1,2},{2,3},{3,0},{4,5},{5,6},{6,7},{7,4},{8,9},{9,10},{10,1... | collective-permute-start | bytes 1572872 | tf_op jit(solution)/shard_map/ppermute | solution.py:24
  128.3 16.1 %collective-permute-start.6 = (bf16[512,512]{1,0:T(8,128)(2,1)}, bf16[512,512]{1,0:T(8,128)(2,1)S(1)}, u32[]{:S(2)}, u32[]{:S(2)}) collective-permute-start(bf16[512,512]{1,0:T(8,128)(2,1)} %get-tuple-element.45), channel_id=1, source_target_pairs={{0,3},{1,0},{2,1},{3,2},{4,7},{5,4},{6,5},{7,6},{8,11},{9,8},{10,9... | collective-permute-start | bytes 1572872 | tf_op jit(solution)/shard_map/ppermute | solution.py:24
  146.4 27.1 %collective-permute-start.7 = (bf16[1024,512]{1,0:T(8,128)(2,1)}, bf16[1024,512]{1,0:T(8,128)(2,1)S(1)}, u32[]{:S(2)}, u32[]{:S(2)}) collective-permute-start(bf16[1024,512]{1,0:T(8,128)(2,1)} %get-tuple-element.51), channel_id=1, source_target_pairs={{0,1},{1,2},{2,3},{3,0},{4,5},{5,6},{6,7},{7,4},{8,9},{9,10},{10,1... | collective-permute-start | bytes 3145736 | tf_op jit(solution)/shard_map/ppermute | solution.py:24
  146.4 27.1 %collective-permute-start.8 = (bf16[1024,512]{1,0:T(8,128)(2,1)}, bf16[1024,512]{1,0:T(8,128)(2,1)S(1)}, u32[]{:S(2)}, u32[]{:S(2)}) collective-permute-start(bf16[1024,512]{1,0:T(8,128)(2,1)} %get-tuple-element.52), channel_id=1, source_target_pairs={{0,3},{1,0},{2,1},{3,2},{4,7},{5,4},{6,5},{7,6},{8,11},{9,8},{10,9... | collective-permute-start | bytes 3145736 | tf_op jit(solution)/shard_map/ppermute | solution.py:24
  160.7 0.8 copy-start.1
  163.4 9.5 %all-to-all-start.4 = ((f32[4,16,128]{2,1,0:T(8,128)}), f32[4,16,128]{2,1,0:T(8,128)S(1)}, u32[]{:S(2)}, u32[]{:S(2)}) async-start(f32[4,16,128]{2,1,0:T(8,128)} %broadcast_in_dim.51), calls=%async_computation.4 | async-start | bytes 65536 | tf_op jit(solution)/shard_map/all_to_all | solution.py:37
  (2 other events, 1.5 us)
Sparse Core Ops, SparseCore 0:
  38.9 45.3 all-gather.2

commit v7 on v6

--- a/solution.py
+++ b/solution.py
@@ -338,11 +338,13 @@
 
     if first:
 
+        step = ff // 2
+
         def dact_tile(n):
-            at = pl.ds(pl.multiple_of(n * FT, FT), FT)
+            at = pl.ds(pl.multiple_of(n * step, L), step)
             g_ref[:, at] = contract_rows(wd_ref[at], g_in[...]).T
 
-        each(ff // FT, dact_tile)
+        each(2, dact_tile)
         source = g_ref
     else:
         source = g_in
@@ -430,12 +432,11 @@
 
 def add_halves(right, left, from_left, from_right):
     half, part = from_left.shape
-    rt = half // 2
-    upper = pl.BlockSpec((rt, part), lambda r: (r, 0))
-    lower = pl.BlockSpec((rt, part), lambda r: (r + 2, 0))
+    upper = pl.BlockSpec((half, part), lambda r: (0, 0))
+    lower = pl.BlockSpec((half, part), lambda r: (1, 0))
     return pl.pallas_call(
         add_kernel,
-        grid=(2,),
+        grid=(1,),
         in_specs=[lower, upper, upper, upper],
         out_specs=[lower, upper],
         out_shape=[pltpu.HBM(right.shape, bf16)] * 2,
@@ -468,7 +469,7 @@
 
 def finish(x, own, one, two, rms, inner, mask, token, gain):
     rows, part = x.shape
-    rt = 256
+    rt = 512
     whole = pl.BlockSpec((rt, part), lambda r: (r, 0))
     column = pl.BlockSpec((rt, 1), lambda r: (r, 0))
     return pl.pallas_call(
@@ -508,9 +509,18 @@
     chip = lax.axis_index(("x", "z"))
     m = mi.astype(jnp.int32).reshape(1)
 
-    mine = lax.all_to_all(
-        queries.reshape(MP, share, part), "mp", split_axis=0, concat_axis=0, tiled=True
+    def share_of(k):
+        return lax.dynamic_slice_in_dim(queries, lax.rem(mi + k, MP) * share, share)
+
+    mine = jnp.stack(
+        [
+            share_of(0),
+            shifted(share_of(3), -1),
+            shifted(share_of(2), 2),
+            shifted(share_of(1), 1),
+        ]
     )
+    mine = lax.dynamic_slice_in_dim(jnp.concatenate([mine, mine], axis=0), MP - mi, MP)
     mine = jnp.moveaxis(mine, 0, 1).reshape(share, width)
     own_positive = lax.dynamic_slice_in_dim(positive_doc, mi * share, share)
     square = jnp.sum(mine.astype(f32) ** 2, axis=1)
@@ -589,7 +599,7 @@
 
     tensors = (w_gate, w_up, w_down)
     none = jnp.zeros((2 * passes, pool.shape[1]), bf16)
-    high, low, g = back(m, (2,), 256, True, a, b, c, token_grad, none, *tensors)
+    high, low, g = back(m, (2,), 512, True, a, b, c, token_grad, none, *tensors)
     from_right = shifted(high, -1)
     from_left = shifted(low, 1)
     right, left = back(m, (1, 3), 512, False, a, b, c, g, none, *tensors)
@@ -604,7 +614,7 @@
         [s.reshape(passes, L), jnp.pad(own_loss[None, :], ((0, 7), (0, L - share)))], axis=0
     )
     small = copies_to_all(small, "mp", MP)
-    inner = small[:, :passes].sum(axis=0).reshape(passes // 2, 2, L) / width
+    inner = small[:, :passes].sum(axis=0).reshape(passes // 4, 4, L) / width
     query_loss = small[:, passes, :share].reshape(MP * share)
     own_gain = lax.dynamic_slice_in_dim(norm_gain, mi * part, part)[None, :]
     own_token = lax.dynamic_slice_in_dim(token_grad, mi * part, part, axis=1).astype(f32)

time: 185 us -> 185 us (level)
  local copies, waits for them, and re-layouts: 10.1 us -> 13 us
  waiting for transfers between devices: 33 us -> 30.8 us
    all_to_all x1 -> x0, waiting for transfers between devices: 11.4 us -> none  [per_device(): lax.all_to_all(queries.reshape(MP, share, part), 'mp', split_axis=0, conc...]
    ppermute x8 -> x11, waiting for transfers between devices: 0.02 us -> 9.6 us  [shifted(): return lax.ppermute(x, 'mp', [(i, (i + by) % MP) for i in range(MP)])]
    all_to_all x1 -> x0, starting transfers between devices: 4.5 us -> none  [per_device(): lax.all_to_all(queries.reshape(MP, share, part), 'mp', split_axis=0, conc...]
    ppermute x8 -> x11, starting transfers between devices: 13.1 us -> 17.2 us  [shifted(): return lax.ppermute(x, 'mp', [(i, (i + by) % MP) for i in range(MP)])]
    unnamed x26 -> x34, local copies, waits for them, and re-layouts: 5.69 us -> 7.16 us
  transfers between devices with their start and end apart: 14 -> 16, of which waited for: 5 -> 7; matrix products, arithmetic and copies ran while one was open for 4% -> 6% of each run, Pallas kernels for 32% -> 33%
where the time goes in v7:
time: 185 us; the launch traced here: 184 us
  Pallas kernels  75.1 us (41%)
  waiting for transfers between devices  30.8 us (17%)
  starting transfers between devices  27.5 us (15%)
  between operations  14.5 us (8%)
  blocking collectives  13.8 us (7%)
  local copies, waits for them, and re-layouts  13 us (7%)
  other arithmetic  5.52 us (3%)
  matrix products  3.77 us (2%)
    pallas_call x3, Pallas kernels, back(): pl.pallas_call(functools.partial(back_kernel, steps, first), in_specs=[sm...  33.8 us
    pallas_call x2, Pallas kernels, encode_near(): pl.pallas_call(functools.partial(encode_near_kernel, steps), in_specs=[sm...  23.6 us
    ppermute x11, starting transfers between devices, shifted(): return lax.ppermute(x, 'mp', [(i, (i + by) % MP) for i in range(MP)])  17.2 us
    all_to_all x1, blocking collectives, copies_to_all(): lax.all_to_all(jnp.broadcast_to(x, (count, *x.shape)), axes, split_axis=0...  13.8 us
    all_to_all x2, waiting for transfers between devices, copies_to_all(): lax.all_to_all(jnp.broadcast_to(x, (count, *x.shape)), axes, split_axis=0...  12.9 us
    pallas_call x1, Pallas kernels, encode_far(): pl.pallas_call(encode_far_kernel, in_specs=[smem] + [anywhere] * 3 + [vme...  12.1 us
    ppermute x11, waiting for transfers between devices, shifted(): return lax.ppermute(x, 'mp', [(i, (i + by) % MP) for i in range(MP)])  9.6 us
    unnamed x34, local copies, waits for them, and re-layouts  7.16 us
  transfers between devices with their start and end apart: 16, of which 7 were waited for; matrix products, arithmetic and copies ran while one was open for 6% of the time, Pallas kernels for 33%

profile of v7, /device:TPU:0, one launch (start us, length us, event | category | flops | bytes accessed | tf_op | source)
XLA Modules:
  0.0 184.0 jit_solution(6994245532637068229)
XLA Ops:
  7.2 3.2 %collective-permute-start = (bf16[1024,512]{1,0:T(8,128)(2,1)}, bf16[1024,512]{1,0:T(8,128)(2,1)S(1)}, u32[]{:S(2)}, u32[]{:S(2)}) collective-permute-start(bf16[1024,512]{1,0:T(8,128)(2,1)} %x_ref.1), channel_id=1, source_target_pairs={{0,3},{1,0},{2,1},{3,2},{4,7},{5,4},{6,5},{7,6},{8,11},{9,8},{10,9... | collective-permute-start | bytes 3145736 | tf_op jit(solution)/shard_map/ppermute | solution.py:24
  11.8 3.2 %collective-permute-start.2 = (bf16[32,512]{1,0:T(8,128)(2,1)}, bf16[32,512]{1,0:T(8,128)(2,1)S(1)}, u32[]{:S(2)}, u32[]{:S(2)}) collective-permute-start(bf16[32,512]{1,0:T(8,128)(2,1)} %get-tuple-element.70), channel_id=1, source_target_pairs={{0,3},{1,0},{2,1},{3,2},{4,7},{5,4},{6,5},{7,6},{8,11},{9,8},{10,9... | collective-permute-start | bytes 98312 | tf_op jit(solution)/shard_map/ppermute | solution.py:24
  19.4 8.8 %encode_near.2 = (f32[7,1024,512]{2,1,0:T(8,128)}, f32[1024,1]{1,0:T(8,128)S(1)}, f32[8,512]{1,0:T(8,128)S(1)}) custom-call(s32[1]{0:T(128)} %bitcast.m_ref, bf16[1024,512]{1,0:T(8,128)(2,1)} %x_ref.1, f32[4,1,512]{2,1,0:T(1,128)S(1)} %bitcast.72, bf16[2048,1792]{1,0:T(8,128)(2,1)} %wg_ref.7, bf16[2048,1792]{1,0:T(8,128)(2,1)} %wu_ref.7, ...), custom_call_target="tpu_custom_call" | custom-call | flops 3758096384 | bytes 8388608 | tf_op jit(solution)/shard_map/encode_near/pallas_call | solution.py:150
  28.2 6.3 %collective-permute-done.2 = bf16[32,512]{1,0:T(8,128)(2,1)S(1)} collective-permute-done((bf16[32,512]{1,0:T(8,128)(2,1)}, bf16[32,512]{1,0:T(8,128)(2,1)S(1)}, u32[]{:S(2)}, u32[]{:S(2)}) %collective-permute-start.2) | collective-permute-done | bytes 32800 | tf_op jit(solution)/shard_map/ppermute | solution.py:24
  34.5 2.0 %collective-permute-done.3 = bf16[32,512]{1,0:T(8,128)(2,1)S(1)} collective-permute-done((bf16[32,512]{1,0:T(8,128)(2,1)}, bf16[32,512]{1,0:T(8,128)(2,1)S(1)}, u32[]{:S(2)}, u32[]{:S(2)}) %collective-permute-start.3) | collective-permute-done | bytes 32800 | tf_op jit(solution)/shard_map/ppermute | solution.py:24
  40.0 3.3 %collective-permute-start.6 = (bf16[512,512]{1,0:T(8,128)(2,1)S(1)}, bf16[512,512]{1,0:T(8,128)(2,1)S(1)}, u32[]{:S(2)}, u32[]{:S(2)}) collective-permute-start(bf16[512,512]{1,0:T(8,128)(2,1)S(1)} %slice.48), channel_id=1, source_target_pairs={{0,3},{1,0},{2,1},{3,2},{4,7},{5,4},{6,5},{7,6},{8,11},{9,8},{10,9... | collective-permute-start | bytes 1572872 | tf_op jit(solution)/shard_map/ppermute | solution.py:24
  43.3 14.9 %encode_near.3 = (f32[7,1024,512]{2,1,0:T(8,128)}, f32[1024,1]{1,0:T(8,128)S(1)}) custom-call(s32[1]{0:T(128)} %bitcast.m_ref, bf16[1024,512]{1,0:T(8,128)(2,1)} %copy-done.4, bf16[1024,512]{1,0:T(8,128)(2,1)} %copy-done.5, f32[4,1,512]{2,1,0:T(1,128)S(1)} %bitcast.73, bf16[2048,1792]{1,0:T(8,128)(2,1)} %wg_ref.7, bf16[2048,1792]{1,0:T(8,128)(2,1)} %wu_ref.7, ...), custom_call_target="tpu_custom_call" | custom-call | flops 7516192768 | bytes 8388608 | tf_op jit(solution)/shard_map/encode_near/pallas_call | solution.py:150
  59.2 12.1 %encode_far.1 = (bf16[1024,1792]{1,0:T(8,128)(2,1)}, bf16[1024,1792]{1,0:T(8,128)(2,1)}, bf16[1024,1792]{1,0:T(8,128)(2,1)}, f32[7,8,256]{2,1,0:T(8,128)S(1)}, f32[1024,1]{1,0:T(8,128)S(1)}) custom-call(s32[1]{0:T(128)} %bitcast.m_ref, bf16[512,512]{1,0:T(8,128)(2,1)} %copy-done.6, bf16[512,512]{1,0:T(8,128)(2,1)} %copy-done.7, ...), custom_call_target="tpu_custom_call" | custom-call | flops 3758096384 | bytes 11010048 | tf_op jit(solution)/shard_map/encode_far/pallas_call | solution.py:260
  73.2 3.4 %all-to-all-start = ((bf16[8,8,2048]{2,1,0:T(8,128)(2,1)}), bf16[8,8,2048]{2,1,0:T(8,128)(2,1)S(1)}, u32[]{:S(2)}, u32[]{:S(2)}) async-start(bf16[8,8,2048]{2,1,0:T(8,128)(2,1)} %broadcast_in_dim.21), calls=%async_computation | async-start | bytes 524288 | tf_op jit(solution)/shard_map/all_to_all | solution.py:37
  76.8 6.7 %all-to-all-done = bf16[8,8,2048]{2,1,0:T(8,128)(2,1)S(1)} async-done(((bf16[8,8,2048]{2,1,0:T(8,128)(2,1)}), bf16[8,8,2048]{2,1,0:T(8,128)(2,1)S(1)}, u32[]{:S(2)}, u32[]{:S(2)}) %all-to-all-start) | async-done | bytes 262176 | tf_op jit(solution)/shard_map/all_to_all | solution.py:37
  86.8 2.3 %fusion.19 = (f32[512]{0:T(512)S(1)}, f32[512]{0:T(512)S(1)}, f32[16,512]{1,0:T(8,128)S(1)}) fusion(f32[16]{0:T(128)S(1)} %rsqrt.32, f32[512]{0:T(512)S(1)} %get-tuple-element.55, f32[16]{0:T(128)S(1)} %fusion.24, f32[16]{0:T(128)S(1)} %fusion.27, f32[512]{0:T(512)S(1)} %get-tuple-element.56, bf16[512,2176]{1,0:T(8,128)(2,1)} %all-gather.3.cloned.1.call-done, ...), kind=kOutput, calls=%fused_computation.49 | convolution fusion | flops 33610752 | bytes 2203840 | tf_op jit(solution)/shard_map/dot_general | solution.py:47
  89.1 13.8 %all_to_all.20 = f32[16,8,128]{2,1,0:T(8,128)S(1)} all-to-all(f32[16,8,128]{2,1,0:T(8,128)S(1)} %broadcast_in_dim.22), channel_id=1, replica_groups=mesh['x'=4,'z'=4,'core'=2,'mp'=4] {'x','z'}, dimensions={0} | all-to-all | bytes 131072 | tf_op jit(solution)/shard_map/all_to_all | solution.py:37
  104.4 3.6 %all-to-all-start.2 = ((bf16[8,8,2176]{2,1,0:T(8,128)(2,1)}), bf16[8,8,2176]{2,1,0:T(8,128)(2,1)S(1)}, u32[]{:S(2)}, u32[]{:S(2)}) async-start(bf16[8,8,2176]{2,1,0:T(8,128)(2,1)} %bitcast.23), calls=%async_computation.2 | async-start | bytes 557056 | tf_op jit(solution)/shard_map/all_to_all | solution.py:593
  108.1 6.8 %all-to-all-done.2 = bf16[8,8,2176]{2,1,0:T(8,128)(2,1)S(1)} async-done(((bf16[8,8,2176]{2,1,0:T(8,128)(2,1)}), bf16[8,8,2176]{2,1,0:T(8,128)(2,1)S(1)}, u32[]{:S(2)}, u32[]{:S(2)}) %all-to-all-start.2) | async-done | bytes 278560 | tf_op jit(solution)/shard_map/all_to_all | solution.py:593
  115.2 3.1 %copy-done = bf16[1792,2048]{1,0:T(8,128)(2,1)S(1)} copy-done((bf16[1792,2048]{1,0:T(8,128)(2,1)S(1)}, bf16[1792,2048]{1,0:T(8,128)(2,1)}, u32[]{:S(2)}) %copy-start) | copy-done | bytes 7340056
  118.3 9.3 %back.3 = (bf16[512,512]{1,0:T(8,128)(2,1)}, bf16[512,512]{1,0:T(8,128)(2,1)}, f32[8,1792]{1,0:T(8,128)S(1)}) custom-call(s32[1]{0:T(128)} %bitcast.m_ref, bf16[1024,1792]{1,0:T(8,128)(2,1)} %get-tuple-element.35.a_ref, bf16[1024,1792]{1,0:T(8,128)(2,1)} %get-tuple-element.36.b_ref, bf16[1024,1792]{1,0:T(8,128)(2,1)} %get-tuple-element.37.c_ref, ...), custom_call_target="tpu_custom_call" | custom-call | flops 1 | bytes 1 | tf_op jit(solution)/shard_map/back/pallas_call | solution.py:410
  128.5 2.4 %collective-permute-start.9 = (bf16[512,512]{1,0:T(8,128)(2,1)}, bf16[512,512]{1,0:T(8,128)(2,1)S(1)}, u32[]{:S(2)}, u32[]{:S(2)}) collective-permute-start(bf16[512,512]{1,0:T(8,128)(2,1)} %get-tuple-element.45), channel_id=1, source_target_pairs={{0,3},{1,0},{2,1},{3,2},{4,7},{5,4},{6,5},{7,6},{8,11},{9,8},{10,9... | collective-permute-start | bytes 1572872 | tf_op jit(solution)/shard_map/ppermute | solution.py:24
  131.0 13.5 %back.4 = (bf16[1024,512]{1,0:T(8,128)(2,1)}, bf16[1024,512]{1,0:T(8,128)(2,1)}) custom-call(s32[1]{0:T(128)} %bitcast.m_ref, bf16[1024,1792]{1,0:T(8,128)(2,1)} %get-tuple-element.35.a_ref, bf16[1024,1792]{1,0:T(8,128)(2,1)} %get-tuple-element.36.b_ref, bf16[1024,1792]{1,0:T(8,128)(2,1)} %get-tuple-element.37.c_ref, f32[8,1792]{1,0:T(8,128)S(1)} %get-tuple-element.48.g_in, ...), custom_call_target="tpu_custom_call" | custom-call | flops 1 | bytes 1 | tf_op jit(solution)/shard_map/back/pallas_call | solution.py:410
  144.5 2.3 %add_halves.1 = (bf16[1024,512]{1,0:T(8,128)(2,1)}, bf16[1024,512]{1,0:T(8,128)(2,1)}) custom-call(bf16[1024,512]{1,0:T(8,128)(2,1)} %get-tuple-element.42.right_ref, bf16[1024,512]{1,0:T(8,128)(2,1)} %get-tuple-element.43.left_ref, bf16[512,512]{1,0:T(8,128)(2,1)S(1)} %collective-permute-done.8.from_left_ref, ...), custom_call_target="tpu_custom_call", output_to_operand_aliasing={{0}: (0, {}), {1}: (1, {})} | custom-call | flops 1 | bytes 1 | tf_op jit(solution)/shard_map/add_halves/pallas_call | solution.py:437
  146.9 3.2 %collective-permute-start.11 = (bf16[1024,512]{1,0:T(8,128)(2,1)}, bf16[1024,512]{1,0:T(8,128)(2,1)S(1)}, u32[]{:S(2)}, u32[]{:S(2)}) collective-permute-start(bf16[1024,512]{1,0:T(8,128)(2,1)} %get-tuple-element.52), channel_id=1, source_target_pairs={{0,3},{1,0},{2,1},{3,2},{4,7},{5,4},{6,5},{7,6},{8,11},{9,8},{10,9... | collective-permute-start | bytes 3145736 | tf_op jit(solution)/shard_map/ppermute | solution.py:24
  150.2 10.9 %back.5 = (bf16[1024,512]{1,0:T(8,128)(2,1)}, f32[1024,1]{1,0:T(8,128)S(1)}) custom-call(s32[1]{0:T(128)} %bitcast.m_ref, bf16[1024,1792]{1,0:T(8,128)(2,1)} %get-tuple-element.35.a_ref, bf16[1024,1792]{1,0:T(8,128)(2,1)} %get-tuple-element.36.b_ref, bf16[1024,1792]{1,0:T(8,128)(2,1)} %get-tuple-element.37.c_ref, f32[8,1792]{1,0:T(8,128)S(1)} %get-tuple-element.48.g_in, ...), custom_call_target="tpu_custom_call" | custom-call | flops 1 | bytes 1 | tf_op jit(solution)/shard_map/back/pallas_call | solution.py:410
  163.8 3.3 %all-to-all-start.3 = ((f32[4,16,128]{2,1,0:T(8,128)}), f32[4,16,128]{2,1,0:T(8,128)S(1)}, u32[]{:S(2)}, u32[]{:S(2)}) async-start(f32[4,16,128]{2,1,0:T(8,128)} %broadcast_in_dim.51), calls=%async_computation.3 | async-start | bytes 65536 | tf_op jit(solution)/shard_map/all_to_all | solution.py:37
  167.1 6.1 %all-to-all-done.3 = f32[4,16,128]{2,1,0:T(8,128)S(1)} async-done(((f32[4,16,128]{2,1,0:T(8,128)}), f32[4,16,128]{2,1,0:T(8,128)S(1)}, u32[]{:S(2)}, u32[]{:S(2)}) %all-to-all-start.3) | async-done | bytes 32800 | tf_op jit(solution)/shard_map/all_to_all | solution.py:37
  173.9 3.2 %finish.1 = bf16[1024,512]{1,0:T(8,128)(2,1)} custom-call(bf16[1024,512]{1,0:T(8,128)(2,1)} %x_ref.1, bf16[1024,512]{1,0:T(8,128)(2,1)} %get-tuple-element.50.own_ref, bf16[1024,512]{1,0:T(8,128)(2,1)S(1)} %collective-permute-done.10.one_ref, bf16[1024,512]{1,0:T(8,128)(2,1)S(1)} %collective-permute-done.11.two_ref, ...), custom_call_target="tpu_custom_call" | custom-call | tf_op jit(solution)/shard_map/finish/pallas_call | solution.py:475
  (118 shorter events, 21.7 us)
Async XLA Ops:
  7.2 78.1 %all-gather.3.cloned.1.call-start = ((), (), s32[]{:S(2)}) async-start(), calls=%async_computation.4 | async-start | bytes 2367488 | tf_op jit(solution)/shard_map/all_gather | solution.py:543
  7.2 32.4 %collective-permute-start = (bf16[1024,512]{1,0:T(8,128)(2,1)}, bf16[1024,512]{1,0:T(8,128)(2,1)S(1)}, u32[]{:S(2)}, u32[]{:S(2)}) collective-permute-start(bf16[1024,512]{1,0:T(8,128)(2,1)} %x_ref.1), channel_id=1, source_target_pairs={{0,3},{1,0},{2,1},{3,2},{4,7},{5,4},{6,5},{7,6},{8,11},{9,8},{10,9... | collective-permute-start | bytes 3145736 | tf_op jit(solution)/shard_map/ppermute | solution.py:24
  10.4 29.2 %collective-permute-start.1 = (bf16[1024,512]{1,0:T(8,128)(2,1)}, bf16[1024,512]{1,0:T(8,128)(2,1)S(1)}, u32[]{:S(2)}, u32[]{:S(2)}) collective-permute-start(bf16[1024,512]{1,0:T(8,128)(2,1)} %x_ref.1), channel_id=1, source_target_pairs={{0,1},{1,2},{2,3},{3,0},{4,5},{5,6},{6,7},{7,4},{8,9},{9,10},{10,1... | collective-permute-start | bytes 3145736 | tf_op jit(solution)/shard_map/ppermute | solution.py:24
  11.8 22.7 %collective-permute-start.2 = (bf16[32,512]{1,0:T(8,128)(2,1)}, bf16[32,512]{1,0:T(8,128)(2,1)S(1)}, u32[]{:S(2)}, u32[]{:S(2)}) collective-permute-start(bf16[32,512]{1,0:T(8,128)(2,1)} %get-tuple-element.70), channel_id=1, source_target_pairs={{0,3},{1,0},{2,1},{3,2},{4,7},{5,4},{6,5},{7,6},{8,11},{9,8},{10,9... | collective-permute-start | bytes 98312 | tf_op jit(solution)/shard_map/ppermute | solution.py:24
  15.0 21.5 %collective-permute-start.3 = (bf16[32,512]{1,0:T(8,128)(2,1)}, bf16[32,512]{1,0:T(8,128)(2,1)S(1)}, u32[]{:S(2)}, u32[]{:S(2)}) collective-permute-start(bf16[32,512]{1,0:T(8,128)(2,1)} %get-tuple-element.71), channel_id=1, source_target_pairs={{0,2},{1,3},{2,0},{3,1},{4,6},{5,7},{6,4},{7,5},{8,10},{9,11},{10,... | collective-permute-start | bytes 98312 | tf_op jit(solution)/shard_map/ppermute | solution.py:24
  15.0 22.8 %collective-permute-start.4 = (bf16[32,512]{1,0:T(8,128)(2,1)}, bf16[32,512]{1,0:T(8,128)(2,1)S(1)}, u32[]{:S(2)}, u32[]{:S(2)}) collective-permute-start(bf16[32,512]{1,0:T(8,128)(2,1)} %get-tuple-element.69), channel_id=1, source_target_pairs={{0,1},{1,2},{2,3},{3,0},{4,5},{5,6},{6,7},{7,4},{8,9},{9,10},{10,1... | collective-permute-start | bytes 98312 | tf_op jit(solution)/shard_map/ppermute | solution.py:24
  19.4 8.8 %copy-start.9 = (s32[128]{0:T(128)S(1)}, s32[128]{0:T(128)}, u32[]{:S(2)}) copy-start(s32[128]{0:T(128)} %param.12) | copy-start | bytes 1540
  28.1 15.1 %copy-start.3 = (f32[2048]{0:T(1024)S(1)}, f32[2048]{0:T(1024)}, u32[]{:S(2)}) copy-start(f32[2048]{0:T(1024)} %param.14) | copy-start | bytes 24580
  39.6 3.7 %copy-start.4 = (bf16[1024,512]{1,0:T(8,128)(2,1)}, bf16[1024,512]{1,0:T(8,128)(2,1)S(1)}, u32[]{:S(2)}) copy-start(bf16[1024,512]{1,0:T(8,128)(2,1)S(1)} %collective-permute-done.refs_0_) | copy-start | bytes 3145732
  39.6 3.7 %copy-start.5 = (bf16[1024,512]{1,0:T(8,128)(2,1)}, bf16[1024,512]{1,0:T(8,128)(2,1)S(1)}, u32[]{:S(2)}) copy-start(bf16[1024,512]{1,0:T(8,128)(2,1)S(1)} %collective-permute-done.1.refs_1_) | copy-start | bytes 3145732
  39.6 37.0 %collective-permute-start.7 = (s32[8]{0:T(128)S(1)}, s32[8]{0:T(128)S(1)}, u32[]{:S(2)}, u32[]{:S(2)}) collective-permute-start(s32[8]{0:T(128)S(1)} %get-tuple-element.63), channel_id=1, source_target_pairs={{0,4},{4,0},{1,5},{5,1},{2,6},{6,2},{3,7},{7,3},{8,12},{12,8},{9,1... | collective-permute-start | bytes 104 | tf_op jit(solution)/shard_map/ppermute | solution.py:33
  39.9 18.3 %collective-permute-start.5 = (bf16[512,512]{1,0:T(8,128)(2,1)S(1)}, bf16[512,512]{1,0:T(8,128)(2,1)S(1)}, u32[]{:S(2)}, u32[]{:S(2)}) collective-permute-start(bf16[512,512]{1,0:T(8,128)(2,1)S(1)} %slice.47), channel_id=1, source_target_pairs={{0,1},{1,2},{2,3},{3,0},{4,5},{5,6},{6,7},{7,4},{8,9},{9,10},{10,1... | collective-permute-start | bytes 1572872 | tf_op jit(solution)/shard_map/ppermute | solution.py:24
  39.9 31.4 %slice-start = ((s8[7340032]{0:T(1024)(128)(4,1)}), s8[4194304]{0:T(1024)(128)(4,1)S(1)}, s32[]{:S(2)}) async-start(s8[7340032]{0:T(1024)(128)(4,1)} %bitcast.70), calls=%async_computation.5 | async-start | bytes 8388608
  40.0 18.2 %collective-permute-start.6 = (bf16[512,512]{1,0:T(8,128)(2,1)S(1)}, bf16[512,512]{1,0:T(8,128)(2,1)S(1)}, u32[]{:S(2)}, u32[]{:S(2)}) collective-permute-start(bf16[512,512]{1,0:T(8,128)(2,1)S(1)} %slice.48), channel_id=1, source_target_pairs={{0,3},{1,0},{2,1},{3,2},{4,7},{5,4},{6,5},{7,6},{8,11},{9,8},{10,9... | collective-permute-start | bytes 1572872 | tf_op jit(solution)/shard_map/ppermute | solution.py:24
  43.3 28.1 %slice-start.1 = ((s8[7340032]{0:T(1024)(128)(4,1)}), s8[3145728]{0:T(1024)(128)(4,1)S(1)}, s32[]{:S(2)}) async-start(s8[7340032]{0:T(1024)(128)(4,1)} %bitcast.70), calls=%async_computation.6 | async-start | bytes 6291456
  73.2 10.3 %all-to-all-start = ((bf16[8,8,2048]{2,1,0:T(8,128)(2,1)}), bf16[8,8,2048]{2,1,0:T(8,128)(2,1)S(1)}, u32[]{:S(2)}, u32[]{:S(2)}) async-start(bf16[8,8,2048]{2,1,0:T(8,128)(2,1)} %broadcast_in_dim.21), calls=%async_computation | async-start | bytes 524288 | tf_op jit(solution)/shard_map/all_to_all | solution.py:37
  85.2 17.9 %copy-start.8 = (bf16[512,2176]{1,0:T(8,128)(2,1)S(1)}, bf16[512,2176]{1,0:T(8,128)(2,1)}, u32[]{:S(2)}) copy-start(bf16[512,2176]{1,0:T(8,128)(2,1)} %all-gather.3.cloned.1.call-done) | copy-start | bytes 6684676
  104.4 10.4 %all-to-all-start.2 = ((bf16[8,8,2176]{2,1,0:T(8,128)(2,1)}), bf16[8,8,2176]{2,1,0:T(8,128)(2,1)S(1)}, u32[]{:S(2)}, u32[]{:S(2)}) async-start(bf16[8,8,2176]{2,1,0:T(8,128)(2,1)} %bitcast.23), calls=%async_computation.2 | async-start | bytes 557056 | tf_op jit(solution)/shard_map/all_to_all | solution.py:593
  115.2 3.1 %copy-start = (bf16[1792,2048]{1,0:T(8,128)(2,1)S(1)}, bf16[1792,2048]{1,0:T(8,128)(2,1)}, u32[]{:S(2)}) copy-start(bf16[1792,2048]{1,0:T(8,128)(2,1)} %refs_0_.3) | copy-start | bytes 22020100
  127.6 16.9 %collective-permute-start.8 = (bf16[512,512]{1,0:T(8,128)(2,1)}, bf16[512,512]{1,0:T(8,128)(2,1)S(1)}, u32[]{:S(2)}, u32[]{:S(2)}) collective-permute-start(bf16[512,512]{1,0:T(8,128)(2,1)} %get-tuple-element.44), channel_id=1, source_target_pairs={{0,1},{1,2},{2,3},{3,0},{4,5},{5,6},{6,7},{7,4},{8,9},{9,10},{10,1... | collective-permute-start | bytes 1572872 | tf_op jit(solution)/shard_map/ppermute | solution.py:24
  128.5 16.0 %collective-permute-start.9 = (bf16[512,512]{1,0:T(8,128)(2,1)}, bf16[512,512]{1,0:T(8,128)(2,1)S(1)}, u32[]{:S(2)}, u32[]{:S(2)}) collective-permute-start(bf16[512,512]{1,0:T(8,128)(2,1)} %get-tuple-element.45), channel_id=1, source_target_pairs={{0,3},{1,0},{2,1},{3,2},{4,7},{5,4},{6,5},{7,6},{8,11},{9,8},{10,9... | collective-permute-start | bytes 1572872 | tf_op jit(solution)/shard_map/ppermute | solution.py:24
  146.9 27.0 %collective-permute-start.10 = (bf16[1024,512]{1,0:T(8,128)(2,1)}, bf16[1024,512]{1,0:T(8,128)(2,1)S(1)}, u32[]{:S(2)}, u32[]{:S(2)}) collective-permute-start(bf16[1024,512]{1,0:T(8,128)(2,1)} %get-tuple-element.51), channel_id=1, source_target_pairs={{0,1},{1,2},{2,3},{3,0},{4,5},{5,6},{6,7},{7,4},{8,9},{9,10},{10,1... | collective-permute-start | bytes 3145736 | tf_op jit(solution)/shard_map/ppermute | solution.py:24
  146.9 27.0 %collective-permute-start.11 = (bf16[1024,512]{1,0:T(8,128)(2,1)}, bf16[1024,512]{1,0:T(8,128)(2,1)S(1)}, u32[]{:S(2)}, u32[]{:S(2)}) collective-permute-start(bf16[1024,512]{1,0:T(8,128)(2,1)} %get-tuple-element.52), channel_id=1, source_target_pairs={{0,3},{1,0},{2,1},{3,2},{4,7},{5,4},{6,5},{7,6},{8,11},{9,8},{10,9... | collective-permute-start | bytes 3145736 | tf_op jit(solution)/shard_map/ppermute | solution.py:24
  163.8 9.5 %all-to-all-start.3 = ((f32[4,16,128]{2,1,0:T(8,128)}), f32[4,16,128]{2,1,0:T(8,128)S(1)}, u32[]{:S(2)}, u32[]{:S(2)}) async-start(f32[4,16,128]{2,1,0:T(8,128)} %broadcast_in_dim.51), calls=%async_computation.3 | async-start | bytes 65536 | tf_op jit(solution)/shard_map/all_to_all | solution.py:37
  (4 other events, 3.2 us)
Sparse Core Ops, SparseCore 0:
  39.7 45.4 all-gather.2

commit v8 on v7

--- a/solution.py
+++ b/solution.py
@@ -432,11 +432,12 @@
 
 def add_halves(right, left, from_left, from_right):
     half, part = from_left.shape
-    upper = pl.BlockSpec((half, part), lambda r: (0, 0))
-    lower = pl.BlockSpec((half, part), lambda r: (1, 0))
+    rt = half // 2
+    upper = pl.BlockSpec((rt, part), lambda r: (r, 0))
+    lower = pl.BlockSpec((rt, part), lambda r: (r + 2, 0))
     return pl.pallas_call(
         add_kernel,
-        grid=(1,),
+        grid=(2,),
         in_specs=[lower, upper, upper, upper],
         out_specs=[lower, upper],
         out_shape=[pltpu.HBM(right.shape, bf16)] * 2,
@@ -512,14 +513,9 @@
     def share_of(k):
         return lax.dynamic_slice_in_dim(queries, lax.rem(mi + k, MP) * share, share)
 
-    mine = jnp.stack(
-        [
-            share_of(0),
-            shifted(share_of(3), -1),
-            shifted(share_of(2), 2),
-            shifted(share_of(1), 1),
-        ]
-    )
+    opposite = shifted(share_of(2), 2)
+    from_right, from_left = shifted(share_of(3), -1), shifted(share_of(1), 1)
+    mine = jnp.stack([share_of(0), from_right, opposite, from_left])
     mine = lax.dynamic_slice_in_dim(jnp.concatenate([mine, mine], axis=0), MP - mi, MP)
     mine = jnp.moveaxis(mine, 0, 1).reshape(share, width)
     own_positive = lax.dynamic_slice_in_dim(positive_doc, mi * share, share)

time: 185 us -> 185 us (level)
  no operation moved by 1% of the time
where the time goes in v8:
time: 185 us; the launch traced here: 184 us
  Pallas kernels  74.9 us (40%)
  waiting for transfers between devices  30.8 us (17%)
  starting transfers between devices  27.5 us (15%)
  between operations  14.5 us (8%)
  blocking collectives  13.8 us (7%)
  local copies, waits for them, and re-layouts  13 us (7%)
  other arithmetic  5.52 us (3%)
  matrix products  3.77 us (2%)
    pallas_call x3, Pallas kernels, back(): pl.pallas_call(functools.partial(back_kernel, steps, first), in_specs=[sm...  33.8 us
    pallas_call x2, Pallas kernels, encode_near(): pl.pallas_call(functools.partial(encode_near_kernel, steps), in_specs=[sm...  23.6 us
    ppermute x11, starting transfers between devices, shifted(): return lax.ppermute(x, 'mp', [(i, (i + by) % MP) for i in range(MP)])  17.2 us
    all_to_all x1, blocking collectives, copies_to_all(): lax.all_to_all(jnp.broadcast_to(x, (count, *x.shape)), axes, split_axis=0...  13.8 us
    all_to_all x2, waiting for transfers between devices, copies_to_all(): lax.all_to_all(jnp.broadcast_to(x, (count, *x.shape)), axes, split_axis=0...  12.9 us
    pallas_call x1, Pallas kernels, encode_far(): pl.pallas_call(encode_far_kernel, in_specs=[smem] + [anywhere] * 3 + [vme...  12.1 us
    ppermute x11, waiting for transfers between devices, shifted(): return lax.ppermute(x, 'mp', [(i, (i + by) % MP) for i in range(MP)])  9.6 us
    unnamed x34, local copies, waits for them, and re-layouts  7.16 us
  transfers between devices with their start and end apart: 16, of which 7 were waited for; matrix products, arithmetic and copies ran while one was open for 6% of the time, Pallas kernels for 33%

profile of v8, /device:TPU:0, one launch (start us, length us, event | category | flops | bytes accessed | tf_op | source)
XLA Modules:
  0.0 183.8 jit_solution(17648654166531178097)
XLA Ops:
  7.2 3.2 %collective-permute-start = (bf16[1024,512]{1,0:T(8,128)(2,1)}, bf16[1024,512]{1,0:T(8,128)(2,1)S(1)}, u32[]{:S(2)}, u32[]{:S(2)}) collective-permute-start(bf16[1024,512]{1,0:T(8,128)(2,1)} %x_ref.1), channel_id=1, source_target_pairs={{0,3},{1,0},{2,1},{3,2},{4,7},{5,4},{6,5},{7,6},{8,11},{9,8},{10,9... | collective-permute-start | bytes 3145736 | tf_op jit(solution)/shard_map/ppermute | solution.py:24
  11.8 3.2 %collective-permute-start.2 = (bf16[32,512]{1,0:T(8,128)(2,1)}, bf16[32,512]{1,0:T(8,128)(2,1)S(1)}, u32[]{:S(2)}, u32[]{:S(2)}) collective-permute-start(bf16[32,512]{1,0:T(8,128)(2,1)} %get-tuple-element.70), channel_id=1, source_target_pairs={{0,3},{1,0},{2,1},{3,2},{4,7},{5,4},{6,5},{7,6},{8,11},{9,8},{10,9... | collective-permute-start | bytes 98312 | tf_op jit(solution)/shard_map/ppermute | solution.py:24
  19.4 8.8 %encode_near.2 = (f32[7,1024,512]{2,1,0:T(8,128)}, f32[1024,1]{1,0:T(8,128)S(1)}, f32[8,512]{1,0:T(8,128)S(1)}) custom-call(s32[1]{0:T(128)} %bitcast.m_ref, bf16[1024,512]{1,0:T(8,128)(2,1)} %x_ref.1, f32[4,1,512]{2,1,0:T(1,128)S(1)} %bitcast.72, bf16[2048,1792]{1,0:T(8,128)(2,1)} %wg_ref.7, bf16[2048,1792]{1,0:T(8,128)(2,1)} %wu_ref.7, ...), custom_call_target="tpu_custom_call" | custom-call | flops 3758096384 | bytes 8388608 | tf_op jit(solution)/shard_map/encode_near/pallas_call | solution.py:150
  28.2 6.3 %collective-permute-done.2 = bf16[32,512]{1,0:T(8,128)(2,1)S(1)} collective-permute-done((bf16[32,512]{1,0:T(8,128)(2,1)}, bf16[32,512]{1,0:T(8,128)(2,1)S(1)}, u32[]{:S(2)}, u32[]{:S(2)}) %collective-permute-start.2) | collective-permute-done | bytes 32800 | tf_op jit(solution)/shard_map/ppermute | solution.py:24
  34.5 2.0 %collective-permute-done.3 = bf16[32,512]{1,0:T(8,128)(2,1)S(1)} collective-permute-done((bf16[32,512]{1,0:T(8,128)(2,1)}, bf16[32,512]{1,0:T(8,128)(2,1)S(1)}, u32[]{:S(2)}, u32[]{:S(2)}) %collective-permute-start.3) | collective-permute-done | bytes 32800 | tf_op jit(solution)/shard_map/ppermute | solution.py:24
  40.0 3.3 %collective-permute-start.6 = (bf16[512,512]{1,0:T(8,128)(2,1)S(1)}, bf16[512,512]{1,0:T(8,128)(2,1)S(1)}, u32[]{:S(2)}, u32[]{:S(2)}) collective-permute-start(bf16[512,512]{1,0:T(8,128)(2,1)S(1)} %slice.48), channel_id=1, source_target_pairs={{0,3},{1,0},{2,1},{3,2},{4,7},{5,4},{6,5},{7,6},{8,11},{9,8},{10,9... | collective-permute-start | bytes 1572872 | tf_op jit(solution)/shard_map/ppermute | solution.py:24
  43.3 14.9 %encode_near.3 = (f32[7,1024,512]{2,1,0:T(8,128)}, f32[1024,1]{1,0:T(8,128)S(1)}) custom-call(s32[1]{0:T(128)} %bitcast.m_ref, bf16[1024,512]{1,0:T(8,128)(2,1)} %copy-done.4, bf16[1024,512]{1,0:T(8,128)(2,1)} %copy-done.5, f32[4,1,512]{2,1,0:T(1,128)S(1)} %bitcast.73, bf16[2048,1792]{1,0:T(8,128)(2,1)} %wg_ref.7, bf16[2048,1792]{1,0:T(8,128)(2,1)} %wu_ref.7, ...), custom_call_target="tpu_custom_call" | custom-call | flops 7516192768 | bytes 8388608 | tf_op jit(solution)/shard_map/encode_near/pallas_call | solution.py:150
  59.2 12.1 %encode_far.1 = (bf16[1024,1792]{1,0:T(8,128)(2,1)}, bf16[1024,1792]{1,0:T(8,128)(2,1)}, bf16[1024,1792]{1,0:T(8,128)(2,1)}, f32[7,8,256]{2,1,0:T(8,128)S(1)}, f32[1024,1]{1,0:T(8,128)S(1)}) custom-call(s32[1]{0:T(128)} %bitcast.m_ref, bf16[512,512]{1,0:T(8,128)(2,1)} %copy-done.6, bf16[512,512]{1,0:T(8,128)(2,1)} %copy-done.7, ...), custom_call_target="tpu_custom_call" | custom-call | flops 3758096384 | bytes 11010048 | tf_op jit(solution)/shard_map/encode_far/pallas_call | solution.py:260
  73.2 3.4 %all-to-all-start = ((bf16[8,8,2048]{2,1,0:T(8,128)(2,1)}), bf16[8,8,2048]{2,1,0:T(8,128)(2,1)S(1)}, u32[]{:S(2)}, u32[]{:S(2)}) async-start(bf16[8,8,2048]{2,1,0:T(8,128)(2,1)} %broadcast_in_dim.21), calls=%async_computation | async-start | bytes 524288 | tf_op jit(solution)/shard_map/all_to_all | solution.py:37
  76.8 6.7 %all-to-all-done = bf16[8,8,2048]{2,1,0:T(8,128)(2,1)S(1)} async-done(((bf16[8,8,2048]{2,1,0:T(8,128)(2,1)}), bf16[8,8,2048]{2,1,0:T(8,128)(2,1)S(1)}, u32[]{:S(2)}, u32[]{:S(2)}) %all-to-all-start) | async-done | bytes 262176 | tf_op jit(solution)/shard_map/all_to_all | solution.py:37
  86.8 2.3 %fusion.19 = (f32[512]{0:T(512)S(1)}, f32[512]{0:T(512)S(1)}, f32[16,512]{1,0:T(8,128)S(1)}) fusion(f32[16]{0:T(128)S(1)} %rsqrt.32, f32[512]{0:T(512)S(1)} %get-tuple-element.55, f32[16]{0:T(128)S(1)} %fusion.24, f32[16]{0:T(128)S(1)} %fusion.27, f32[512]{0:T(512)S(1)} %get-tuple-element.56, bf16[512,2176]{1,0:T(8,128)(2,1)} %all-gather.3.cloned.1.call-done, ...), kind=kOutput, calls=%fused_computation.49 | convolution fusion | flops 33610752 | bytes 2203840 | tf_op jit(solution)/shard_map/dot_general | solution.py:47
  89.1 13.8 %all_to_all.20 = f32[16,8,128]{2,1,0:T(8,128)S(1)} all-to-all(f32[16,8,128]{2,1,0:T(8,128)S(1)} %broadcast_in_dim.22), channel_id=1, replica_groups=mesh['x'=4,'z'=4,'core'=2,'mp'=4] {'x','z'}, dimensions={0} | all-to-all | bytes 131072 | tf_op jit(solution)/shard_map/all_to_all | solution.py:37
  104.4 3.6 %all-to-all-start.2 = ((bf16[8,8,2176]{2,1,0:T(8,128)(2,1)}), bf16[8,8,2176]{2,1,0:T(8,128)(2,1)S(1)}, u32[]{:S(2)}, u32[]{:S(2)}) async-start(bf16[8,8,2176]{2,1,0:T(8,128)(2,1)} %bitcast.23), calls=%async_computation.2 | async-start | bytes 557056 | tf_op jit(solution)/shard_map/all_to_all | solution.py:589
  108.1 6.8 %all-to-all-done.2 = bf16[8,8,2176]{2,1,0:T(8,128)(2,1)S(1)} async-done(((bf16[8,8,2176]{2,1,0:T(8,128)(2,1)}), bf16[8,8,2176]{2,1,0:T(8,128)(2,1)S(1)}, u32[]{:S(2)}, u32[]{:S(2)}) %all-to-all-start.2) | async-done | bytes 278560 | tf_op jit(solution)/shard_map/all_to_all | solution.py:589
  115.2 3.1 %copy-done = bf16[1792,2048]{1,0:T(8,128)(2,1)S(1)} copy-done((bf16[1792,2048]{1,0:T(8,128)(2,1)S(1)}, bf16[1792,2048]{1,0:T(8,128)(2,1)}, u32[]{:S(2)}) %copy-start) | copy-done | bytes 7340056
  118.3 9.3 %back.3 = (bf16[512,512]{1,0:T(8,128)(2,1)}, bf16[512,512]{1,0:T(8,128)(2,1)}, f32[8,1792]{1,0:T(8,128)S(1)}) custom-call(s32[1]{0:T(128)} %bitcast.m_ref, bf16[1024,1792]{1,0:T(8,128)(2,1)} %get-tuple-element.35.a_ref, bf16[1024,1792]{1,0:T(8,128)(2,1)} %get-tuple-element.36.b_ref, bf16[1024,1792]{1,0:T(8,128)(2,1)} %get-tuple-element.37.c_ref, ...), custom_call_target="tpu_custom_call" | custom-call | flops 1 | bytes 1 | tf_op jit(solution)/shard_map/back/pallas_call | solution.py:410
  128.5 2.4 %collective-permute-start.9 = (bf16[512,512]{1,0:T(8,128)(2,1)}, bf16[512,512]{1,0:T(8,128)(2,1)S(1)}, u32[]{:S(2)}, u32[]{:S(2)}) collective-permute-start(bf16[512,512]{1,0:T(8,128)(2,1)} %get-tuple-element.45), channel_id=1, source_target_pairs={{0,3},{1,0},{2,1},{3,2},{4,7},{5,4},{6,5},{7,6},{8,11},{9,8},{10,9... | collective-permute-start | bytes 1572872 | tf_op jit(solution)/shard_map/ppermute | solution.py:24
  131.0 13.5 %back.4 = (bf16[1024,512]{1,0:T(8,128)(2,1)}, bf16[1024,512]{1,0:T(8,128)(2,1)}) custom-call(s32[1]{0:T(128)} %bitcast.m_ref, bf16[1024,1792]{1,0:T(8,128)(2,1)} %get-tuple-element.35.a_ref, bf16[1024,1792]{1,0:T(8,128)(2,1)} %get-tuple-element.36.b_ref, bf16[1024,1792]{1,0:T(8,128)(2,1)} %get-tuple-element.37.c_ref, f32[8,1792]{1,0:T(8,128)S(1)} %get-tuple-element.48.g_in, ...), custom_call_target="tpu_custom_call" | custom-call | flops 1 | bytes 1 | tf_op jit(solution)/shard_map/back/pallas_call | solution.py:410
  144.5 2.1 %add_halves.1 = (bf16[1024,512]{1,0:T(8,128)(2,1)}, bf16[1024,512]{1,0:T(8,128)(2,1)}) custom-call(bf16[1024,512]{1,0:T(8,128)(2,1)} %get-tuple-element.42.right_ref, bf16[1024,512]{1,0:T(8,128)(2,1)} %get-tuple-element.43.left_ref, bf16[512,512]{1,0:T(8,128)(2,1)S(1)} %collective-permute-done.8.from_left_ref, ...), custom_call_target="tpu_custom_call", output_to_operand_aliasing={{0}: (0, {}), {1}: (1, {})} | custom-call | flops 1 | bytes 1 | tf_op jit(solution)/shard_map/add_halves/pallas_call | solution.py:438
  146.6 3.2 %collective-permute-start.11 = (bf16[1024,512]{1,0:T(8,128)(2,1)}, bf16[1024,512]{1,0:T(8,128)(2,1)S(1)}, u32[]{:S(2)}, u32[]{:S(2)}) collective-permute-start(bf16[1024,512]{1,0:T(8,128)(2,1)} %get-tuple-element.52), channel_id=1, source_target_pairs={{0,3},{1,0},{2,1},{3,2},{4,7},{5,4},{6,5},{7,6},{8,11},{9,8},{10,9... | collective-permute-start | bytes 3145736 | tf_op jit(solution)/shard_map/ppermute | solution.py:24
  150.0 10.9 %back.5 = (bf16[1024,512]{1,0:T(8,128)(2,1)}, f32[1024,1]{1,0:T(8,128)S(1)}) custom-call(s32[1]{0:T(128)} %bitcast.m_ref, bf16[1024,1792]{1,0:T(8,128)(2,1)} %get-tuple-element.35.a_ref, bf16[1024,1792]{1,0:T(8,128)(2,1)} %get-tuple-element.36.b_ref, bf16[1024,1792]{1,0:T(8,128)(2,1)} %get-tuple-element.37.c_ref, f32[8,1792]{1,0:T(8,128)S(1)} %get-tuple-element.48.g_in, ...), custom_call_target="tpu_custom_call" | custom-call | flops 1 | bytes 1 | tf_op jit(solution)/shard_map/back/pallas_call | solution.py:410
  163.6 3.3 %all-to-all-start.3 = ((f32[4,16,128]{2,1,0:T(8,128)}), f32[4,16,128]{2,1,0:T(8,128)S(1)}, u32[]{:S(2)}, u32[]{:S(2)}) async-start(f32[4,16,128]{2,1,0:T(8,128)} %broadcast_in_dim.51), calls=%async_computation.3 | async-start | bytes 65536 | tf_op jit(solution)/shard_map/all_to_all | solution.py:37
  166.9 6.2 %all-to-all-done.3 = f32[4,16,128]{2,1,0:T(8,128)S(1)} async-done(((f32[4,16,128]{2,1,0:T(8,128)}), f32[4,16,128]{2,1,0:T(8,128)S(1)}, u32[]{:S(2)}, u32[]{:S(2)}) %all-to-all-start.3) | async-done | bytes 32800 | tf_op jit(solution)/shard_map/all_to_all | solution.py:37
  173.7 3.2 %finish.1 = bf16[1024,512]{1,0:T(8,128)(2,1)} custom-call(bf16[1024,512]{1,0:T(8,128)(2,1)} %x_ref.1, bf16[1024,512]{1,0:T(8,128)(2,1)} %get-tuple-element.50.own_ref, bf16[1024,512]{1,0:T(8,128)(2,1)S(1)} %collective-permute-done.10.one_ref, bf16[1024,512]{1,0:T(8,128)(2,1)S(1)} %collective-permute-done.11.two_ref, ...), custom_call_target="tpu_custom_call" | custom-call | tf_op jit(solution)/shard_map/finish/pallas_call | solution.py:476
  (118 shorter events, 21.7 us)
Async XLA Ops:
  7.2 78.1 %all-gather.3.cloned.1.call-start = ((), (), s32[]{:S(2)}) async-start(), calls=%async_computation.4 | async-start | bytes 2367488 | tf_op jit(solution)/shard_map/all_gather | solution.py:539
  7.2 32.4 %collective-permute-start = (bf16[1024,512]{1,0:T(8,128)(2,1)}, bf16[1024,512]{1,0:T(8,128)(2,1)S(1)}, u32[]{:S(2)}, u32[]{:S(2)}) collective-permute-start(bf16[1024,512]{1,0:T(8,128)(2,1)} %x_ref.1), channel_id=1, source_target_pairs={{0,3},{1,0},{2,1},{3,2},{4,7},{5,4},{6,5},{7,6},{8,11},{9,8},{10,9... | collective-permute-start | bytes 3145736 | tf_op jit(solution)/shard_map/ppermute | solution.py:24
  10.4 29.2 %collective-permute-start.1 = (bf16[1024,512]{1,0:T(8,128)(2,1)}, bf16[1024,512]{1,0:T(8,128)(2,1)S(1)}, u32[]{:S(2)}, u32[]{:S(2)}) collective-permute-start(bf16[1024,512]{1,0:T(8,128)(2,1)} %x_ref.1), channel_id=1, source_target_pairs={{0,1},{1,2},{2,3},{3,0},{4,5},{5,6},{6,7},{7,4},{8,9},{9,10},{10,1... | collective-permute-start | bytes 3145736 | tf_op jit(solution)/shard_map/ppermute | solution.py:24
  11.8 22.7 %collective-permute-start.2 = (bf16[32,512]{1,0:T(8,128)(2,1)}, bf16[32,512]{1,0:T(8,128)(2,1)S(1)}, u32[]{:S(2)}, u32[]{:S(2)}) collective-permute-start(bf16[32,512]{1,0:T(8,128)(2,1)} %get-tuple-element.70), channel_id=1, source_target_pairs={{0,3},{1,0},{2,1},{3,2},{4,7},{5,4},{6,5},{7,6},{8,11},{9,8},{10,9... | collective-permute-start | bytes 98312 | tf_op jit(solution)/shard_map/ppermute | solution.py:24
  15.0 21.5 %collective-permute-start.3 = (bf16[32,512]{1,0:T(8,128)(2,1)}, bf16[32,512]{1,0:T(8,128)(2,1)S(1)}, u32[]{:S(2)}, u32[]{:S(2)}) collective-permute-start(bf16[32,512]{1,0:T(8,128)(2,1)} %get-tuple-element.71), channel_id=1, source_target_pairs={{0,2},{1,3},{2,0},{3,1},{4,6},{5,7},{6,4},{7,5},{8,10},{9,11},{10,... | collective-permute-start | bytes 98312 | tf_op jit(solution)/shard_map/ppermute | solution.py:24
  15.0 22.8 %collective-permute-start.4 = (bf16[32,512]{1,0:T(8,128)(2,1)}, bf16[32,512]{1,0:T(8,128)(2,1)S(1)}, u32[]{:S(2)}, u32[]{:S(2)}) collective-permute-start(bf16[32,512]{1,0:T(8,128)(2,1)} %get-tuple-element.69), channel_id=1, source_target_pairs={{0,1},{1,2},{2,3},{3,0},{4,5},{5,6},{6,7},{7,4},{8,9},{9,10},{10,1... | collective-permute-start | bytes 98312 | tf_op jit(solution)/shard_map/ppermute | solution.py:24
  19.4 8.8 %copy-start.9 = (s32[128]{0:T(128)S(1)}, s32[128]{0:T(128)}, u32[]{:S(2)}) copy-start(s32[128]{0:T(128)} %param.12) | copy-start | bytes 1540
  28.1 15.1 %copy-start.3 = (f32[2048]{0:T(1024)S(1)}, f32[2048]{0:T(1024)}, u32[]{:S(2)}) copy-start(f32[2048]{0:T(1024)} %param.14) | copy-start | bytes 24580
  39.6 3.7 %copy-start.4 = (bf16[1024,512]{1,0:T(8,128)(2,1)}, bf16[1024,512]{1,0:T(8,128)(2,1)S(1)}, u32[]{:S(2)}) copy-start(bf16[1024,512]{1,0:T(8,128)(2,1)S(1)} %collective-permute-done.refs_0_) | copy-start | bytes 3145732
  39.6 3.7 %copy-start.5 = (bf16[1024,512]{1,0:T(8,128)(2,1)}, bf16[1024,512]{1,0:T(8,128)(2,1)S(1)}, u32[]{:S(2)}) copy-start(bf16[1024,512]{1,0:T(8,128)(2,1)S(1)} %collective-permute-done.1.refs_1_) | copy-start | bytes 3145732
  39.6 37.0 %collective-permute-start.7 = (s32[8]{0:T(128)S(1)}, s32[8]{0:T(128)S(1)}, u32[]{:S(2)}, u32[]{:S(2)}) collective-permute-start(s32[8]{0:T(128)S(1)} %get-tuple-element.63), channel_id=1, source_target_pairs={{0,4},{4,0},{1,5},{5,1},{2,6},{6,2},{3,7},{7,3},{8,12},{12,8},{9,1... | collective-permute-start | bytes 104 | tf_op jit(solution)/shard_map/ppermute | solution.py:33
  39.9 18.3 %collective-permute-start.5 = (bf16[512,512]{1,0:T(8,128)(2,1)S(1)}, bf16[512,512]{1,0:T(8,128)(2,1)S(1)}, u32[]{:S(2)}, u32[]{:S(2)}) collective-permute-start(bf16[512,512]{1,0:T(8,128)(2,1)S(1)} %slice.47), channel_id=1, source_target_pairs={{0,1},{1,2},{2,3},{3,0},{4,5},{5,6},{6,7},{7,4},{8,9},{9,10},{10,1... | collective-permute-start | bytes 1572872 | tf_op jit(solution)/shard_map/ppermute | solution.py:24
  39.9 31.4 %slice-start = ((s8[7340032]{0:T(1024)(128)(4,1)}), s8[4194304]{0:T(1024)(128)(4,1)S(1)}, s32[]{:S(2)}) async-start(s8[7340032]{0:T(1024)(128)(4,1)} %bitcast.70), calls=%async_computation.5 | async-start | bytes 8388608
  40.0 18.2 %collective-permute-start.6 = (bf16[512,512]{1,0:T(8,128)(2,1)S(1)}, bf16[512,512]{1,0:T(8,128)(2,1)S(1)}, u32[]{:S(2)}, u32[]{:S(2)}) collective-permute-start(bf16[512,512]{1,0:T(8,128)(2,1)S(1)} %slice.48), channel_id=1, source_target_pairs={{0,3},{1,0},{2,1},{3,2},{4,7},{5,4},{6,5},{7,6},{8,11},{9,8},{10,9... | collective-permute-start | bytes 1572872 | tf_op jit(solution)/shard_map/ppermute | solution.py:24
  43.3 28.1 %slice-start.1 = ((s8[7340032]{0:T(1024)(128)(4,1)}), s8[3145728]{0:T(1024)(128)(4,1)S(1)}, s32[]{:S(2)}) async-start(s8[7340032]{0:T(1024)(128)(4,1)} %bitcast.70), calls=%async_computation.6 | async-start | bytes 6291456
  73.2 10.3 %all-to-all-start = ((bf16[8,8,2048]{2,1,0:T(8,128)(2,1)}), bf16[8,8,2048]{2,1,0:T(8,128)(2,1)S(1)}, u32[]{:S(2)}, u32[]{:S(2)}) async-start(bf16[8,8,2048]{2,1,0:T(8,128)(2,1)} %broadcast_in_dim.21), calls=%async_computation | async-start | bytes 524288 | tf_op jit(solution)/shard_map/all_to_all | solution.py:37
  85.2 17.9 %copy-start.8 = (bf16[512,2176]{1,0:T(8,128)(2,1)S(1)}, bf16[512,2176]{1,0:T(8,128)(2,1)}, u32[]{:S(2)}) copy-start(bf16[512,2176]{1,0:T(8,128)(2,1)} %all-gather.3.cloned.1.call-done) | copy-start | bytes 6684676
  104.4 10.4 %all-to-all-start.2 = ((bf16[8,8,2176]{2,1,0:T(8,128)(2,1)}), bf16[8,8,2176]{2,1,0:T(8,128)(2,1)S(1)}, u32[]{:S(2)}, u32[]{:S(2)}) async-start(bf16[8,8,2176]{2,1,0:T(8,128)(2,1)} %bitcast.23), calls=%async_computation.2 | async-start | bytes 557056 | tf_op jit(solution)/shard_map/all_to_all | solution.py:589
  115.2 3.1 %copy-start = (bf16[1792,2048]{1,0:T(8,128)(2,1)S(1)}, bf16[1792,2048]{1,0:T(8,128)(2,1)}, u32[]{:S(2)}) copy-start(bf16[1792,2048]{1,0:T(8,128)(2,1)} %refs_0_.3) | copy-start | bytes 22020100
  127.6 16.9 %collective-permute-start.8 = (bf16[512,512]{1,0:T(8,128)(2,1)}, bf16[512,512]{1,0:T(8,128)(2,1)S(1)}, u32[]{:S(2)}, u32[]{:S(2)}) collective-permute-start(bf16[512,512]{1,0:T(8,128)(2,1)} %get-tuple-element.44), channel_id=1, source_target_pairs={{0,1},{1,2},{2,3},{3,0},{4,5},{5,6},{6,7},{7,4},{8,9},{9,10},{10,1... | collective-permute-start | bytes 1572872 | tf_op jit(solution)/shard_map/ppermute | solution.py:24
  128.5 16.0 %collective-permute-start.9 = (bf16[512,512]{1,0:T(8,128)(2,1)}, bf16[512,512]{1,0:T(8,128)(2,1)S(1)}, u32[]{:S(2)}, u32[]{:S(2)}) collective-permute-start(bf16[512,512]{1,0:T(8,128)(2,1)} %get-tuple-element.45), channel_id=1, source_target_pairs={{0,3},{1,0},{2,1},{3,2},{4,7},{5,4},{6,5},{7,6},{8,11},{9,8},{10,9... | collective-permute-start | bytes 1572872 | tf_op jit(solution)/shard_map/ppermute | solution.py:24
  146.6 27.0 %collective-permute-start.10 = (bf16[1024,512]{1,0:T(8,128)(2,1)}, bf16[1024,512]{1,0:T(8,128)(2,1)S(1)}, u32[]{:S(2)}, u32[]{:S(2)}) collective-permute-start(bf16[1024,512]{1,0:T(8,128)(2,1)} %get-tuple-element.51), channel_id=1, source_target_pairs={{0,1},{1,2},{2,3},{3,0},{4,5},{5,6},{6,7},{7,4},{8,9},{9,10},{10,1... | collective-permute-start | bytes 3145736 | tf_op jit(solution)/shard_map/ppermute | solution.py:24
  146.6 27.0 %collective-permute-start.11 = (bf16[1024,512]{1,0:T(8,128)(2,1)}, bf16[1024,512]{1,0:T(8,128)(2,1)S(1)}, u32[]{:S(2)}, u32[]{:S(2)}) collective-permute-start(bf16[1024,512]{1,0:T(8,128)(2,1)} %get-tuple-element.52), channel_id=1, source_target_pairs={{0,3},{1,0},{2,1},{3,2},{4,7},{5,4},{6,5},{7,6},{8,11},{9,8},{10,9... | collective-permute-start | bytes 3145736 | tf_op jit(solution)/shard_map/ppermute | solution.py:24
  163.6 9.5 %all-to-all-start.3 = ((f32[4,16,128]{2,1,0:T(8,128)}), f32[4,16,128]{2,1,0:T(8,128)S(1)}, u32[]{:S(2)}, u32[]{:S(2)}) async-start(f32[4,16,128]{2,1,0:T(8,128)} %broadcast_in_dim.51), calls=%async_computation.3 | async-start | bytes 65536 | tf_op jit(solution)/shard_map/all_to_all | solution.py:37
  (4 other events, 3.2 us)
Sparse Core Ops, SparseCore 0:
  39.7 45.4 all-gather.2
